TPU v7x, 256 devices: a whole 4x4x8 slice. The times are simulated.
256 devices in a mesh: space: 16 (over x_hi, z), chan: 16 (over x_lo, y, core).
Axes of the slice: x: 4 (x_hi: 2, x_lo: 2; x = x_hi * 2 + x_lo), y: 4, z: 8, core: 2. Of those that a mesh axis runs over, the one named last changes fastest.
Arguments:
- volume: bfloat16 [4, 512, 16384], P(None, ('space', 'chan')), may hold values from -6 to 6
- conv1_weight: bfloat16 [3, 3, 3, 4, 128], replicated, may hold values from -0.625 to 0.625
- conv1_bias: float32 [128], replicated, may hold values from -3 to 3
- conv2_weight: bfloat16 [3, 3, 3, 128, 128], replicated, may hold values from -0.109375 to 0.109375
- conv2_bias: float32 [128], replicated, may hold values from -3 to 3
Outputs:
- pooled: bfloat16 [128, 128, 1024], P('chan', 'space')
All inputs are finite; a program needn't handle non-finite values.
Results may differ from a plain program's by a relative error of at most 0.0085.
Values may be sent and summed in bfloat16 or wider, within the bound.
No kernel may reach another device: no remote copies, remote signals or barrier semaphores. Data moves between devices by JAX's collectives and lax.ppermute only.
A program may use at most 128 MiB of HBM per device.

v0:
```python
import jax
import jax.numpy as jnp
from jax import lax
from jax.sharding import PartitionSpec as P

SIDE = 128


def from_behind(shard, axis, by):
    peers = lax.axis_size(axis)
    pairs = [(i, i + by) for i in range(peers) if 0 <= i + by < peers]
    return lax.ppermute(shard, axis, pairs)


def with_halo(shard, sides, width):
    edges = {}
    for axis, dim in sides:
        peers, length = (lax.axis_size(axis), shard.shape[dim])
        up = [(i, (i + 1) % peers) for i in range(peers - 1)]
        last = lax.slice_in_dim(shard, length - width, length, axis=dim)
        initial = lax.slice_in_dim(shard, 0, width, axis=dim)
        edges[dim] = (
            lax.ppermute(last, axis, up),
            lax.ppermute(initial, axis, [(b, a) for a, b in up]),
        )
    done = []
    for _, dim in sides:
        low, high = edges[dim]
        around = [(width, width) if d in done else (0, 0) for d in range(shard.ndim)]
        shard = jnp.concatenate([jnp.pad(low, around), shard, jnp.pad(high, around)], axis=dim)
        done.append(dim)
    return shard


def leaky_relu(value):
    return jnp.where(value > 0, value, 0.2 * value)


def strided_conv(stacked, weights, bias):
    fields, depth_ext, cells = stacked.shape
    grid = stacked.reshape(1, fields, depth_ext, SIDE, SIDE)
    result = lax.conv_general_dilated(
        grid,
        weights,
        (2, 2, 2),
        ((0, 0), (1, 0), (1, 0)),
        dimension_numbers=("NCDHW", "DHWIO", "NCDHW"),
        preferred_element_type=jnp.float32,
    )
    channels = weights.shape[4]
    result = result[0].reshape(channels, result.shape[2], SIDE // 2 * (SIDE // 2))
    return leaky_relu(result + bias[:, None, None]).astype(jnp.bfloat16)


def second_conv(padded, weights):
    channels, depth_ext, cells = padded.shape
    half_side = SIDE // 2
    grid = padded.reshape(1, channels, depth_ext, half_side, half_side)
    result = lax.conv_general_dilated(
        grid,
        weights,
        (1, 1, 1),
        ((0, 0), (1, 1), (1, 1)),
        dimension_numbers=("NCDHW", "DHWIO", "NCDHW"),
        preferred_element_type=jnp.float32,
    )
    return result.reshape(weights.shape[4], depth_ext - 2, cells)


def shards(volume, conv1_weight, conv1_bias, conv2_weight, conv2_bias):
    fields, in_planes, cells = volume.shape
    out_planes = in_planes // 2
    channels = conv1_weight.shape[4]
    quarter = SIDE // 4
    lower_plane = from_behind(volume[:, in_planes - 1 :, :], ("space", "chan"), 1)
    stacked = jnp.concatenate([lower_plane, volume], axis=1)
    first_layer = strided_conv(stacked, conv1_weight, conv1_bias)
    padded = with_halo(first_layer, ((("space", "chan"), 1),), 1)
    summed = second_conv(padded, conv2_weight)
    active_slab = leaky_relu(summed + conv2_bias[:, None, None]).astype(jnp.bfloat16)
    lateral = active_slab.astype(jnp.float32).reshape(channels, out_planes, quarter, 2, quarter, 2)
    lateral = jnp.mean(lateral, axis=(3, 5)).reshape(channels, out_planes, quarter * quarter)
    moved = lax.all_to_all(
        lateral.astype(jnp.bfloat16), "chan", split_axis=0, concat_axis=1, tiled=True
    ).astype(lateral.dtype)
    group, depth, small_cells = moved.shape
    return jnp.mean(moved.reshape(group, depth // 2, 2, small_cells), axis=2).astype(jnp.bfloat16)


def solution(mesh):
    in_specs = (P(None, ("space", "chan"), None), P(), P(), P(), P())
    out_specs = P("chan", "space", None)
    return jax.shard_map(shards, mesh=mesh, in_specs=in_specs, out_specs=out_specs, check_vma=False)
```

profile of v0, /device:TPU:96, one launch (start us, length us, event | category | flops | bytes accessed | tf_op | source)
XLA Modules:
  0.0 95.5 jit_solution(15656083008884899499)
XLA Ops:
  0.0 0.0 copy-start
  0.0 1.3 %slice.3 = bf16[4,1,16384]{2,1,0:T(2,128)(2,1)S(1)} slice(bf16[4,2,16384]{2,1,0:T(2,128)(2,1)} %param.5), slice={[0:4], [1:2], [0:16384]} | slice | bytes 262144 | tf_op jit(solution)/shard_map/slice | solution.py:75
  1.3 1.9 %collective-permute-start = (bf16[4,1,16384]{2,1,0:T(2,128)(2,1)S(1)}, bf16[4,1,16384]{2,1,0:T(2,128)(2,1)S(1)}, u32[]{:S(2)}, u32[]{:S(2)}) collective-permute-start(bf16[4,1,16384]{2,1,0:T(2,128)(2,1)S(1)} %slice.3), channel_id=1, source_target_pairs={{0,1},{1,2},{2,3},{3,4},{4,5},{5,6},{6,7},{7,8},{8,9},{9,10},{10,1... | collective-permute-start | bytes 393224 | tf_op jit(solution)/shard_map/ppermute | solution.py:12
  3.2 8.8 %collective-permute-done = bf16[4,1,16384]{2,1,0:T(2,128)(2,1)S(1)} collective-permute-done((bf16[4,1,16384]{2,1,0:T(2,128)(2,1)S(1)}, bf16[4,1,16384]{2,1,0:T(2,128)(2,1)S(1)}, u32[]{:S(2)}, u32[]{:S(2)}) %collective-permute-start) | collective-permute-done | bytes 131104 | tf_op jit(solution)/shard_map/ppermute | solution.py:12
  12.0 1.5 %pad_maximum_fusion = bf16[4,3,16384]{2,1,0:T(4,128)(2,1)S(1)} fusion(bf16[4,2,16384]{2,1,0:T(2,128)(2,1)} %param.5, bf16[4,1,16384]{2,1,0:T(2,128)(2,1)S(1)} %collective-permute-done), kind=kLoop, calls=%fused_computation.28 | loop fusion | flops 786432 | bytes 786432 | tf_op jit(solution)/shard_map/concatenate | solution.py:76
  13.5 0.5 reshape.166
  14.1 0.3 copy.63
  14.3 0.2 pad.clone
  14.5 0.0 copy-start.1
  14.5 0.0 copy-start.3
  14.5 0.0 copy-start.4
  14.5 7.6 %copy.48 = bf16[4,3,128,1,8,18]{4,0,5,2,1,3:T(4,128)(2,1)} copy(bf16[4,3,128,1,8,18]{2,0,5,4,1,3:T(4,128)(2,1)S(1)} %bitcast.49) | data formatting | bytes 884736 | tf_op jit(solution)/shard_map/conv_general_dilated | solution.py:42
  22.1 1.7 %slice.9 = bf16[4,3,128,1,7,2]{4,0,5,2,1,3:T(4,128)(2,1)S(1)} slice(bf16[4,3,128,1,8,18]{4,0,5,2,1,3:T(4,128)(2,1)} %copy.48), slice={[0:4], [0:3], [0:128], [0:1], [1:8], [0:2]} | slice | bytes 86016 | tf_op jit(solution)/shard_map/conv_general_dilated | solution.py:42
  23.8 0.0 copy-done.1
  23.8 0.0 copy-done.3
  23.8 0.0 copy-done.4
  23.8 8.9 %fusion.14 = (bf16[1,64,8,9,128]{4,2,3,1,0:T(8,128)(2,1)S(1)}, f32[1,64,8,9,128]{4,2,3,1,0:T(8,128)S(1)}) fusion(f32[128]{0:T(128)S(1)} %copy-done.1, bf16[3,3,3,4,128]{4,3,2,1,0:T(4,128)(2,1)S(1)} %copy-done.3, bf16[4,3,128,1,7,2]{4,0,5,2,1,3:T(4,128)(2,1)S(1)} %slice.9, bf16[4,3,128,1,8,18]{4,0,5,2,1,3:T(4,128)(2,1)} %copy.48, pred[8,9]{0,1:T(8,128)(4,1)S(1)} %copy-done.4), kind=kOutput, calls=%fused_computation.18 | convolution fusion | flops 131751936 | bytes 4052552 | tf_op jit(solution)/shard_map/conv_general_dilated | solution.py:42
  32.7 0.5 copy.49
  33.1 0.2 slice_bitcast_fusion
  33.4 1.2 %copy.50 = f32[1,128,1,64,64]{1,4,3,2,0:T(8,128)S(1)} copy(f32[1,128,1,64,64]{1,3,4,0,2:T(8,128)S(1)} %slice_bitcast_fusion) | data formatting | bytes 4194304 | tf_op jit(solution)/shard_map/conv_general_dilated | solution.py:42
  34.6 0.3 fusion.16
  35.0 1.9 %collective-permute-start.1 = (bf16[128,1,4096]{0,2,1:T(8,128)(2,1)S(1)}, bf16[128,1,4096]{0,2,1:T(8,128)(2,1)S(1)}, u32[]{:S(2)}, u32[]{:S(2)}) collective-permute-start(bf16[128,1,4096]{0,2,1:T(8,128)(2,1)S(1)} %fusion.16), channel_id=1, source_target_pairs={{0,1},{1,2},{2,3},{3,4},{4,5},{5,6},{6,7},{7,8},{8,9},{9,10},{10,1... | collective-permute-start | bytes 3145736 | tf_op jit(solution)/shard_map/ppermute | solution.py:23
  36.9 6.8 %collective-permute-start.2 = (bf16[128,1,4096]{0,2,1:T(8,128)(2,1)S(1)}, bf16[128,1,4096]{0,2,1:T(8,128)(2,1)S(1)}, u32[]{:S(2)}, u32[]{:S(2)}) collective-permute-start(bf16[128,1,4096]{0,2,1:T(8,128)(2,1)S(1)} %fusion.16), channel_id=1, source_target_pairs={{1,0},{2,1},{3,2},{4,3},{5,4},{6,5},{7,6},{8,7},{9,8},{10,9},{11,1... | collective-permute-start | bytes 3145736 | tf_op jit(solution)/shard_map/ppermute | solution.py:24
  43.7 0.3 copy.51
  44.0 0.1 slice.11
  44.1 0.7 copy.68
  44.8 9.3 %collective-permute-done.1 = bf16[128,1,4096]{0,2,1:T(8,128)(2,1)S(1)} collective-permute-done((bf16[128,1,4096]{0,2,1:T(8,128)(2,1)S(1)}, bf16[128,1,4096]{0,2,1:T(8,128)(2,1)S(1)}, u32[]{:S(2)}, u32[]{:S(2)}) %collective-permute-start.1) | collective-permute-done | bytes 1048608 | tf_op jit(solution)/shard_map/ppermute | solution.py:23
  54.1 1.8 %collective-permute-done.2 = bf16[128,1,4096]{0,2,1:T(8,128)(2,1)S(1)} collective-permute-done((bf16[128,1,4096]{0,2,1:T(8,128)(2,1)S(1)}, bf16[128,1,4096]{0,2,1:T(8,128)(2,1)S(1)}, u32[]{:S(2)}, u32[]{:S(2)}) %collective-permute-start.2) | collective-permute-done | bytes 1048608 | tf_op jit(solution)/shard_map/ppermute | solution.py:24
  55.8 0.3 maximum_bitcast_fusion
  56.2 2.0 %copy.64 = bf16[128,3,64,1,64]{0,2,4,1,3:T(8,128)(2,1)S(1)} copy(bf16[128,3,64,1,64]{0,4,2,1,3:T(8,128)(2,1)S(1)} %maximum_bitcast_fusion) | data formatting | bytes 6291456
  58.2 0.8 pad.2.clone
  59.0 2.3 %copy.55 = bf16[128,3,64,1,8,9]{0,4,5,2,1,3:T(8,128)(2,1)S(1)} copy(bf16[128,3,64,1,8,9]{0,2,5,4,1,3:T(8,128)(2,1)S(1)} %bitcast.42) | data formatting | bytes 7077888 | tf_op jit(solution)/shard_map/conv_general_dilated | solution.py:59
  61.3 0.2 slice.12
  61.5 0.0 copy-done
  61.5 9.2 %fusion.18 = f32[1,64,8,9,128]{4,2,3,1,0:T(8,128)S(1)} fusion(bf16[3,3,3,128,128]{4,3,2,1,0:T(8,128)(2,1)S(1)} %copy-done, bf16[128,3,64,1,7,2]{0,4,5,2,1,3:T(8,128)(2,1)S(1)} %slice.12, bf16[128,3,64,1,8,9]{0,4,5,2,1,3:T(8,128)(2,1)S(1)} %copy.55, pred[8,9]{0,1:T(8,128)(4,1)S(1)} %copy-done.4), kind=kOutput, calls=%fused_computation.25 | convolution fusion | flops 4047962112 | bytes 7471176 | tf_op jit(solution)/shard_map/conv_general_dilated | solution.py:59
  70.7 0.5 copy.56
  71.2 0.0 copy-start.2
  71.2 0.2 slice.13
  71.4 0.4 copy-done.2
  71.8 2.5 %convert_reduce_fusion = f32[128,32,32]{0,1,2:T(8,128)S(1)} fusion(f32[128,1,32,2,32,2]{0,3,2,5,4,1:T(2,128)S(1)} %bitcast.45, f32[128]{0:T(128)S(1)} %copy-done.2), kind=kLoop, calls=%fused_computation.24 | loop fusion | flops 3538944 | bytes 2621952 | tf_op jit(solution)/shard_map/reduce_sum | solution.py:82
  74.3 0.1 multiply_convert_fusion
  74.4 0.1 copy.57
  74.5 0.5 broadcast.164
  75.0 0.8 reduce.1
  75.8 0.1 copy.69
  76.0 0.2 reshape.167
  76.1 18.2 %all_to_all.4 = bf16[16,2,4096]{2,1,0:T(2,128)(2,1)S(1)} all-to-all(bf16[16,2,4096]{2,1,0:T(2,128)(2,1)S(1)} %reshape.167), channel_id=1, replica_groups=mesh['space'=16,'chan'=16] {'chan'}, dimensions={0} | all-to-all | bytes 524288 | tf_op jit(solution)/shard_map/all_to_all | solution.py:83
  94.3 0.3 reshape.168
  94.6 0.1 bitcast_convert_fusion
  94.8 0.7 copy.60
  (2 shorter events, 0.1 us)
Async XLA Ops:
  0.0 61.5 %copy-start = (bf16[3,3,3,128,128]{4,3,2,1,0:T(8,128)(2,1)S(1)}, bf16[3,3,3,128,128]{4,3,2,1,0:T(8,128)(2,1)}, u32[]{:S(2)}) copy-start(bf16[3,3,3,128,128]{4,3,2,1,0:T(8,128)(2,1)} %param.8) | copy-start | bytes 2654212
  1.3 10.7 %collective-permute-start = (bf16[4,1,16384]{2,1,0:T(2,128)(2,1)S(1)}, bf16[4,1,16384]{2,1,0:T(2,128)(2,1)S(1)}, u32[]{:S(2)}, u32[]{:S(2)}) collective-permute-start(bf16[4,1,16384]{2,1,0:T(2,128)(2,1)S(1)} %slice.3), channel_id=1, source_target_pairs={{0,1},{1,2},{2,3},{3,4},{4,5},{5,6},{6,7},{7,8},{8,9},{9,10},{10,1... | collective-permute-start | bytes 393224 | tf_op jit(solution)/shard_map/ppermute | solution.py:12
  14.5 9.3 %copy-start.1 = (f32[128]{0:T(128)S(1)}, f32[128]{0:T(128)}, u32[]{:S(2)}) copy-start(f32[128]{0:T(128)} %param.7) | copy-start | bytes 1540
  14.5 9.3 %copy-start.3 = (bf16[3,3,3,4,128]{4,3,2,1,0:T(4,128)(2,1)S(1)}, bf16[3,3,3,4,128]{4,3,2,1,0:T(4,128)(2,1)}, u32[]{:S(2)}) copy-start(bf16[3,3,3,4,128]{4,3,2,1,0:T(4,128)(2,1)} %param.6) | copy-start | bytes 82948
  14.5 9.3 %copy-start.4 = (pred[8,9]{0,1:T(8,128)(4,1)S(1)}, pred[8,9]{0,1:T(8,128)(4,1)}, u32[]{:S(2)}) copy-start(pred[8,9]{0,1:T(8,128)(4,1)} %constant.21) | copy-start | bytes 220
  35.0 19.1 %collective-permute-start.1 = (bf16[128,1,4096]{0,2,1:T(8,128)(2,1)S(1)}, bf16[128,1,4096]{0,2,1:T(8,128)(2,1)S(1)}, u32[]{:S(2)}, u32[]{:S(2)}) collective-permute-start(bf16[128,1,4096]{0,2,1:T(8,128)(2,1)S(1)} %fusion.16), channel_id=1, source_target_pairs={{0,1},{1,2},{2,3},{3,4},{4,5},{5,6},{6,7},{7,8},{8,9},{9,10},{10,1... | collective-permute-start | bytes 3145736 | tf_op jit(solution)/shard_map/ppermute | solution.py:23
  36.9 19.0 %collective-permute-start.2 = (bf16[128,1,4096]{0,2,1:T(8,128)(2,1)S(1)}, bf16[128,1,4096]{0,2,1:T(8,128)(2,1)S(1)}, u32[]{:S(2)}, u32[]{:S(2)}) collective-permute-start(bf16[128,1,4096]{0,2,1:T(8,128)(2,1)S(1)} %fusion.16), channel_id=1, source_target_pairs={{1,0},{2,1},{3,2},{4,3},{5,4},{6,5},{7,6},{8,7},{9,8},{10,9},{11,1... | collective-permute-start | bytes 3145736 | tf_op jit(solution)/shard_map/ppermute | solution.py:24
  71.2 0.7 copy-start.2
where the time goes:
time: 95.8 us; the launch traced here: 95.5 us
  local copies, waits for them, and re-layouts  22.8 us (24%)
  waiting for transfers between devices  19.8 us (21%)
  blocking collectives  18.2 us (19%)
  matrix products  18.1 us (19%)
  starting transfers between devices  10.7 us (11%)
  other arithmetic  5.65 us (6%)
    all_to_all x1, blocking collectives, shards(): lax.all_to_all(lateral.astype(jnp.bfloat16), 'chan', split_axis=0, concat...  18.2 us
    conv_general_dilated x5, local copies, waits for them, and re-layouts, strided_conv(): lax.conv_general_dilated(grid, weights, (2, 2, 2), ((0, 0), (1, 0), (1, 0...  11.1 us
    ppermute x1, waiting for transfers between devices, with_halo(): lax.ppermute(last, axis, up)  9.3 us
    conv_general_dilated x1, matrix products, second_conv(): lax.conv_general_dilated(grid, weights, (1, 1, 1), ((0, 0), (1, 1), (1, 1...  9.19 us
    conv_general_dilated x1, matrix products, strided_conv(): lax.conv_general_dilated(grid, weights, (2, 2, 2), ((0, 0), (1, 0), (1, 0...  8.88 us
    ppermute x1, waiting for transfers between devices, from_behind(): return lax.ppermute(shard, axis, pairs)  8.77 us
    ppermute x1, starting transfers between devices, with_halo(): lax.ppermute(initial, axis, [(b, a) for a, b in up])  6.83 us
    unnamed x16, local copies, waits for them, and re-layouts  3.97 us
  transfers between devices with their start and end apart: 3, of which 3 were waited for; matrix products, arithmetic and copies ran while one was open for 1% of the time, Pallas kernels for 0%

commit v1 on v0

v1 whole, which is shorter than its diff:
```python
import functools

import jax
import jax.numpy as jnp
from jax import lax
from jax.experimental import pallas as pl
from jax.experimental.pallas import tpu as pltpu
from jax.sharding import PartitionSpec as P

SIDE = 128
AXES = ("space", "chan")
WINDOW = 72
STEPS = 17


def leaky_relu(value):
    return jnp.where(value > 0, value, 0.2 * value)


def one_hot(condition):
    return jnp.where(condition, 1.0, 0.0).astype(jnp.bfloat16)


def body(own, mate, near, far, extra, w1, b1, w2, b2, out, grid, pick, pool):
    core = lax.axis_index("chan") % 2
    pair = lax.axis_index("space") * (lax.axis_size("chan") // 2) + lax.axis_index("chan") // 2
    pairs = lax.axis_size("space") * (lax.axis_size("chan") // 2)
    upper = core == 1

    r = lax.broadcasted_iota(jnp.int32, (384, 256), 0)
    k = lax.broadcasted_iota(jnp.int32, (384, 256), 1)
    cell = r % 128
    pick[...] = one_hot(k == (cell // 64) * 128 + 2 * (cell % 64) - 1 + r // 128) * one_hot(k // 128 == cell // 64)
    r = lax.broadcasted_iota(jnp.int32, (128, 512), 0)
    k = lax.broadcasted_iota(jnp.int32, (128, 512), 1)
    pool[...] = one_hot(r == (k // 128) * 32 + (k % 64) // 2)

    bias1 = jnp.concatenate([b1[...]] * 4, axis=1)
    lane = lax.broadcasted_iota(jnp.int32, (128, 512), 1)
    cells = lax.broadcasted_iota(jnp.int32, (128, 512), 0)
    lowest = jnp.where(pair == 0, 128, 0)
    highest = jnp.where(pair == pairs - 1, 384, 512)
    plane_ok = (lane >= lowest) & (lane < highest)
    first_col = cells % 64 == 0
    last_col = cells % 64 == 63

    def first_rows(j, _):
        halves = []
        for half in range(2):
            parts = []
            for tap in range(3):
                row = 64 * core - 3 + 4 * j + tap + 2 * half
                at = jnp.clip(row, 0, SIDE - 1)
                a, b = own[at].astype(jnp.float32), mate[at].astype(jnp.float32)
                c, d = near[at].astype(jnp.float32), far[at].astype(jnp.float32)
                e = extra[jnp.clip(row - (SIDE - WINDOW) * core, 0, WINDOW - 1)].astype(jnp.float32)
                tile = [
                    jnp.where(upper, d, c),
                    jnp.where(upper, b, a),
                    jnp.where(upper, a, b),
                    jnp.where(upper, c, d),
                    jnp.concatenate([e, jnp.zeros((4, 128), jnp.float32)], axis=0),
                ]
                tile = jnp.concatenate(tile, axis=0)
                parts.append(jnp.where(row >= 0, tile, 0.0))
            parts.append(jnp.zeros((8, 128), jnp.float32))
            halves.append(jnp.concatenate(parts, axis=0))
        lines = jnp.concatenate(halves, axis=1).astype(jnp.bfloat16)
        picked = lax.dot_general(
            pick[...], lines, (((1,), (1,)), ((), ())), preferred_element_type=jnp.float32
        ).astype(jnp.bfloat16)
        patches = jnp.concatenate([picked[0:128], picked[128:256], picked[256:384]], axis=1)
        first = jnp.dot(patches, w1[...], preferred_element_type=jnp.float32)
        first = leaky_relu(first + bias1)
        index = 2 * j + cells // 64
        ok = plane_ok & (index >= jnp.where(upper, 0, 1)) & (index < jnp.where(upper, 33, 34))
        first = jnp.where(ok, first, 0.0)
        left = jnp.where(first_col, 0.0, pltpu.roll(first, 1, 0)).astype(jnp.bfloat16)
        right = jnp.where(last_col, 0.0, pltpu.roll(first, 127, 0)).astype(jnp.bfloat16)
        first = first.astype(jnp.bfloat16)
        rows = pl.ds(pl.multiple_of(j * 128, 128), 128)
        for plane in range(4):
            span = slice(plane * 128, plane * 128 + 128)
            grid[plane, rows, 0:128] = left[:, span]
            grid[plane, rows, 128:256] = first[:, span]
            grid[plane, rows, 256:384] = right[:, span]
        return 0

    lax.fori_loop(0, STEPS, first_rows, 0)

    bias2 = jnp.concatenate([b2[...]] * 2, axis=1)

    def second_rows(m, _):
        def rows_of(plane):
            return jnp.concatenate(
                [grid[plane, pl.ds(pl.multiple_of(m * 512 + tap * 64, 64), 512), :] for tap in range(3)], axis=1
            )

        both = jnp.dot(
            rows_of(1), jnp.concatenate([w2[1], w2[0]], axis=1), preferred_element_type=jnp.float32
        )
        both += jnp.dot(
            rows_of(2), jnp.concatenate([w2[2], w2[1]], axis=1), preferred_element_type=jnp.float32
        )
        low = jnp.dot(rows_of(0), w2[0], preferred_element_type=jnp.float32)
        high = jnp.dot(rows_of(3), w2[2], preferred_element_type=jnp.float32)
        both += jnp.concatenate([low, high], axis=1)
        active = leaky_relu(both + bias2).astype(jnp.bfloat16)
        sums = jnp.dot(pool[...], active, preferred_element_type=jnp.float32)
        mean = (sums[:, 0:128] + sums[:, 128:256]) * 0.125
        out[:, pl.ds(pl.multiple_of(m * 128, 128), 128)] = jnp.transpose(mean).astype(jnp.bfloat16)
        return 0

    lax.fori_loop(0, 4, second_rows, 0)


def convolve(own, mate, near, far, extra, w1, b1, w2, b2):
    vmem = pl.BlockSpec(memory_space=pltpu.VMEM)
    return pl.pallas_call(
        body,
        out_shape=jax.ShapeDtypeStruct((128, 512), jnp.bfloat16),
        in_specs=[vmem] * 9,
        out_specs=vmem,
        scratch_shapes=[
            pltpu.VMEM((4, STEPS * 128, 384), jnp.bfloat16),
            pltpu.VMEM((384, 256), jnp.bfloat16),
            pltpu.VMEM((128, 512), jnp.bfloat16),
        ],
        compiler_params=pltpu.CompilerParams(vmem_limit_bytes=40 << 20),
        cost_estimate=pl.CostEstimate(flops=12_000_000_000, bytes_accessed=4_000_000, transcendentals=0),
        name="convolve",
    )(own, mate, near, far, extra, w1, b1, w2, b2)


def spread_weights(weight):
    channels = weight.shape[4]
    taps = jnp.transpose(weight, (2, 1, 0, 3, 4)).reshape(3, 3, 12, channels)

    def pad(value, before, after):
        return jnp.pad(value, ((0, 0), (0, 0), (before, after), (0, 0)))

    planes = [
        pad(taps[:, :, 4:], 0, 32) + pad(taps[:, :, :4], 32, 4),
        pad(taps, 4, 24),
        pad(taps, 12, 16),
        pad(taps, 20, 8),
    ]
    spread = jnp.concatenate(planes, axis=3).reshape(3, 120, 4 * channels)
    return jnp.pad(spread, ((0, 0), (0, 8), (0, 0))).reshape(384, 4 * channels)


def shards(volume, conv1_weight, conv1_bias, conv2_weight, conv2_bias):
    peers = lax.axis_size("space") * lax.axis_size("chan")
    upper = lax.axis_index("chan") % 2 == 1
    own = jnp.transpose(volume.reshape(4, 2, SIDE, SIDE), (2, 1, 0, 3)).reshape(SIDE, 8, SIDE)
    near = lax.ppermute(own, AXES, [p for i in range(1, peers - 1, 2) for p in ((i, i + 1), (i + 1, i))])
    mate = lax.ppermute(own, AXES, [(i, i ^ 1) for i in range(peers)])
    part = jnp.where(upper, mate[SIDE - WINDOW :, 4:], own[:WINDOW, 4:])
    extra = lax.ppermute(part, AXES, [(i, i + 2) for i in range(peers - 2)])
    far = lax.ppermute(near, AXES, [(i, i ^ 1) for i in range(peers)])
    w1 = spread_weights(conv1_weight)
    half = convolve(
        own, mate, near, far, extra, w1, conv1_bias[None], conv2_weight.reshape(3, 1152, 128), conv2_bias[None]
    )
    moved = lax.all_to_all(half.reshape(16, 8, 512), "chan", split_axis=0, concat_axis=0, tiled=True)
    return jnp.transpose(moved.reshape(8, 2, 8, 512), (2, 0, 1, 3)).reshape(8, 8, 1024)


def solution(mesh):
    in_specs = (P(None, AXES, None), P(), P(), P(), P())
    out_specs = P("chan", "space", None)
    return jax.shard_map(shards, mesh=mesh, in_specs=in_specs, out_specs=out_specs, check_vma=False)
```

time: 95.8 us -> 52.2 us (0.54)
  the two profiles are of different devices: /device:TPU:96 before, /device:TPU:5 now
where the time goes in v1:
time: 52.2 us; the launch traced here: 51.9 us
  starting transfers between devices  16.1 us (31%)
  Pallas kernels  15.3 us (29%)
  blocking collectives  9.57 us (18%)
  waiting for transfers between devices  7.81 us (15%)
  local copies, waits for them, and re-layouts  2.85 us (5%)
    pallas_call x1, Pallas kernels, convolve(): pl.pallas_call(body, out_shape=jax.ShapeDtypeStruct((128, 512), jnp.bfloa...  15.3 us
    all_to_all x1, blocking collectives, shards(): lax.all_to_all(half.reshape(16, 8, 512), 'chan', split_axis=0, concat_axi...  9.57 us
    ppermute x1, waiting for transfers between devices, shards(): extra = lax.ppermute(part, AXES, [(i, i + 2) for i in range(peers - 2)])  7.8 us
    ppermute x1, starting transfers between devices, shards(): mate = lax.ppermute(own, AXES, [(i, i ^ 1) for i in range(peers)])  6.62 us
    ppermute x1, starting transfers between devices, shards(): far = lax.ppermute(near, AXES, [(i, i ^ 1) for i in range(peers)])  3.82 us
    ppermute x1, starting transfers between devices, shards(): lax.ppermute(own, AXES, [p for i in range(1, peers - 1, 2) for p in ((i,...  3.77 us
    ppermute x1, starting transfers between devices, shards(): extra = lax.ppermute(part, AXES, [(i, i + 2) for i in range(peers - 2)])  1.92 us
    reshape x2, local copies, waits for them, and re-layouts, shards(): volume.reshape(4, 2, SIDE, SIDE)  1.36 us
  transfers between devices with their start and end apart: 4, of which 1 were waited for; matrix products, arithmetic and copies ran while one was open for 0% of the time, Pallas kernels for 0%

profile of v1, /device:TPU:5, one launch (start us, length us, event | category | flops | bytes accessed | tf_op | source)
XLA Modules:
  0.0 51.9 jit_solution(9914501462698402037)
XLA Ops:
  0.0 1.2 %reshape.27 = bf16[4,2,128,128]{3,2,1,0:T(8,128)(2,1)S(1)} reshape(bf16[4,2,16384]{2,1,0:T(2,128)(2,1)} %param.5) | data formatting | bytes 524288 | tf_op jit(solution)/shard_map/reshape | solution.py:155
  1.2 0.0 copy-start.3
  1.2 0.2 copy.8
  1.4 3.8 %collective-permute-start.1 = (bf16[128,8,128]{2,1,0:T(8,128)(2,1)S(1)}, bf16[128,8,128]{2,1,0:T(8,128)(2,1)S(1)}, u32[]{:S(2)}, u32[]{:S(2)}) collective-permute-start(bf16[128,8,128]{2,1,0:T(8,128)(2,1)S(1)} %bitcast.14), channel_id=1, source_target_pairs={{1,2},{2,1},{3,4},{4,3},{5,6},{6,5},{7,8},{8,7},{9,10},{10,9},{11,... | collective-permute-start | bytes 786440 | tf_op jit(solution)/shard_map/ppermute | solution.py:156
  5.2 6.6 %collective-permute-start = (bf16[128,8,128]{2,1,0:T(8,128)(2,1)S(1)}, bf16[128,8,128]{2,1,0:T(8,128)(2,1)S(1)}, u32[]{:S(2)}, u32[]{:S(2)}) collective-permute-start(bf16[128,8,128]{2,1,0:T(8,128)(2,1)S(1)} %bitcast.15), channel_id=1, source_target_pairs={{0,1},{1,0},{2,3},{3,2},{4,5},{5,4},{6,7},{7,6},{8,9},{9,8},{10,11... | collective-permute-start | bytes 786440 | tf_op jit(solution)/shard_map/ppermute | solution.py:157
  11.8 0.0 copy-done.3
  11.8 0.0 copy-start
  11.9 0.0 collective-permute-done.1.near
  11.9 3.8 %collective-permute-start.2 = (bf16[128,8,128]{2,1,0:T(8,128)(2,1)S(1)}, bf16[128,8,128]{2,1,0:T(8,128)(2,1)S(1)}, u32[]{:S(2)}, u32[]{:S(2)}) collective-permute-start(bf16[128,8,128]{2,1,0:T(8,128)(2,1)S(1)} %collective-permute-done.1.near), channel_id=1, source_target_pairs={{0,1},{1,0},{2,3},{3,2},{4,5},{5,4},{6,7},{7,6},{8,9},{9,8},{10,11... | collective-permute-start | bytes 786440 | tf_op jit(solution)/shard_map/ppermute | solution.py:160
  15.7 0.0 collective-permute-done.mate
  15.7 0.1 slice_select_fusion
  15.8 1.9 %collective-permute-start.3 = (bf16[72,4,128]{2,1,0:T(4,128)(2,1)S(1)}, bf16[72,4,128]{2,1,0:T(4,128)(2,1)S(1)}, u32[]{:S(2)}, u32[]{:S(2)}) collective-permute-start(bf16[72,4,128]{2,1,0:T(4,128)(2,1)S(1)} %slice_select_fusion), channel_id=1, source_target_pairs={{0,2},{1,3},{2,4},{3,5},{4,6},{5,7},{6,8},{7,9},{8,10},{9,11},{10,... | collective-permute-start | bytes 221192 | tf_op jit(solution)/shard_map/ppermute | solution.py:159
  17.8 0.1 fusion.6
  17.9 7.8 %collective-permute-done.3.extra = bf16[72,4,128]{2,1,0:T(4,128)(2,1)S(1)} collective-permute-done((bf16[72,4,128]{2,1,0:T(4,128)(2,1)S(1)}, bf16[72,4,128]{2,1,0:T(4,128)(2,1)S(1)}, u32[]{:S(2)}, u32[]{:S(2)}) %collective-permute-start.3) | collective-permute-done | bytes 73760 | tf_op jit(solution)/shard_map/ppermute | solution.py:159
  25.7 0.0 collective-permute-done.2.far
  25.7 0.0 copy-start.1
  25.7 0.0 copy-start.2
  25.7 0.0 copy-done
  25.7 0.6 %copy-done.1 = f32[128]{0:T(128)S(1)} copy-done((f32[128]{0:T(128)S(1)}, f32[128]{0:T(128)}, u32[]{:S(2)}) %copy-start.1) | copy-done | bytes 536
  26.3 0.0 copy-done.2
  26.3 15.3 %convolve.1 = bf16[128,512]{1,0:T(8,128)(2,1)S(1)} custom-call(bf16[128,8,128]{2,1,0:T(8,128)(2,1)S(1)} %bitcast.17, bf16[128,8,128]{2,1,0:T(8,128)(2,1)S(1)} %collective-permute-done.mate, bf16[128,8,128]{2,1,0:T(8,128)(2,1)S(1)} %collective-permute-done.1.near, bf16[128,8,128]{2,1,0:T(8,128)(2,1)S(1)} %collective-permute-done.2.far, ...), custom_call_target="tpu_custom_call" | custom-call | flops 12000000000 | bytes 4000000 | tf_op jit(solution)/shard_map/convolve/pallas_call | solution.py:119
  41.6 9.6 %all_to_all.5 = bf16[16,8,512]{2,1,0:T(8,128)(2,1)S(1)} all-to-all(bf16[16,8,512]{2,1,0:T(8,128)(2,1)S(1)} %bitcast.19), channel_id=1, replica_groups=mesh['space'=16,'chan'=16] {'chan'}, dimensions={0} | all-to-all | bytes 262144 | tf_op jit(solution)/shard_map/all_to_all | solution.py:165
  51.2 0.7 %copy.10 = bf16[8,2,8,512]{3,0,1,2:T(8,128)(2,1)} copy(bf16[8,2,8,512]{3,2,1,0:T(8,128)(2,1)S(1)} %bitcast.24) | data formatting | bytes 262144 | tf_op jit(solution)/shard_map/reshape | solution.py:166
  (6 shorter events, 0.1 us)
Async XLA Ops:
  1.2 10.6 %copy-start.3 = (bf16[3,3,3,4,128]{4,3,2,1,0:T(4,128)(2,1)S(1)}, bf16[3,3,3,4,128]{4,3,2,1,0:T(4,128)(2,1)}, u32[]{:S(2)}) copy-start(bf16[3,3,3,4,128]{4,3,2,1,0:T(4,128)(2,1)} %param.6) | copy-start | bytes 82948
  1.4 10.5 %collective-permute-start.1 = (bf16[128,8,128]{2,1,0:T(8,128)(2,1)S(1)}, bf16[128,8,128]{2,1,0:T(8,128)(2,1)S(1)}, u32[]{:S(2)}, u32[]{:S(2)}) collective-permute-start(bf16[128,8,128]{2,1,0:T(8,128)(2,1)S(1)} %bitcast.14), channel_id=1, source_target_pairs={{1,2},{2,1},{3,4},{4,3},{5,6},{6,5},{7,8},{8,7},{9,10},{10,9},{11,... | collective-permute-start | bytes 786440 | tf_op jit(solution)/shard_map/ppermute | solution.py:156
  5.2 10.6 %collective-permute-start = (bf16[128,8,128]{2,1,0:T(8,128)(2,1)S(1)}, bf16[128,8,128]{2,1,0:T(8,128)(2,1)S(1)}, u32[]{:S(2)}, u32[]{:S(2)}) collective-permute-start(bf16[128,8,128]{2,1,0:T(8,128)(2,1)S(1)} %bitcast.15), channel_id=1, source_target_pairs={{0,1},{1,0},{2,3},{3,2},{4,5},{5,4},{6,7},{7,6},{8,9},{9,8},{10,11... | collective-permute-start | bytes 786440 | tf_op jit(solution)/shard_map/ppermute | solution.py:157
  11.8 13.9 %copy-start = (bf16[3,3,3,128,128]{4,3,2,1,0:T(8,128)(2,1)S(1)}, bf16[3,3,3,128,128]{4,3,2,1,0:T(8,128)(2,1)}, u32[]{:S(2)}) copy-start(bf16[3,3,3,128,128]{4,3,2,1,0:T(8,128)(2,1)} %param.8) | copy-start | bytes 2654212
  11.9 13.8 %collective-permute-start.2 = (bf16[128,8,128]{2,1,0:T(8,128)(2,1)S(1)}, bf16[128,8,128]{2,1,0:T(8,128)(2,1)S(1)}, u32[]{:S(2)}, u32[]{:S(2)}) collective-permute-start(bf16[128,8,128]{2,1,0:T(8,128)(2,1)S(1)} %collective-permute-done.1.near), channel_id=1, source_target_pairs={{0,1},{1,0},{2,3},{3,2},{4,5},{5,4},{6,7},{7,6},{8,9},{9,8},{10,11... | collective-permute-start | bytes 786440 | tf_op jit(solution)/shard_map/ppermute | solution.py:160
  15.8 9.8 %collective-permute-start.3 = (bf16[72,4,128]{2,1,0:T(4,128)(2,1)S(1)}, bf16[72,4,128]{2,1,0:T(4,128)(2,1)S(1)}, u32[]{:S(2)}, u32[]{:S(2)}) collective-permute-start(bf16[72,4,128]{2,1,0:T(4,128)(2,1)S(1)} %slice_select_fusion), channel_id=1, source_target_pairs={{0,2},{1,3},{2,4},{3,5},{4,6},{5,7},{6,8},{7,9},{8,10},{9,11},{10,... | collective-permute-start | bytes 221192 | tf_op jit(solution)/shard_map/ppermute | solution.py:159
  25.7 0.7 %copy-start.1 = (f32[128]{0:T(128)S(1)}, f32[128]{0:T(128)}, u32[]{:S(2)}) copy-start(f32[128]{0:T(128)} %param.7) | copy-start | bytes 1540
  25.7 0.7 %copy-start.2 = (f32[128]{0:T(128)S(1)}, f32[128]{0:T(128)}, u32[]{:S(2)}) copy-start(f32[128]{0:T(128)} %param.9) | copy-start | bytes 1540

commit v2 on v1

v2 whole, which is shorter than its diff:
```python
import jax
import jax.numpy as jnp
import numpy as np
from jax import lax
from jax.experimental import pallas as pl
from jax.experimental.pallas import tpu as pltpu
from jax.sharding import PartitionSpec as P

SIDE = 128
AXES = ("space", "chan")
WINDOW = 67
ROWS = 36
LINE = 40
LINES = 2960


def leaky_relu(value):
    return jnp.maximum(value, 0.2 * value)


def column(place):
    return 8 * (place % 8) + place // 8


def pick_matrix():
    row, source = np.arange(384)[:, None], np.arange(256)[None, :]
    half, place = row % 128 // 64, row % 64
    wanted = 2 * column(place) - 1 + row // 128
    return (source // 128 == half) & (source % 128 == wanted)


def pool_matrix():
    pooled, cell = np.arange(128)[:, None], np.arange(512)[None, :]
    return pooled == cell // 128 * 32 + column(cell % 64) // 2


def body(below, low, high, above, w1, b1, w2, b2, pick, pool, out, lines, center, shift):
    core = lax.axis_index("chan") % 2
    pair = lax.axis_index("space") * (lax.axis_size("chan") // 2) + lax.axis_index("chan") // 2
    pairs = lax.axis_size("space") * (lax.axis_size("chan") // 2)

    lines[0:3] = jnp.zeros((3, LINE, 128), jnp.float32)
    lines[67:74] = jnp.zeros((7, LINE, 128), jnp.float32)
    span = pl.ds(3 - 3 * core, WINDOW)
    lines[span, 0:12] = jnp.where(pair == 0, 0.0, below[...].astype(jnp.float32))
    lines[span, 12:16] = jnp.zeros((WINDOW, 4, 128), jnp.float32)
    lines[span, 16:24] = low[...].astype(jnp.float32)
    lines[span, 24:32] = high[...].astype(jnp.float32)
    lines[span, 32:40] = above[...].astype(jnp.float32)
    flat = lines.reshape(LINES, 128)

    bias1 = jnp.concatenate([b1[...]] * 4, axis=1)
    sublane = lax.broadcasted_iota(jnp.int32, (8, 512), 0)

    def first_rows(step, _):
        taken = []
        for j in range(2):
            at = step * 320 + j * 160
            taken.append(
                jnp.concatenate(
                    [flat[pl.ds(pl.multiple_of(at, 16), 128)], flat[pl.ds(pl.multiple_of(at + 80, 16), 128)]], axis=1
                )
            )
        taken = jnp.concatenate(taken, axis=0).astype(jnp.bfloat16)
        picked = lax.dot_general(
            pick[...], taken, (((1,), (1,)), ((), ())), preferred_element_type=jnp.float32
        ).astype(jnp.bfloat16)
        patches = jnp.concatenate(
            [
                jnp.concatenate([picked[tap * 128 : tap * 128 + 128, j * 128 : j * 128 + 128] for tap in range(3)], axis=1)
                for j in range(2)
            ],
            axis=0,
        )
        first = jnp.dot(patches, w1[...], preferred_element_type=jnp.float32)
        first = leaky_relu(first + bias1)
        for r in range(4):
            row = first[r * 64 : r * 64 + 64]
            before = jnp.where(sublane == 0, 0.0, pltpu.roll(row[56:64], 1, 0))
            after = jnp.where(sublane == 7, 0.0, pltpu.roll(row[0:8], 7, 0))
            wide = jnp.concatenate([before, row, after], axis=0).astype(jnp.bfloat16)
            row = row.astype(jnp.bfloat16)
            index = step * 4 + r
            for plane in range(4):
                lanes = slice(plane * 128, plane * 128 + 128)
                center[plane, pl.ds(pl.multiple_of(index * 64, 64), 64), :] = row[:, lanes]
                shift[plane, pl.ds(pl.multiple_of(index * 80, 16), 80), :] = wide[:, lanes]
        return 0

    lax.fori_loop(0, ROWS // 4, first_rows, 0)

    @pl.when(core == 0)
    def _():
        center[:, 0:64, :] = jnp.zeros((4, 64, 128), jnp.bfloat16)
        shift[:, 0:80, :] = jnp.zeros((4, 80, 128), jnp.bfloat16)

    @pl.when(core == 1)
    def _():
        center[:, 33 * 64 : 34 * 64, :] = jnp.zeros((4, 64, 128), jnp.bfloat16)
        shift[:, 33 * 80 : 34 * 80, :] = jnp.zeros((4, 80, 128), jnp.bfloat16)

    @pl.when(pair == 0)
    def _():
        center[0] = jnp.zeros((ROWS * 64, 128), jnp.bfloat16)
        shift[0] = jnp.zeros((ROWS * 80, 128), jnp.bfloat16)

    @pl.when(pair == pairs - 1)
    def _():
        center[3] = jnp.zeros((ROWS * 64, 128), jnp.bfloat16)
        shift[3] = jnp.zeros((ROWS * 80, 128), jnp.bfloat16)

    bias2 = jnp.concatenate([b2[...]] * 2, axis=1)
    nothing = jnp.zeros((384, 128), jnp.bfloat16)

    def second_rows(m, _):
        def taps_of(plane, rows):
            pieces = [
                [shift[plane, pl.ds(pl.multiple_of((m * 8 + r) * 80, 16), 64), :] for r in rows],
                [center[plane, pl.ds(pl.multiple_of((m * 8 + r) * 64, 64), 64), :] for r in rows],
                [shift[plane, pl.ds(pl.multiple_of((m * 8 + r) * 80 + 16, 16), 64), :] for r in rows],
            ]
            return [jnp.concatenate(p, axis=0) for p in pieces]

        def all_taps(plane):
            return [x for tap in range(3) for x in taps_of(plane, range(tap, tap + 8))]

        both = jnp.dot(
            jnp.concatenate(all_taps(1), axis=1), jnp.concatenate([w2[1], w2[0]], axis=1), preferred_element_type=jnp.float32
        )
        both += jnp.dot(
            jnp.concatenate(all_taps(2), axis=1), jnp.concatenate([w2[2], w2[1]], axis=1), preferred_element_type=jnp.float32
        )

        def row_pairs(plane, depth_tap):
            lines_of = jnp.concatenate([x for tap in range(4) for x in taps_of(plane, range(tap, tap + 8, 2))], axis=1)
            w = [w2[depth_tap, tap * 384 : tap * 384 + 384] for tap in range(3)]
            weights = jnp.concatenate(
                [
                    jnp.concatenate(w + [nothing], axis=0),
                    jnp.concatenate([nothing] + w, axis=0),
                ],
                axis=1,
            )
            pairs_of = jnp.dot(lines_of, weights, preferred_element_type=jnp.float32)
            return jnp.concatenate(
                [pairs_of[i * 64 : i * 64 + 64, h * 128 : h * 128 + 128] for i in range(4) for h in range(2)], axis=0
            )

        both += jnp.concatenate([row_pairs(0, 0), row_pairs(3, 2)], axis=1)
        active = leaky_relu(both + bias2).astype(jnp.bfloat16)
        sums = jnp.dot(pool[...], active, preferred_element_type=jnp.float32)
        mean = (sums[:, 0:128] + sums[:, 128:256]) * 0.125
        out[:, pl.ds(pl.multiple_of(m * 128, 128), 128)] = jnp.transpose(mean).astype(jnp.bfloat16)
        return 0

    lax.fori_loop(0, 4, second_rows, 0)


def convolve(*operands):
    vmem = pl.BlockSpec(memory_space=pltpu.VMEM)
    return pl.pallas_call(
        body,
        out_shape=jax.ShapeDtypeStruct((128, 512), jnp.bfloat16),
        in_specs=[vmem] * len(operands),
        out_specs=vmem,
        scratch_shapes=[
            pltpu.VMEM((LINES // LINE, LINE, 128), jnp.float32),
            pltpu.VMEM((4, ROWS * 64, 128), jnp.bfloat16),
            pltpu.VMEM((4, ROWS * 80, 128), jnp.bfloat16),
        ],
        compiler_params=pltpu.CompilerParams(vmem_limit_bytes=40 << 20),
        cost_estimate=pl.CostEstimate(flops=12_000_000_000, bytes_accessed=4_000_000, transcendentals=0),
        name="convolve",
    )(*operands)


def spread_weights(weight):
    channels = weight.shape[4]
    taps = jnp.transpose(weight, (2, 1, 0, 3, 4)).reshape(3, 3, 12, channels)

    def pad(value, before, after):
        return jnp.pad(value, ((0, 0), (0, 0), (before, after), (0, 0)))

    planes = [
        pad(taps, 0, 28),
        pad(taps[:, :, :4], 8, 28) + pad(taps[:, :, 4:], 16, 16),
        pad(taps, 20, 8),
        pad(taps, 28, 0),
    ]
    spread = jnp.concatenate(planes, axis=3).reshape(3, 120, 4 * channels)
    return jnp.pad(spread, ((0, 0), (0, 8), (0, 0))).reshape(384, 4 * channels)


def shards(volume, conv1_weight, conv1_bias, conv2_weight, conv2_bias):
    peers = lax.axis_size("space") * lax.axis_size("chan")
    upper = lax.axis_index("chan") % 2 == 1
    own = jnp.transpose(volume.reshape(4, 2, SIDE, SIDE), (2, 1, 0, 3)).reshape(SIDE, 8, SIDE)
    mate = lax.ppermute(own, AXES, [(i, i ^ 1) for i in range(peers)])
    low = jnp.where(upper, mate[SIDE - WINDOW :], own[:WINDOW])
    high = jnp.where(upper, own[SIDE - WINDOW :], mate[:WINDOW])
    upward = jnp.concatenate([low[:, 4:], high], axis=1)
    below = lax.ppermute(upward, AXES, [(i, (i + 2) % peers) for i in range(peers)])
    above = lax.ppermute(low, AXES, [((i + 2) % peers, i) for i in range(peers)])
    half = convolve(
        below,
        low,
        high,
        above,
        spread_weights(conv1_weight),
        conv1_bias[None],
        conv2_weight.reshape(3, 1152, 128),
        conv2_bias[None],
        jnp.asarray(pick_matrix(), jnp.bfloat16),
        jnp.asarray(pool_matrix(), jnp.bfloat16),
    )
    moved = lax.all_to_all(half.reshape(16, 8, 512), "chan", split_axis=0, concat_axis=0, tiled=True)
    return jnp.transpose(moved.reshape(8, 2, 8, 512), (2, 0, 1, 3)).reshape(8, 8, 1024)


def solution(mesh):
    in_specs = (P(None, AXES, None), P(), P(), P(), P())
    out_specs = P("chan", "space", None)
    return jax.shard_map(shards, mesh=mesh, in_specs=in_specs, out_specs=out_specs, check_vma=False)
```

time: 52.2 us -> 50.9 us (0.975)
  the two profiles are of different devices: /device:TPU:5 before, /device:TPU:1 now
where the time goes in v2:
time: 50.9 us; the launch traced here: 50.7 us
  waiting for transfers between devices  13.7 us (27%)
  starting transfers between devices  12 us (24%)
  Pallas kernels  11.5 us (23%)
  blocking collectives  10.1 us (20%)
  local copies, waits for them, and re-layouts  2.98 us (6%)
    pallas_call x1, Pallas kernels, convolve(): pl.pallas_call(body, out_shape=jax.ShapeDtypeStruct((128, 512), jnp.bfloa...  11.5 us
    ppermute x1, waiting for transfers between devices, shards(): lax.ppermute(upward, AXES, [(i, (i + 2) % peers) for i in range(peers)])  10.5 us
    all_to_all x1, blocking collectives, shards(): lax.all_to_all(half.reshape(16, 8, 512), 'chan', split_axis=0, concat_axi...  10.1 us
    ppermute x1, starting transfers between devices, shards(): lax.ppermute(low, AXES, [((i + 2) % peers, i) for i in range(peers)])  8.59 us
    ppermute x1, starting transfers between devices, shards(): mate = lax.ppermute(own, AXES, [(i, i ^ 1) for i in range(peers)])  3.29 us
    ppermute x1, waiting for transfers between devices, shards(): lax.ppermute(low, AXES, [((i + 2) % peers, i) for i in range(peers)])  2.28 us
    reshape x2, local copies, waits for them, and re-layouts, shards(): volume.reshape(4, 2, SIDE, SIDE)  1.36 us
  transfers between devices with their start and end apart: 3, of which 3 were waited for; matrix products, arithmetic and copies ran while one was open for 1% of the time, Pallas kernels for 0%

profile of v2, /device:TPU:1, one launch (start us, length us, event | category | flops | bytes accessed | tf_op | source)
XLA Modules:
  0.0 50.7 jit_solution(11259192017113698479)
XLA Ops:
  0.0 1.2 %reshape.29 = bf16[4,2,128,128]{3,2,1,0:T(8,128)(2,1)S(1)} reshape(bf16[4,2,16384]{2,1,0:T(2,128)(2,1)} %param.7) | data formatting | bytes 524288 | tf_op jit(solution)/shard_map/reshape | solution.py:197
  1.2 0.0 copy-start.5
  1.2 0.2 copy.15
  1.4 3.3 %collective-permute-start = (bf16[128,8,128]{2,1,0:T(8,128)(2,1)S(1)}, bf16[128,8,128]{2,1,0:T(8,128)(2,1)S(1)}, u32[]{:S(2)}, u32[]{:S(2)}) collective-permute-start(bf16[128,8,128]{2,1,0:T(8,128)(2,1)S(1)} %bitcast.23), channel_id=1, source_target_pairs={{0,1},{1,0},{2,3},{3,2},{4,5},{5,4},{6,7},{7,6},{8,9},{9,8},{10,11... | collective-permute-start | bytes 786440 | tf_op jit(solution)/shard_map/ppermute | solution.py:198
  4.7 0.0 copy-done.5
  4.8 0.1 fusion.7
  4.9 1.0 %collective-permute-done = bf16[128,8,128]{2,1,0:T(8,128)(2,1)S(1)} collective-permute-done((bf16[128,8,128]{2,1,0:T(8,128)(2,1)S(1)}, bf16[128,8,128]{2,1,0:T(8,128)(2,1)S(1)}, u32[]{:S(2)}, u32[]{:S(2)}) %collective-permute-start) | collective-permute-done | bytes 262176 | tf_op jit(solution)/shard_map/ppermute | solution.py:198
  5.8 0.1 slice_select_fusion.1
  6.0 8.6 %collective-permute-start.2 = (bf16[67,8,128]{2,1,0:T(8,128)(2,1)S(1)}, bf16[67,8,128]{2,1,0:T(8,128)(2,1)S(1)}, u32[]{:S(2)}, u32[]{:S(2)}) collective-permute-start(bf16[67,8,128]{2,1,0:T(8,128)(2,1)S(1)} %get-tuple-element.5.low), channel_id=1, source_target_pairs={{2,0},{3,1},{4,2},{5,3},{6,4},{7,5},{8,6},{9,7},{10,8},{11,9},{12,... | collective-permute-start | bytes 411656 | tf_op jit(solution)/shard_map/ppermute | solution.py:203
  14.6 0.0 copy-start
  14.6 0.1 pad_maximum_fusion
  14.7 0.1 collective-permute-start.1
  14.8 0.1 fusion.5
  14.8 0.0 copy-start.3
  14.8 0.0 copy-start.4
  14.9 2.3 %collective-permute-done.2.above = bf16[67,8,128]{2,1,0:T(8,128)(2,1)S(1)} collective-permute-done((bf16[67,8,128]{2,1,0:T(8,128)(2,1)S(1)}, bf16[67,8,128]{2,1,0:T(8,128)(2,1)S(1)}, u32[]{:S(2)}, u32[]{:S(2)}) %collective-permute-start.2) | collective-permute-done | bytes 137248 | tf_op jit(solution)/shard_map/ppermute | solution.py:203
  17.2 10.5 %collective-permute-done.1.below = bf16[67,12,128]{2,1,0:T(8,128)(2,1)S(1)} collective-permute-done((bf16[67,12,128]{2,1,0:T(8,128)(2,1)S(1)}, bf16[67,12,128]{2,1,0:T(8,128)(2,1)S(1)}, u32[]{:S(2)}, u32[]{:S(2)}) %collective-permute-start.1) | collective-permute-done | bytes 205856 | tf_op jit(solution)/shard_map/ppermute | solution.py:202
  27.6 0.0 copy-start.1
  27.6 0.0 copy-start.2
  27.6 0.0 copy-done
  27.6 0.0 copy-done.3
  27.7 0.0 copy-done.4
  27.7 0.6 %copy-done.1 = f32[128]{0:T(128)S(1)} copy-done((f32[128]{0:T(128)S(1)}, f32[128]{0:T(128)}, u32[]{:S(2)}) %copy-start.1) | copy-done | bytes 536
  28.3 0.0 copy-done.2
  28.3 11.5 %convolve.1 = bf16[128,512]{1,0:T(8,128)(2,1)S(1)} custom-call(bf16[67,12,128]{2,1,0:T(8,128)(2,1)S(1)} %collective-permute-done.1.below, bf16[67,8,128]{2,1,0:T(8,128)(2,1)S(1)} %get-tuple-element.5.low, bf16[67,8,128]{2,1,0:T(8,128)(2,1)S(1)} %get-tuple-element.6.high, bf16[67,8,128]{2,1,0:T(8,128)(2,1)S(1)} %collective-permute-done.2.above, ...), custom_call_target="tpu_custom_call" | custom-call | flops 12000000000 | bytes 4000000 | tf_op jit(solution)/shard_map/convolve/pallas_call | solution.py:161
  39.8 10.1 %all_to_all.5 = bf16[16,8,512]{2,1,0:T(8,128)(2,1)S(1)} all-to-all(bf16[16,8,512]{2,1,0:T(8,128)(2,1)S(1)} %bitcast.18), channel_id=1, replica_groups=mesh['space'=16,'chan'=16] {'chan'}, dimensions={0} | all-to-all | bytes 262144 | tf_op jit(solution)/shard_map/all_to_all | solution.py:216
  50.0 0.7 %copy.12 = bf16[8,2,8,512]{3,0,1,2:T(8,128)(2,1)} copy(bf16[8,2,8,512]{3,2,1,0:T(8,128)(2,1)S(1)} %bitcast.27) | data formatting | bytes 262144 | tf_op jit(solution)/shard_map/reshape | solution.py:217
  (7 shorter events, 0.1 us)
Async XLA Ops:
  1.2 3.5 %copy-start.5 = (bf16[3,3,3,4,128]{4,3,2,1,0:T(4,128)(2,1)S(1)}, bf16[3,3,3,4,128]{4,3,2,1,0:T(4,128)(2,1)}, u32[]{:S(2)}) copy-start(bf16[3,3,3,4,128]{4,3,2,1,0:T(4,128)(2,1)} %param.8) | copy-start | bytes 82948
  1.4 4.5 %collective-permute-start = (bf16[128,8,128]{2,1,0:T(8,128)(2,1)S(1)}, bf16[128,8,128]{2,1,0:T(8,128)(2,1)S(1)}, u32[]{:S(2)}, u32[]{:S(2)}) collective-permute-start(bf16[128,8,128]{2,1,0:T(8,128)(2,1)S(1)} %bitcast.23), channel_id=1, source_target_pairs={{0,1},{1,0},{2,3},{3,2},{4,5},{5,4},{6,7},{7,6},{8,9},{9,8},{10,11... | collective-permute-start | bytes 786440 | tf_op jit(solution)/shard_map/ppermute | solution.py:198
  6.0 11.2 %collective-permute-start.2 = (bf16[67,8,128]{2,1,0:T(8,128)(2,1)S(1)}, bf16[67,8,128]{2,1,0:T(8,128)(2,1)S(1)}, u32[]{:S(2)}, u32[]{:S(2)}) collective-permute-start(bf16[67,8,128]{2,1,0:T(8,128)(2,1)S(1)} %get-tuple-element.5.low), channel_id=1, source_target_pairs={{2,0},{3,1},{4,2},{5,3},{6,4},{7,5},{8,6},{9,7},{10,8},{11,9},{12,... | collective-permute-start | bytes 411656 | tf_op jit(solution)/shard_map/ppermute | solution.py:203
  14.6 13.1 %copy-start = (bf16[3,3,3,128,128]{4,3,2,1,0:T(8,128)(2,1)S(1)}, bf16[3,3,3,128,128]{4,3,2,1,0:T(8,128)(2,1)}, u32[]{:S(2)}) copy-start(bf16[3,3,3,128,128]{4,3,2,1,0:T(8,128)(2,1)} %param.10) | copy-start | bytes 2654212
  14.7 13.0 %collective-permute-start.1 = (bf16[67,12,128]{2,1,0:T(8,128)(2,1)S(1)}, bf16[67,12,128]{2,1,0:T(8,128)(2,1)S(1)}, u32[]{:S(2)}, u32[]{:S(2)}) collective-permute-start(bf16[67,12,128]{2,1,0:T(8,128)(2,1)S(1)} %pad_maximum_fusion), channel_id=1, source_target_pairs={{0,2},{1,3},{2,4},{3,5},{4,6},{5,7},{6,8},{7,9},{8,10},{9,11},{10,... | collective-permute-start | bytes 617480 | tf_op jit(solution)/shard_map/ppermute | solution.py:202
  14.8 12.8 %copy-start.3 = (bf16[384,256]{1,0:T(8,128)(2,1)S(1)}, bf16[384,256]{1,0:T(8,128)(2,1)}, u32[]{:S(2)}) copy-start(bf16[384,256]{1,0:T(8,128)(2,1)} %constant.25.clone.pick) | copy-start | bytes 589828
  14.8 12.8 %copy-start.4 = (bf16[128,512]{1,0:T(8,128)(2,1)S(1)}, bf16[128,512]{1,0:T(8,128)(2,1)}, u32[]{:S(2)}) copy-start(bf16[128,512]{1,0:T(8,128)(2,1)} %constant.26.clone.pool) | copy-start | bytes 393220
  27.6 0.7 %copy-start.1 = (f32[128]{0:T(128)S(1)}, f32[128]{0:T(128)}, u32[]{:S(2)}) copy-start(f32[128]{0:T(128)} %param.9) | copy-start | bytes 1540
  27.6 0.7 %copy-start.2 = (f32[128]{0:T(128)S(1)}, f32[128]{0:T(128)}, u32[]{:S(2)}) copy-start(f32[128]{0:T(128)} %param.11) | copy-start | bytes 1540

commit v3 on v2

v3 whole, which is shorter than its diff:
```python
import jax
import jax.numpy as jnp
import numpy as np
from jax import lax
from jax.experimental import pallas as pl
from jax.experimental.pallas import tpu as pltpu
from jax.sharding import PartitionSpec as P

SIDE = 128
AXES = ("space", "chan")
WINDOW = 67
ROWS = 36
LINE = 40
LINES = 2960


def leaky_relu(value):
    return jnp.maximum(value, 0.2 * value)


def column(place):
    return 8 * (place % 8) + place // 8


def pick_matrix():
    row, source = np.arange(384)[:, None], np.arange(256)[None, :]
    half, place = row % 128 // 64, row % 64
    wanted = 2 * column(place) - 1 + row // 128
    return (source // 128 == half) & (source % 128 == wanted)


def order_matrix():
    pooled, place = np.arange(256)[:, None], np.arange(256)[None, :]
    return (pooled // 32 == place // 32) & (pooled % 32 == 4 * (place % 8) + place % 32 // 8)


def body(first_swap, second_swap, low, high, w1, b1, w2, b2, pick, order, out, lines, patches, center, shift):
    sums = pltpu.ACC
    pl.run_scoped(
        lambda *accumulators: compute(
            (accumulators[:16], accumulators[16:]),
            *(first_swap, second_swap, low, high, w1, b1, w2, b2, pick, order, out, lines, patches, center, shift),
        ),
        *[sums(unit)((64, 256), jnp.float32) for unit in range(2) for _ in range(16)],
    )


def compute(
    acc, first_swap, second_swap, low, high, w1, b1, w2, b2, pick, order, out, lines, patches, center, shift
):
    core = lax.axis_index("chan") % 2
    pair = lax.axis_index("space") * (lax.axis_size("chan") // 2) + lax.axis_index("chan") // 2
    pairs = lax.axis_size("space") * (lax.axis_size("chan") // 2)
    odd = pair % 2 == 1

    lines[0:3] = jnp.zeros((3, LINE, 128), jnp.float32)
    lines[67:74] = jnp.zeros((7, LINE, 128), jnp.float32)
    span = pl.ds(3 - 3 * core, WINDOW)
    one, two = first_swap[...].astype(jnp.float32), second_swap[...].astype(jnp.float32)
    lines[span, 0:12] = jnp.where(pair == 0, 0.0, jnp.where(odd, one, two))
    lines[span, 12:16] = jnp.zeros((WINDOW, 4, 128), jnp.float32)
    lines[span, 16:24] = low[...].astype(jnp.float32)
    lines[span, 24:32] = high[...].astype(jnp.float32)
    lines[span, 32:40] = jnp.where(odd, two[:, :8], one[:, :8])
    flat = lines.reshape(LINES, 128)

    for step in range(ROWS // 4):
        unit, base = step % 2, step // 2 % 2 * 6
        taken = []
        for j in range(2):
            at = step * 320 + j * 160
            taken.append(jnp.concatenate([flat[at : at + 128], flat[at + 80 : at + 208]], axis=1))
        taken = jnp.concatenate(taken, axis=0).astype(jnp.bfloat16)
        pltpu.matmul_push_rhs(taken, step // 2 % 2, unit, transpose=True)
        for piece in range(6):
            staged = step // 2 % 2 if piece == 0 else None
            pltpu.matmul_acc_lhs(acc[unit][base + piece], pick[piece * 64 : piece * 64 + 64, :], staged)
        for piece in range(6):
            picked = pltpu.matmul_pop(acc[unit][base + piece]).astype(jnp.bfloat16)
            lanes = slice(piece // 2 * 128, piece // 2 * 128 + 128)
            for j in range(2):
                at = step * 256 + j * 128 + piece % 2 * 64
                patches[at : at + 64, lanes] = picked[:, j * 128 : j * 128 + 128]

    sublane = lax.broadcasted_iota(jnp.int32, (8, 256), 0)
    bias1 = jnp.concatenate([b1[...]] * 2, axis=1)
    for chunk in range(ROWS // 6):
        base = chunk % 2 * 6
        for unit in range(2):
            for half in range(2):
                pltpu.matmul_push_rhs(w1[half * 256 : half * 256 + 256, unit * 256 : unit * 256 + 256], half, unit)
                for r in range(6):
                    at = (chunk * 6 + r) * 64
                    if half == 0:
                        lhs = patches[at : at + 64, 0:256]
                    else:
                        lhs = patches[at : at + 64, 256:384]
                        lhs = jnp.concatenate([lhs, lhs], axis=1)
                    pltpu.matmul_acc_lhs(acc[unit][base + r], lhs, half if r == 0 else None)
        for unit in range(2):
            for r in range(6):
                index = chunk * 6 + r
                row = leaky_relu(pltpu.matmul_pop(acc[unit][base + r]) + bias1)
                before = jnp.where(sublane == 0, 0.0, pltpu.roll(row[56:64], 1, 0))
                after = jnp.where(sublane == 7, 0.0, pltpu.roll(row[0:8], 7, 0))
                wide = jnp.concatenate([before, row, after], axis=0).astype(jnp.bfloat16)
                row = row.astype(jnp.bfloat16)
                for side in range(2):
                    lanes = slice(side * 128, side * 128 + 128)
                    center[unit * 2 + side, index * 64 : index * 64 + 64, :] = row[:, lanes]
                    shift[unit * 2 + side, index * 80 : index * 80 + 80, :] = wide[:, lanes]

    @pl.when(core == 0)
    def _():
        center[:, 0:64, :] = jnp.zeros((4, 64, 128), jnp.bfloat16)
        shift[:, 0:80, :] = jnp.zeros((4, 80, 128), jnp.bfloat16)

    @pl.when(core == 1)
    def _():
        center[:, 33 * 64 : 34 * 64, :] = jnp.zeros((4, 64, 128), jnp.bfloat16)
        shift[:, 33 * 80 : 34 * 80, :] = jnp.zeros((4, 80, 128), jnp.bfloat16)

    @pl.when(pair == 0)
    def _():
        center[0] = jnp.zeros((ROWS * 64, 128), jnp.bfloat16)
        shift[0] = jnp.zeros((ROWS * 80, 128), jnp.bfloat16)

    @pl.when(pair == pairs - 1)
    def _():
        center[3] = jnp.zeros((ROWS * 64, 128), jnp.bfloat16)
        shift[3] = jnp.zeros((ROWS * 80, 128), jnp.bfloat16)

    bias2 = jnp.concatenate([b2[...]] * 2, axis=1)
    nothing = jnp.zeros((128, 128), jnp.bfloat16)

    def block(plane, row, tap):
        if tap == 1:
            return center[plane, row * 64 : row * 64 + 64, :]
        at = row * 80 + (0 if tap == 0 else 16)
        return shift[plane, at : at + 64, :]

    def weight(depth_tap, row_tap, tap):
        if not 0 <= row_tap < 3:
            return nothing
        at = (row_tap * 3 + tap) * 128
        return w2[depth_tap, at : at + 128]

    inner = [(plane, r, c) for plane in (1, 2) for r in range(3) for c in range(3)]
    outer = [(r, c) for r in range(4) for c in range(3)]
    pooled = []
    for m in range(2):
        turn = 0
        for t in range(0, 18, 2):
            rhs = jnp.concatenate(
                [
                    jnp.concatenate([weight(plane, r, c), weight(plane - 1, r, c)], axis=1)
                    for plane, r, c in inner[t : t + 2]
                ],
                axis=0,
            )
            for unit in range(2):
                pltpu.matmul_push_rhs(rhs, turn % 2, unit)
                for i in range(8):
                    row = m * 16 + unit * 8 + i
                    lhs = jnp.concatenate([block(plane, row + r, c) for plane, r, c in inner[t : t + 2]], axis=1)
                    pltpu.matmul_acc_lhs(acc[unit][i], lhs, turn % 2 if i == 0 else None)
            turn += 1
        for plane, depth_tap, base in ((0, 0, 8), (3, 2, 12)):
            for t in range(0, 12, 2):
                rhs = jnp.concatenate(
                    [
                        jnp.concatenate([weight(depth_tap, r, c), weight(depth_tap, r - 1, c)], axis=1)
                        for r, c in outer[t : t + 2]
                    ],
                    axis=0,
                )
                for unit in range(2):
                    pltpu.matmul_push_rhs(rhs, turn % 2, unit)
                    for i in range(4):
                        row = m * 16 + unit * 8 + 2 * i
                        lhs = jnp.concatenate([block(plane, row + r, c) for r, c in outer[t : t + 2]], axis=1)
                        pltpu.matmul_acc_lhs(acc[unit][base + i], lhs, turn % 2 if i == 0 else None)
                turn += 1
        for unit in range(2):
            for i in range(4):
                lower = pltpu.matmul_pop(acc[unit][8 + i])
                upper = pltpu.matmul_pop(acc[unit][12 + i])
                total = None
                for side in range(2):
                    lanes = slice(side * 128, side * 128 + 128)
                    value = pltpu.matmul_pop(acc[unit][2 * i + side])
                    value += jnp.concatenate([lower[:, lanes], upper[:, lanes]], axis=1)
                    value = leaky_relu(value + bias2).astype(jnp.bfloat16).astype(jnp.float32)
                    value = value[:, :128] + value[:, 128:]
                    total = value if total is None else total + value
                total = jnp.concatenate(
                    [total[16 * k : 16 * k + 8] + total[16 * k + 8 : 16 * k + 16] for k in range(4)], axis=0
                )
                pooled.append((total * 0.125).astype(jnp.bfloat16))

    for k in range(2):
        rhs = jnp.concatenate(pooled[k * 8 : k * 8 + 8], axis=0)
        pltpu.matmul_push_rhs(jnp.concatenate([rhs, rhs], axis=1), k % 2, k)
        for piece in range(4):
            pltpu.matmul_acc_lhs(acc[k][piece], order[piece * 64 : piece * 64 + 64, :], k % 2 if piece == 0 else None)
        for h in range(2):
            ordered = [pltpu.matmul_pop(acc[k][2 * h + piece])[:, :128] for piece in range(2)]
            at = k * 256 + h * 128
            out[:, at : at + 128] = jnp.transpose(jnp.concatenate(ordered, axis=0)).astype(jnp.bfloat16)


def convolve(*operands):
    vmem = pl.BlockSpec(memory_space=pltpu.VMEM)
    return pl.pallas_call(
        body,
        out_shape=jax.ShapeDtypeStruct((128, 512), jnp.bfloat16),
        in_specs=[vmem] * len(operands),
        out_specs=vmem,
        scratch_shapes=[
            pltpu.VMEM((LINES // LINE, LINE, 128), jnp.float32),
            pltpu.VMEM((ROWS * 64, 384), jnp.bfloat16),
            pltpu.VMEM((4, ROWS * 64, 128), jnp.bfloat16),
            pltpu.VMEM((4, ROWS * 80, 128), jnp.bfloat16),
        ],
        compiler_params=pltpu.CompilerParams(vmem_limit_bytes=40 << 20),
        cost_estimate=pl.CostEstimate(flops=12_000_000_000, bytes_accessed=4_000_000, transcendentals=0),
        name="convolve",
    )(*operands)


def spread_weights(weight):
    channels = weight.shape[4]
    taps = jnp.transpose(weight, (2, 1, 0, 3, 4)).reshape(3, 3, 12, channels)

    def pad(value, before, after):
        return jnp.pad(value, ((0, 0), (0, 0), (before, after), (0, 0)))

    planes = [
        pad(taps, 0, 28),
        pad(taps[:, :, :4], 8, 28) + pad(taps[:, :, 4:], 16, 16),
        pad(taps, 20, 8),
        pad(taps, 28, 0),
    ]
    spread = jnp.concatenate(planes, axis=3).reshape(3, 120, 4 * channels)
    return jnp.pad(spread, ((0, 1), (0, 8), (0, 0))).reshape(512, 4 * channels)


def shards(volume, conv1_weight, conv1_bias, conv2_weight, conv2_bias):
    peers = lax.axis_size("space") * lax.axis_size("chan")
    upper = lax.axis_index("chan") % 2 == 1
    own = jnp.transpose(volume.reshape(4, 2, SIDE, SIDE), (2, 1, 0, 3)).reshape(SIDE, 8, SIDE)
    mate = lax.ppermute(own, AXES, [(i, i ^ 1) for i in range(peers)])
    low = jnp.where(upper, mate[SIDE - WINDOW :], own[:WINDOW])
    high = jnp.where(upper, own[SIDE - WINDOW :], mate[:WINDOW])
    upward = jnp.concatenate([low[:, 4:], high], axis=1)
    downward = jnp.pad(low, ((0, 0), (0, 4), (0, 0)))
    odd = lax.axis_index("chan") // 2 % 2 == 1
    ends = (0, 1, peers - 2, peers - 1)
    first_swap = lax.ppermute(jnp.where(odd, downward, upward), AXES, [(i, i ^ 2) for i in range(peers)])
    second_swap = lax.ppermute(
        jnp.where(odd, upward, downward),
        AXES,
        [(i, i ^ 1) if i in ends else (i, i + 2 if i // 2 % 2 else i - 2) for i in range(peers)],
    )
    half = convolve(
        first_swap,
        second_swap,
        low,
        high,
        spread_weights(conv1_weight),
        conv1_bias[None],
        conv2_weight.reshape(3, 1152, 128),
        conv2_bias[None],
        jnp.asarray(pick_matrix(), jnp.bfloat16),
        jnp.asarray(order_matrix(), jnp.bfloat16),
    )
    moved = lax.all_to_all(half.reshape(16, 8, 512), "chan", split_axis=0, concat_axis=0, tiled=True)
    return jnp.transpose(moved.reshape(8, 2, 8, 512), (2, 0, 1, 3)).reshape(8, 8, 1024)


def solution(mesh):
    in_specs = (P(None, AXES, None), P(), P(), P(), P())
    out_specs = P("chan", "space", None)
    function = jax.shard_map(shards, mesh=mesh, in_specs=in_specs, out_specs=out_specs, check_vma=False)
    return function
```

time: 50.9 us -> 37.9 us (0.74)
  the two profiles are of different devices: /device:TPU:1 before, /device:TPU:5 now
where the time goes in v3:
time: 37.9 us; the launch traced here: 37.7 us
  blocking collectives  10.1 us (27%)
  starting transfers between devices  8.85 us (23%)
  waiting for transfers between devices  7.54 us (20%)
  Pallas kernels  6.99 us (18%)
  local copies, waits for them, and re-layouts  3.73 us (10%)
    all_to_all x1, blocking collectives, shards(): lax.all_to_all(half.reshape(16, 8, 512), 'chan', split_axis=0, concat_axi...  10.1 us
    ppermute x1, starting transfers between devices, shards(): lax.ppermute(jnp.where(odd, upward, downward), AXES, [(i, i ^ 1) if i in...  8.08 us
    pallas_call x1, Pallas kernels, convolve(): pl.pallas_call(body, out_shape=jax.ShapeDtypeStruct((128, 512), jnp.bfloa...  6.99 us
    ppermute x1, waiting for transfers between devices, shards(): lax.ppermute(jnp.where(odd, upward, downward), AXES, [(i, i ^ 1) if i in...  6.43 us
    unnamed x12, local copies, waits for them, and re-layouts  1.42 us
    reshape x2, local copies, waits for them, and re-layouts, shards(): volume.reshape(4, 2, SIDE, SIDE)  1.36 us
    ppermute x1, waiting for transfers between devices, shards(): lax.ppermute(jnp.where(odd, downward, upward), AXES, [(i, i ^ 2) for i in...  0.89 us
    ppermute x1, starting transfers between devices, shards(): mate = lax.ppermute(own, AXES, [(i, i ^ 1) for i in range(peers)])  0.76 us
  transfers between devices with their start and end apart: 3, of which 3 were waited for; matrix products, arithmetic and copies ran while one was open for 1% of the time, Pallas kernels for 0%

profile of v3, /device:TPU:5, one launch (start us, length us, event | category | flops | bytes accessed | tf_op | source)
XLA Modules:
  0.0 37.7 jit_solution(718699971350848522)
XLA Ops:
  0.0 1.2 %reshape.29 = bf16[4,2,128,128]{3,2,1,0:T(8,128)(2,1)S(1)} reshape(bf16[4,2,16384]{2,1,0:T(2,128)(2,1)} %param.7) | data formatting | bytes 524288 | tf_op jit(solution)/shard_map/reshape | solution.py:251
  1.2 0.2 copy.15
  1.4 0.8 %collective-permute-start = (bf16[128,8,128]{2,1,0:T(8,128)(2,1)S(1)}, bf16[128,8,128]{2,1,0:T(8,128)(2,1)S(1)}, u32[]{:S(2)}, u32[]{:S(2)}) collective-permute-start(bf16[128,8,128]{2,1,0:T(8,128)(2,1)S(1)} %bitcast.23), channel_id=1, source_target_pairs={{0,1},{1,0},{2,3},{3,2},{4,5},{5,4},{6,7},{7,6},{8,9},{9,8},{10,11... | collective-permute-start | bytes 786440 | tf_op jit(solution)/shard_map/ppermute | solution.py:252
  2.1 0.0 copy-start.5
  2.1 0.7 %copy-done.5 = bf16[3,3,3,4,128]{4,3,2,1,0:T(4,128)(2,1)S(1)} copy-done((bf16[3,3,3,4,128]{4,3,2,1,0:T(4,128)(2,1)S(1)}, bf16[3,3,3,4,128]{4,3,2,1,0:T(4,128)(2,1)}, u32[]{:S(2)}) %copy-start.5) | copy-done | bytes 27672
  3.0 0.1 fusion.7
  3.1 0.2 collective-permute-done
  3.3 0.1 slice_select_fusion
  3.4 0.2 pad_select_fusion
  3.6 0.0 copy-start
  3.6 8.1 %collective-permute-start.2 = (bf16[67,12,128]{2,1,0:T(8,128)(2,1)S(1)}, bf16[67,12,128]{2,1,0:T(8,128)(2,1)S(1)}, u32[]{:S(2)}, u32[]{:S(2)}) collective-permute-start(bf16[67,12,128]{2,1,0:T(8,128)(2,1)S(1)} %get-tuple-element.5), channel_id=1, source_target_pairs={{0,1},{1,0},{2,4},{3,5},{4,2},{5,3},{6,8},{7,9},{8,6},{9,7},{10,12... | collective-permute-start | bytes 617480 | tf_op jit(solution)/shard_map/ppermute | solution.py:260
  11.7 0.0 collective-permute-start.1
  11.7 0.1 fusion.5
  11.8 0.0 copy-start.3
  11.8 0.0 copy-start.4
  11.8 6.4 %collective-permute-done.2.second_swap = bf16[67,12,128]{2,1,0:T(8,128)(2,1)S(1)} collective-permute-done((bf16[67,12,128]{2,1,0:T(8,128)(2,1)S(1)}, bf16[67,12,128]{2,1,0:T(8,128)(2,1)S(1)}, u32[]{:S(2)}, u32[]{:S(2)}) %collective-permute-start.2) | collective-permute-done | bytes 205856 | tf_op jit(solution)/shard_map/ppermute | solution.py:260
  18.3 0.9 %collective-permute-done.1.first_swap = bf16[67,12,128]{2,1,0:T(8,128)(2,1)S(1)} collective-permute-done((bf16[67,12,128]{2,1,0:T(8,128)(2,1)S(1)}, bf16[67,12,128]{2,1,0:T(8,128)(2,1)S(1)}, u32[]{:S(2)}, u32[]{:S(2)}) %collective-permute-start.1) | collective-permute-done | bytes 205856 | tf_op jit(solution)/shard_map/ppermute | solution.py:259
  19.2 0.0 copy-start.1
  19.2 0.0 copy-start.2
  19.2 0.0 copy-done
  19.2 0.0 copy-done.3
  19.2 0.0 copy-done.4
  19.2 0.6 %copy-done.1 = f32[128]{0:T(128)S(1)} copy-done((f32[128]{0:T(128)S(1)}, f32[128]{0:T(128)}, u32[]{:S(2)}) %copy-start.1) | copy-done | bytes 536
  19.8 0.0 copy-done.2
  19.8 7.0 %convolve.1 = bf16[128,512]{1,0:T(8,128)(2,1)S(1)} custom-call(bf16[67,12,128]{2,1,0:T(8,128)(2,1)S(1)} %collective-permute-done.1.first_swap, bf16[67,12,128]{2,1,0:T(8,128)(2,1)S(1)} %collective-permute-done.2.second_swap, bf16[67,8,128]{2,1,0:T(8,128)(2,1)S(1)} %get-tuple-element.8.low, bf16[67,8,128]{2,1,0:T(8,128)(2,1)S(1)} %get-tuple-element.7.high, ...), custom_call_target="tpu_custom_call" | custom-call | flops 12000000000 | bytes 4000000 | tf_op jit(solution)/shard_map/convolve/pallas_call | solution.py:214
  26.8 10.1 %all_to_all.5 = bf16[16,8,512]{2,1,0:T(8,128)(2,1)S(1)} all-to-all(bf16[16,8,512]{2,1,0:T(8,128)(2,1)S(1)} %bitcast.18), channel_id=1, replica_groups=mesh['space'=16,'chan'=16] {'chan'}, dimensions={0} | all-to-all | bytes 262144 | tf_op jit(solution)/shard_map/all_to_all | solution.py:277
  36.9 0.7 %copy.12 = bf16[8,2,8,512]{3,0,1,2:T(8,128)(2,1)} copy(bf16[8,2,8,512]{3,2,1,0:T(8,128)(2,1)S(1)} %bitcast.27) | data formatting | bytes 262144 | tf_op jit(solution)/shard_map/reshape | solution.py:278
  (7 shorter events, 0.1 us)
Async XLA Ops:
  1.4 1.9 %collective-permute-start = (bf16[128,8,128]{2,1,0:T(8,128)(2,1)S(1)}, bf16[128,8,128]{2,1,0:T(8,128)(2,1)S(1)}, u32[]{:S(2)}, u32[]{:S(2)}) collective-permute-start(bf16[128,8,128]{2,1,0:T(8,128)(2,1)S(1)} %bitcast.23), channel_id=1, source_target_pairs={{0,1},{1,0},{2,3},{3,2},{4,5},{5,4},{6,7},{7,6},{8,9},{9,8},{10,11... | collective-permute-start | bytes 786440 | tf_op jit(solution)/shard_map/ppermute | solution.py:252
  2.1 0.7 %copy-start.5 = (bf16[3,3,3,4,128]{4,3,2,1,0:T(4,128)(2,1)S(1)}, bf16[3,3,3,4,128]{4,3,2,1,0:T(4,128)(2,1)}, u32[]{:S(2)}) copy-start(bf16[3,3,3,4,128]{4,3,2,1,0:T(4,128)(2,1)} %param.8) | copy-start | bytes 82948
  3.6 15.6 %copy-start = (bf16[3,3,3,128,128]{4,3,2,1,0:T(8,128)(2,1)S(1)}, bf16[3,3,3,128,128]{4,3,2,1,0:T(8,128)(2,1)}, u32[]{:S(2)}) copy-start(bf16[3,3,3,128,128]{4,3,2,1,0:T(8,128)(2,1)} %param.10) | copy-start | bytes 2654212
  3.6 14.7 %collective-permute-start.2 = (bf16[67,12,128]{2,1,0:T(8,128)(2,1)S(1)}, bf16[67,12,128]{2,1,0:T(8,128)(2,1)S(1)}, u32[]{:S(2)}, u32[]{:S(2)}) collective-permute-start(bf16[67,12,128]{2,1,0:T(8,128)(2,1)S(1)} %get-tuple-element.5), channel_id=1, source_target_pairs={{0,1},{1,0},{2,4},{3,5},{4,2},{5,3},{6,8},{7,9},{8,6},{9,7},{10,12... | collective-permute-start | bytes 617480 | tf_op jit(solution)/shard_map/ppermute | solution.py:260
  11.7 7.5 %collective-permute-start.1 = (bf16[67,12,128]{2,1,0:T(8,128)(2,1)S(1)}, bf16[67,12,128]{2,1,0:T(8,128)(2,1)S(1)}, u32[]{:S(2)}, u32[]{:S(2)}) collective-permute-start(bf16[67,12,128]{2,1,0:T(8,128)(2,1)S(1)} %get-tuple-element.6), channel_id=1, source_target_pairs={{0,2},{1,3},{2,0},{3,1},{4,6},{5,7},{6,4},{7,5},{8,10},{9,11},{10,... | collective-permute-start | bytes 617480 | tf_op jit(solution)/shard_map/ppermute | solution.py:259
  11.8 7.4 %copy-start.3 = (bf16[384,256]{1,0:T(8,128)(2,1)S(1)}, bf16[384,256]{1,0:T(8,128)(2,1)}, u32[]{:S(2)}) copy-start(bf16[384,256]{1,0:T(8,128)(2,1)} %constant.40.clone.pick) | copy-start | bytes 589828
  11.8 7.4 %copy-start.4 = (bf16[256,256]{1,0:T(8,128)(2,1)S(1)}, bf16[256,256]{1,0:T(8,128)(2,1)}, u32[]{:S(2)}) copy-start(bf16[256,256]{1,0:T(8,128)(2,1)} %constant.41.clone.order) | copy-start | bytes 393220
  19.2 0.7 %copy-start.1 = (f32[128]{0:T(128)S(1)}, f32[128]{0:T(128)}, u32[]{:S(2)}) copy-start(f32[128]{0:T(128)} %param.9) | copy-start | bytes 1540
  19.2 0.7 %copy-start.2 = (f32[128]{0:T(128)S(1)}, f32[128]{0:T(128)}, u32[]{:S(2)}) copy-start(f32[128]{0:T(128)} %param.11) | copy-start | bytes 1540

commit v4 on v3

--- a/solution.py
+++ b/solution.py
@@ -12,6 +12,7 @@
 ROWS = 36
 LINE = 40
 LINES = 2960
+SPLIT = 2
 
 
 def leaky_relu(value):
@@ -34,19 +35,19 @@
     return (pooled // 32 == place // 32) & (pooled % 32 == 4 * (place % 8) + place % 32 // 8)
 
 
-def body(first_swap, second_swap, low, high, w1, b1, w2, b2, pick, order, out, lines, patches, center, shift):
+def body(first_swap, second_swap, low, high, w1, w2, bias, pick, order, out, lines, patches, center, shift, edges):
     sums = pltpu.ACC
     pl.run_scoped(
         lambda *accumulators: compute(
             (accumulators[:16], accumulators[16:]),
-            *(first_swap, second_swap, low, high, w1, b1, w2, b2, pick, order, out, lines, patches, center, shift),
+            *(first_swap, second_swap, low, high, w1, w2, bias, pick, order, out, lines, patches, center, shift, edges),
         ),
         *[sums(unit)((64, 256), jnp.float32) for unit in range(2) for _ in range(16)],
     )
 
 
 def compute(
-    acc, first_swap, second_swap, low, high, w1, b1, w2, b2, pick, order, out, lines, patches, center, shift
+    acc, first_swap, second_swap, low, high, w1, w2, bias, pick, order, out, lines, patches, center, shift, edges
 ):
     core = lax.axis_index("chan") % 2
     pair = lax.axis_index("space") * (lax.axis_size("chan") // 2) + lax.axis_index("chan") // 2
@@ -57,21 +58,26 @@
     lines[67:74] = jnp.zeros((7, LINE, 128), jnp.float32)
     span = pl.ds(3 - 3 * core, WINDOW)
     one, two = first_swap[...].astype(jnp.float32), second_swap[...].astype(jnp.float32)
-    lines[span, 0:12] = jnp.where(pair == 0, 0.0, jnp.where(odd, one, two))
+    below = jnp.where(pair == 0, 0.0, jnp.where(odd, one, two))
+    above = jnp.where(odd, two[:2], one[:2])
+    for plane in range(3):
+        lines[span, plane * 4 : plane * 4 + 4] = below[plane]
     lines[span, 12:16] = jnp.zeros((WINDOW, 4, 128), jnp.float32)
     lines[span, 16:24] = low[...].astype(jnp.float32)
     lines[span, 24:32] = high[...].astype(jnp.float32)
-    lines[span, 32:40] = jnp.where(odd, two[:, :8], one[:, :8])
+    for plane in range(2):
+        lines[span, 32 + plane * 4 : 36 + plane * 4] = above[plane]
     flat = lines.reshape(LINES, 128)
 
     for step in range(ROWS // 4):
         unit, base = step % 2, step // 2 % 2 * 6
         taken = []
-        for j in range(2):
-            at = step * 320 + j * 160
-            taken.append(jnp.concatenate([flat[at : at + 128], flat[at + 80 : at + 208]], axis=1))
-        taken = jnp.concatenate(taken, axis=0).astype(jnp.bfloat16)
-        pltpu.matmul_push_rhs(taken, step // 2 % 2, unit, transpose=True)
+        for half in range(2):
+            starts = [step * 320 + half * 80, step * 320 + half * 80 + 160]
+            taken.append(
+                jnp.concatenate([jnp.transpose(flat[at : at + 128].astype(jnp.bfloat16)) for at in starts], axis=1)
+            )
+        pltpu.matmul_push_rhs(jnp.concatenate(taken, axis=0), step // 2 % 2, unit)
         for piece in range(6):
             staged = step // 2 % 2 if piece == 0 else None
             pltpu.matmul_acc_lhs(acc[unit][base + piece], pick[piece * 64 : piece * 64 + 64, :], staged)
@@ -83,7 +89,7 @@
                 patches[at : at + 64, lanes] = picked[:, j * 128 : j * 128 + 128]
 
     sublane = lax.broadcasted_iota(jnp.int32, (8, 256), 0)
-    bias1 = jnp.concatenate([b1[...]] * 2, axis=1)
+    bias1 = jnp.concatenate([bias[0:1]] * 2, axis=1)
     for chunk in range(ROWS // 6):
         base = chunk % 2 * 6
         for unit in range(2):
@@ -130,7 +136,7 @@
         center[3] = jnp.zeros((ROWS * 64, 128), jnp.bfloat16)
         shift[3] = jnp.zeros((ROWS * 80, 128), jnp.bfloat16)
 
-    bias2 = jnp.concatenate([b2[...]] * 2, axis=1)
+    bias2 = jnp.concatenate([bias[1:2]] * 2, axis=1)
     nothing = jnp.zeros((128, 128), jnp.bfloat16)
 
     def block(plane, row, tap):
@@ -147,9 +153,30 @@
 
     inner = [(plane, r, c) for plane in (1, 2) for r in range(3) for c in range(3)]
     outer = [(r, c) for r in range(4) for c in range(3)]
-    pooled = []
-    for m in range(2):
-        turn = 0
+    turn = 0
+    for t in range(0, 12, 2):
+        for unit, (plane, depth_tap) in enumerate(((0, 0), (3, 2))):
+            rhs = jnp.concatenate(
+                [
+                    jnp.concatenate([weight(depth_tap, r, c), weight(depth_tap, r - 1, c)], axis=1)
+                    for r, c in outer[t : t + 2]
+                ],
+                axis=0,
+            )
+            pltpu.matmul_push_rhs(rhs, turn % 2, unit)
+            for i in range(16):
+                lhs = jnp.concatenate([block(plane, 2 * i + r, c) for r, c in outer[t : t + 2]], axis=1)
+                pltpu.matmul_acc_lhs(acc[unit][i], lhs, turn % 2 if i == 0 else None)
+        turn += 1
+    for unit in range(2):
+        for i in range(16):
+            value = pltpu.matmul_pop(acc[unit][i])
+            for side in range(2):
+                edges[2 * i + side, :, unit * 128 : unit * 128 + 128] = value[:, side * 128 : side * 128 + 128]
+
+    pooled = {}
+    for m in range(SPLIT):
+        rows = 16 // SPLIT
         for t in range(0, 18, 2):
             rhs = jnp.concatenate(
                 [
@@ -160,46 +187,27 @@
             )
             for unit in range(2):
                 pltpu.matmul_push_rhs(rhs, turn % 2, unit)
-                for i in range(8):
-                    row = m * 16 + unit * 8 + i
+                for i in range(rows):
+                    row = unit * 16 + m * rows + i
                     lhs = jnp.concatenate([block(plane, row + r, c) for plane, r, c in inner[t : t + 2]], axis=1)
-                    pltpu.matmul_acc_lhs(acc[unit][i], lhs, turn % 2 if i == 0 else None)
+                    pltpu.matmul_acc_lhs(acc[unit][m * rows + i], lhs, turn % 2 if i == 0 else None)
             turn += 1
-        for plane, depth_tap, base in ((0, 0, 8), (3, 2, 12)):
-            for t in range(0, 12, 2):
-                rhs = jnp.concatenate(
-                    [
-                        jnp.concatenate([weight(depth_tap, r, c), weight(depth_tap, r - 1, c)], axis=1)
-                        for r, c in outer[t : t + 2]
-                    ],
-                    axis=0,
-                )
-                for unit in range(2):
-                    pltpu.matmul_push_rhs(rhs, turn % 2, unit)
-                    for i in range(4):
-                        row = m * 16 + unit * 8 + 2 * i
-                        lhs = jnp.concatenate([block(plane, row + r, c) for r, c in outer[t : t + 2]], axis=1)
-                        pltpu.matmul_acc_lhs(acc[unit][base + i], lhs, turn % 2 if i == 0 else None)
-                turn += 1
-        for unit in range(2):
-            for i in range(4):
-                lower = pltpu.matmul_pop(acc[unit][8 + i])
-                upper = pltpu.matmul_pop(acc[unit][12 + i])
+        for i in range(rows // 2):
+            for unit in range(2):
                 total = None
                 for side in range(2):
-                    lanes = slice(side * 128, side * 128 + 128)
-                    value = pltpu.matmul_pop(acc[unit][2 * i + side])
-                    value += jnp.concatenate([lower[:, lanes], upper[:, lanes]], axis=1)
+                    piece = m * rows + 2 * i + side
+                    value = pltpu.matmul_pop(acc[unit][piece]) + edges[unit * 16 + piece]
                     value = leaky_relu(value + bias2).astype(jnp.bfloat16).astype(jnp.float32)
                     value = value[:, :128] + value[:, 128:]
                     total = value if total is None else total + value
                 total = jnp.concatenate(
                     [total[16 * k : 16 * k + 8] + total[16 * k + 8 : 16 * k + 16] for k in range(4)], axis=0
                 )
-                pooled.append((total * 0.125).astype(jnp.bfloat16))
+                pooled[unit * 8 + m * (rows // 2) + i] = (total * 0.125).astype(jnp.bfloat16)
 
     for k in range(2):
-        rhs = jnp.concatenate(pooled[k * 8 : k * 8 + 8], axis=0)
+        rhs = jnp.concatenate([pooled[i] for i in range(k * 8, k * 8 + 8)], axis=0)
         pltpu.matmul_push_rhs(jnp.concatenate([rhs, rhs], axis=1), k % 2, k)
         for piece in range(4):
             pltpu.matmul_acc_lhs(acc[k][piece], order[piece * 64 : piece * 64 + 64, :], k % 2 if piece == 0 else None)
@@ -221,6 +229,7 @@
             pltpu.VMEM((ROWS * 64, 384), jnp.bfloat16),
             pltpu.VMEM((4, ROWS * 64, 128), jnp.bfloat16),
             pltpu.VMEM((4, ROWS * 80, 128), jnp.bfloat16),
+            pltpu.VMEM((32, 64, 256), jnp.float32),
         ],
         compiler_params=pltpu.CompilerParams(vmem_limit_bytes=40 << 20),
         cost_estimate=pl.CostEstimate(flops=12_000_000_000, bytes_accessed=4_000_000, transcendentals=0),
@@ -252,8 +261,9 @@
     mate = lax.ppermute(own, AXES, [(i, i ^ 1) for i in range(peers)])
     low = jnp.where(upper, mate[SIDE - WINDOW :], own[:WINDOW])
     high = jnp.where(upper, own[SIDE - WINDOW :], mate[:WINDOW])
-    upward = jnp.concatenate([low[:, 4:], high], axis=1)
-    downward = jnp.pad(low, ((0, 0), (0, 4), (0, 0)))
+    planes = [low[:, :4], low[:, 4:], high[:, :4], high[:, 4:]]
+    upward = jnp.stack(planes[1:])
+    downward = jnp.stack(planes[:2] + [jnp.zeros_like(planes[0])])
     odd = lax.axis_index("chan") // 2 % 2 == 1
     ends = (0, 1, peers - 2, peers - 1)
     first_swap = lax.ppermute(jnp.where(odd, downward, upward), AXES, [(i, i ^ 2) for i in range(peers)])
@@ -268,9 +278,8 @@
         low,
         high,
         spread_weights(conv1_weight),
-        conv1_bias[None],
         conv2_weight.reshape(3, 1152, 128),
-        conv2_bias[None],
+        jnp.stack([conv1_bias, conv2_bias]),
         jnp.asarray(pick_matrix(), jnp.bfloat16),
         jnp.asarray(order_matrix(), jnp.bfloat16),
     )

time: 37.9 us -> 35.9 us (0.947)
  waiting for transfers between devices: 7.54 us -> 5.95 us
  local copies, waits for them, and re-layouts: 3.73 us -> 3.22 us
    ppermute x1, waiting for transfers between devices: 6.43 us -> 4.21 us  [shards(): lax.ppermute(jnp.where(odd, upward, downward), AXES, [(i, i ^ 1) if i in...]
    unnamed x12, local copies, waits for them, and re-layouts: 1.42 us -> 0.77 us
    ppermute x1, waiting for transfers between devices: 0.22 us -> 0.84 us  [shards(): mate = lax.ppermute(own, AXES, [(i, i ^ 1) for i in range(peers)])]
where the time goes in v4:
time: 35.9 us; the launch traced here: 35.7 us
  blocking collectives  10.1 us (28%)
  starting transfers between devices  8.85 us (25%)
  Pallas kernels  6.98 us (19%)
  waiting for transfers between devices  5.95 us (17%)
  local copies, waits for them, and re-layouts  3.22 us (9%)
  other arithmetic  0.39 us (1%)
    all_to_all x1, blocking collectives, shards(): lax.all_to_all(half.reshape(16, 8, 512), 'chan', split_axis=0, concat_axi...  10.1 us
    ppermute x1, starting transfers between devices, shards(): lax.ppermute(jnp.where(odd, upward, downward), AXES, [(i, i ^ 1) if i in...  8.08 us
    pallas_call x1, Pallas kernels, convolve(): pl.pallas_call(body, out_shape=jax.ShapeDtypeStruct((128, 512), jnp.bfloa...  6.98 us
    ppermute x1, waiting for transfers between devices, shards(): lax.ppermute(jnp.where(odd, upward, downward), AXES, [(i, i ^ 1) if i in...  4.21 us
    reshape x2, local copies, waits for them, and re-layouts, shards(): volume.reshape(4, 2, SIDE, SIDE)  1.36 us
    ppermute x1, waiting for transfers between devices, shards(): lax.ppermute(jnp.where(odd, downward, upward), AXES, [(i, i ^ 2) for i in...  0.9 us
    ppermute x1, waiting for transfers between devices, shards(): mate = lax.ppermute(own, AXES, [(i, i ^ 1) for i in range(peers)])  0.84 us
    unnamed x12, local copies, waits for them, and re-layouts  0.77 us
  transfers between devices with their start and end apart: 3, of which 3 were waited for; matrix products, arithmetic and copies ran while one was open for 1% of the time, Pallas kernels for 0%

profile of v4, /device:TPU:5, one launch (start us, length us, event | category | flops | bytes accessed | tf_op | source)
XLA Modules:
  0.0 35.7 jit_solution(8968374846362865720)
XLA Ops:
  0.0 1.2 %reshape.29 = bf16[4,2,128,128]{3,2,1,0:T(8,128)(2,1)S(1)} reshape(bf16[4,2,16384]{2,1,0:T(2,128)(2,1)} %param.7) | data formatting | bytes 524288 | tf_op jit(solution)/shard_map/reshape | solution.py:260
  1.2 0.0 copy-start.3
  1.2 0.2 copy.15
  1.4 0.8 %collective-permute-start = (bf16[128,8,128]{2,1,0:T(8,128)(2,1)S(1)}, bf16[128,8,128]{2,1,0:T(8,128)(2,1)S(1)}, u32[]{:S(2)}, u32[]{:S(2)}) collective-permute-start(bf16[128,8,128]{2,1,0:T(8,128)(2,1)S(1)} %bitcast.30), channel_id=1, source_target_pairs={{0,1},{1,0},{2,3},{3,2},{4,5},{5,4},{6,7},{7,6},{8,9},{9,8},{10,11... | collective-permute-start | bytes 786440 | tf_op jit(solution)/shard_map/ppermute | solution.py:261
  2.1 0.0 copy-done.3
  2.3 0.1 pad.41.clone
  2.4 0.1 fusion.7
  2.5 0.8 %collective-permute-done = bf16[128,8,128]{2,1,0:T(8,128)(2,1)S(1)} collective-permute-done((bf16[128,8,128]{2,1,0:T(8,128)(2,1)S(1)}, bf16[128,8,128]{2,1,0:T(8,128)(2,1)S(1)}, u32[]{:S(2)}, u32[]{:S(2)}) %collective-permute-start) | collective-permute-done | bytes 262176 | tf_op jit(solution)/shard_map/ppermute | solution.py:261
  3.3 0.1 slice_select_fusion.1
  3.4 0.1 slice_bitcast_fusion.1
  3.5 0.0 copy-start
  3.5 0.2 broadcast_select_fusion
  3.7 8.1 %collective-permute-start.2 = (bf16[3,67,4,128]{3,2,1,0:T(4,128)(2,1)S(1)}, bf16[3,67,4,128]{3,2,1,0:T(4,128)(2,1)S(1)}, u32[]{:S(2)}, u32[]{:S(2)}) collective-permute-start(bf16[3,67,4,128]{3,2,1,0:T(4,128)(2,1)S(1)} %get-tuple-element.5), channel_id=1, source_target_pairs={{0,1},{1,0},{2,4},{3,5},{4,2},{5,3},{6,8},{7,9},{8,6},{9,7},{10,12... | collective-permute-start | bytes 617480 | tf_op jit(solution)/shard_map/ppermute | solution.py:270
  11.8 0.0 collective-permute-start.1
  11.8 0.1 fusion.5
  11.9 0.0 copy-start.1
  11.9 0.0 copy-start.2
  12.0 0.0 copy-start.4
  12.0 0.0 copy-start.5
  12.0 0.7 %copy-done.4 = f32[128]{0:T(128)S(1)} copy-done((f32[128]{0:T(128)S(1)}, f32[128]{0:T(128)}, u32[]{:S(2)}) %copy-start.4) | copy-done | bytes 536
  12.7 0.0 copy-done.5
  12.7 4.2 %collective-permute-done.2.second_swap = bf16[3,67,4,128]{3,2,1,0:T(4,128)(2,1)S(1)} collective-permute-done((bf16[3,67,4,128]{3,2,1,0:T(4,128)(2,1)S(1)}, bf16[3,67,4,128]{3,2,1,0:T(4,128)(2,1)S(1)}, u32[]{:S(2)}, u32[]{:S(2)}) %collective-permute-start.2) | collective-permute-done | bytes 205856 | tf_op jit(solution)/shard_map/ppermute | solution.py:270
  16.9 0.9 %collective-permute-done.1.first_swap = bf16[3,67,4,128]{3,2,1,0:T(4,128)(2,1)S(1)} collective-permute-done((bf16[3,67,4,128]{3,2,1,0:T(4,128)(2,1)S(1)}, bf16[3,67,4,128]{3,2,1,0:T(4,128)(2,1)S(1)}, u32[]{:S(2)}, u32[]{:S(2)}) %collective-permute-start.1) | collective-permute-done | bytes 205856 | tf_op jit(solution)/shard_map/ppermute | solution.py:269
  17.8 0.0 copy-done
  17.8 0.0 copy-done.1
  17.8 0.0 copy-done.2
  17.8 7.0 %convolve.1 = bf16[128,512]{1,0:T(8,128)(2,1)S(1)} custom-call(bf16[3,67,4,128]{3,2,1,0:T(4,128)(2,1)S(1)} %collective-permute-done.1.first_swap, bf16[3,67,4,128]{3,2,1,0:T(4,128)(2,1)S(1)} %collective-permute-done.2.second_swap, bf16[67,8,128]{2,1,0:T(8,128)(2,1)S(1)} %get-tuple-element.7.low, bf16[67,8,128]{2,1,0:T(8,128)(2,1)S(1)} %get-tuple-element.8.high, ...), custom_call_target="tpu_custom_call" | custom-call | flops 12000000000 | bytes 4000000 | tf_op jit(solution)/shard_map/convolve/pallas_call | solution.py:222
  24.8 10.1 %all_to_all.5 = bf16[16,8,512]{2,1,0:T(8,128)(2,1)S(1)} all-to-all(bf16[16,8,512]{2,1,0:T(8,128)(2,1)S(1)} %bitcast.27), channel_id=1, replica_groups=mesh['space'=16,'chan'=16] {'chan'}, dimensions={0} | all-to-all | bytes 262144 | tf_op jit(solution)/shard_map/all_to_all | solution.py:286
  34.9 0.7 %copy.12 = bf16[8,2,8,512]{3,0,1,2:T(8,128)(2,1)} copy(bf16[8,2,8,512]{3,2,1,0:T(8,128)(2,1)S(1)} %bitcast.34) | data formatting | bytes 262144 | tf_op jit(solution)/shard_map/reshape | solution.py:287
  (7 shorter events, 0.1 us)
Async XLA Ops:
  1.2 1.0 %copy-start.3 = (bf16[3,3,3,4,128]{4,3,2,1,0:T(4,128)(2,1)S(1)}, bf16[3,3,3,4,128]{4,3,2,1,0:T(4,128)(2,1)}, u32[]{:S(2)}) copy-start(bf16[3,3,3,4,128]{4,3,2,1,0:T(4,128)(2,1)} %param.8) | copy-start | bytes 82948
  1.4 1.9 %collective-permute-start = (bf16[128,8,128]{2,1,0:T(8,128)(2,1)S(1)}, bf16[128,8,128]{2,1,0:T(8,128)(2,1)S(1)}, u32[]{:S(2)}, u32[]{:S(2)}) collective-permute-start(bf16[128,8,128]{2,1,0:T(8,128)(2,1)S(1)} %bitcast.30), channel_id=1, source_target_pairs={{0,1},{1,0},{2,3},{3,2},{4,5},{5,4},{6,7},{7,6},{8,9},{9,8},{10,11... | collective-permute-start | bytes 786440 | tf_op jit(solution)/shard_map/ppermute | solution.py:261
  3.5 14.3 %copy-start = (bf16[3,3,3,128,128]{4,3,2,1,0:T(8,128)(2,1)S(1)}, bf16[3,3,3,128,128]{4,3,2,1,0:T(8,128)(2,1)}, u32[]{:S(2)}) copy-start(bf16[3,3,3,128,128]{4,3,2,1,0:T(8,128)(2,1)} %param.10) | copy-start | bytes 2654212
  3.7 13.2 %collective-permute-start.2 = (bf16[3,67,4,128]{3,2,1,0:T(4,128)(2,1)S(1)}, bf16[3,67,4,128]{3,2,1,0:T(4,128)(2,1)S(1)}, u32[]{:S(2)}, u32[]{:S(2)}) collective-permute-start(bf16[3,67,4,128]{3,2,1,0:T(4,128)(2,1)S(1)} %get-tuple-element.5), channel_id=1, source_target_pairs={{0,1},{1,0},{2,4},{3,5},{4,2},{5,3},{6,8},{7,9},{8,6},{9,7},{10,12... | collective-permute-start | bytes 617480 | tf_op jit(solution)/shard_map/ppermute | solution.py:270
  11.8 6.0 %collective-permute-start.1 = (bf16[3,67,4,128]{3,2,1,0:T(4,128)(2,1)S(1)}, bf16[3,67,4,128]{3,2,1,0:T(4,128)(2,1)S(1)}, u32[]{:S(2)}, u32[]{:S(2)}) collective-permute-start(bf16[3,67,4,128]{3,2,1,0:T(4,128)(2,1)S(1)} %get-tuple-element.6), channel_id=1, source_target_pairs={{0,2},{1,3},{2,0},{3,1},{4,6},{5,7},{6,4},{7,5},{8,10},{9,11},{10,... | collective-permute-start | bytes 617480 | tf_op jit(solution)/shard_map/ppermute | solution.py:269
  11.9 5.9 %copy-start.1 = (bf16[384,256]{1,0:T(8,128)(2,1)S(1)}, bf16[384,256]{1,0:T(8,128)(2,1)}, u32[]{:S(2)}) copy-start(bf16[384,256]{1,0:T(8,128)(2,1)} %constant.41.clone.pick) | copy-start | bytes 589828
  11.9 5.9 %copy-start.2 = (bf16[256,256]{1,0:T(8,128)(2,1)S(1)}, bf16[256,256]{1,0:T(8,128)(2,1)}, u32[]{:S(2)}) copy-start(bf16[256,256]{1,0:T(8,128)(2,1)} %constant.42.clone.order) | copy-start | bytes 393220
  12.0 0.7 %copy-start.4 = (f32[128]{0:T(128)S(1)}, f32[128]{0:T(128)}, u32[]{:S(2)}) copy-start(f32[128]{0:T(128)} %param.11) | copy-start | bytes 1540
  12.0 0.7 %copy-start.5 = (f32[128]{0:T(128)S(1)}, f32[128]{0:T(128)}, u32[]{:S(2)}) copy-start(f32[128]{0:T(128)} %param.9) | copy-start | bytes 1540

commit v5 on v4

--- a/solution.py
+++ b/solution.py
@@ -35,38 +35,35 @@
     return (pooled // 32 == place // 32) & (pooled % 32 == 4 * (place % 8) + place % 32 // 8)
 
 
-def body(first_swap, second_swap, low, high, w1, w2, bias, pick, order, out, lines, patches, center, shift, edges):
+def body(lowest, kept, given, low, high, w1, w2, bias, pick, order, out, lines, patches, center, shift, edges):
     sums = pltpu.ACC
     pl.run_scoped(
         lambda *accumulators: compute(
             (accumulators[:16], accumulators[16:]),
-            *(first_swap, second_swap, low, high, w1, w2, bias, pick, order, out, lines, patches, center, shift, edges),
+            *(lowest, kept, given, low, high, w1, w2, bias, pick, order, out, lines, patches, center, shift, edges),
         ),
         *[sums(unit)((64, 256), jnp.float32) for unit in range(2) for _ in range(16)],
     )
 
 
 def compute(
-    acc, first_swap, second_swap, low, high, w1, w2, bias, pick, order, out, lines, patches, center, shift, edges
+    acc, lowest, kept, given, low, high, w1, w2, bias, pick, order, out, lines, patches, center, shift, edges
 ):
     core = lax.axis_index("chan") % 2
     pair = lax.axis_index("space") * (lax.axis_size("chan") // 2) + lax.axis_index("chan") // 2
     pairs = lax.axis_size("space") * (lax.axis_size("chan") // 2)
-    odd = pair % 2 == 1
+    upper = core == 1
 
     lines[0:3] = jnp.zeros((3, LINE, 128), jnp.float32)
     lines[67:74] = jnp.zeros((7, LINE, 128), jnp.float32)
     span = pl.ds(3 - 3 * core, WINDOW)
-    one, two = first_swap[...].astype(jnp.float32), second_swap[...].astype(jnp.float32)
-    below = jnp.where(pair == 0, 0.0, jnp.where(odd, one, two))
-    above = jnp.where(odd, two[:2], one[:2])
-    for plane in range(3):
-        lines[span, plane * 4 : plane * 4 + 4] = below[plane]
+    mine, other = kept[...].astype(jnp.float32), given[...].astype(jnp.float32)
+    lines[span, 0:8] = jnp.where(pair == 0, 0.0, jnp.where(upper, other, mine))
+    lines[span, 8:12] = jnp.where(pair == 0, 0.0, lowest[...].astype(jnp.float32))
     lines[span, 12:16] = jnp.zeros((WINDOW, 4, 128), jnp.float32)
     lines[span, 16:24] = low[...].astype(jnp.float32)
     lines[span, 24:32] = high[...].astype(jnp.float32)
-    for plane in range(2):
-        lines[span, 32 + plane * 4 : 36 + plane * 4] = above[plane]
+    lines[span, 32:40] = jnp.where(upper, mine, other)
     flat = lines.reshape(LINES, 128)
 
     for step in range(ROWS // 4):
@@ -245,8 +242,8 @@
         return jnp.pad(value, ((0, 0), (0, 0), (before, after), (0, 0)))
 
     planes = [
-        pad(taps, 0, 28),
-        pad(taps[:, :, :4], 8, 28) + pad(taps[:, :, 4:], 16, 16),
+        pad(taps[:, :, :4], 8, 28) + pad(taps[:, :, 4:], 0, 32),
+        pad(taps[:, :, :4], 4, 32) + pad(taps[:, :, 4:], 16, 16),
         pad(taps, 20, 8),
         pad(taps, 28, 0),
     ]
@@ -254,27 +251,29 @@
     return jnp.pad(spread, ((0, 1), (0, 8), (0, 0))).reshape(512, 4 * channels)
 
 
+def by_rows(planes):
+    return jnp.transpose(planes.reshape(4, 2, SIDE, SIDE), (2, 1, 0, 3)).reshape(SIDE, 8, SIDE)
+
+
 def shards(volume, conv1_weight, conv1_bias, conv2_weight, conv2_bias):
     peers = lax.axis_size("space") * lax.axis_size("chan")
     upper = lax.axis_index("chan") % 2 == 1
-    own = jnp.transpose(volume.reshape(4, 2, SIDE, SIDE), (2, 1, 0, 3)).reshape(SIDE, 8, SIDE)
-    mate = lax.ppermute(own, AXES, [(i, i ^ 1) for i in range(peers)])
+    mates = [(i, i ^ 1) for i in range(peers)]
+    bridges = [(i, i) if i in (0, peers - 1) else (i, i + 1 if i % 2 else i - 1) for i in range(peers)]
+    across = lax.ppermute(volume, AXES, bridges)
+    own = by_rows(volume)
+    mate = lax.ppermute(own, AXES, mates)
     low = jnp.where(upper, mate[SIDE - WINDOW :], own[:WINDOW])
     high = jnp.where(upper, own[SIDE - WINDOW :], mate[:WINDOW])
-    planes = [low[:, :4], low[:, 4:], high[:, :4], high[:, 4:]]
-    upward = jnp.stack(planes[1:])
-    downward = jnp.stack(planes[:2] + [jnp.zeros_like(planes[0])])
-    odd = lax.axis_index("chan") // 2 % 2 == 1
-    ends = (0, 1, peers - 2, peers - 1)
-    first_swap = lax.ppermute(jnp.where(odd, downward, upward), AXES, [(i, i ^ 2) for i in range(peers)])
-    second_swap = lax.ppermute(
-        jnp.where(odd, upward, downward),
-        AXES,
-        [(i, i ^ 1) if i in ends else (i, i + 2 if i // 2 % 2 else i - 2) for i in range(peers)],
-    )
+    cut = low[:, 4:]
+    lowest = lax.ppermute(cut, AXES, [(i, i + 2) for i in range(peers - 2)])
+    across = by_rows(across)
+    kept = jnp.where(upper, across[SIDE - WINDOW :], across[:WINDOW])
+    given = lax.ppermute(jnp.where(upper, across[:WINDOW], across[SIDE - WINDOW :]), AXES, mates)
     half = convolve(
-        first_swap,
-        second_swap,
+        lowest,
+        kept,
+        given,
         low,
         high,
         spread_weights(conv1_weight),
@@ -290,5 +289,4 @@
 def solution(mesh):
     in_specs = (P(None, AXES, None), P(), P(), P(), P())
     out_specs = P("chan", "space", None)
-    function = jax.shard_map(shards, mesh=mesh, in_specs=in_specs, out_specs=out_specs, check_vma=False)
-    return function
+    return jax.shard_map(shards, mesh=mesh, in_specs=in_specs, out_specs=out_specs, check_vma=False)

time: 35.9 us -> 42.5 us (1.18)
  starting transfers between devices: 8.85 us -> 14.2 us
  waiting for transfers between devices: 5.95 us -> 7.11 us
  local copies, waits for them, and re-layouts: 3.22 us -> 4.06 us
  blocking collectives: 10.1 us -> 9.56 us
    ppermute x3 -> x4, starting transfers between devices: 8.85 us -> 14.2 us  [the longest x1 6.62 us: shards(): mate = lax.ppermute(own, AXES, mates)]
    ppermute x3 -> x4, waiting for transfers between devices: 5.95 us -> 7.11 us  [the longest x1 7.1 us: shards(): lowest = lax.ppermute(cut, AXES, [(i, i + 2) for i in range(peers - 2)])]
    unnamed x12, local copies, waits for them, and re-layouts: 0.77 us -> 1.32 us
    all_to_all x1, blocking collectives: 10.1 us -> 9.56 us  [shards(): lax.all_to_all(half.reshape(16, 8, 512), 'chan', split_axis=0, concat_axi...]
    reshape x2 -> x4, local copies, waits for them, and re-layouts: 1.36 us -> 1.78 us  [by_rows(): planes.reshape(4, 2, SIDE, SIDE)]
  transfers between devices with their start and end apart: 3 -> 4, of which waited for: 3 -> 1; matrix products, arithmetic and copies ran while one was open for 1% -> 5% of each run, Pallas kernels for 0% -> 0%
where the time goes in v5:
time: 42.5 us; the launch traced here: 42.2 us
  starting transfers between devices  14.2 us (33%)
  blocking collectives  9.56 us (22%)
  waiting for transfers between devices  7.11 us (17%)
  Pallas kernels  6.87 us (16%)
  local copies, waits for them, and re-layouts  4.06 us (10%)
    all_to_all x1, blocking collectives, shards(): lax.all_to_all(half.reshape(16, 8, 512), 'chan', split_axis=0, concat_axi...  9.56 us
    ppermute x1, waiting for transfers between devices, shards(): lowest = lax.ppermute(cut, AXES, [(i, i + 2) for i in range(peers - 2)])  7.1 us
    pallas_call x1, Pallas kernels, convolve(): pl.pallas_call(body, out_shape=jax.ShapeDtypeStruct((128, 512), jnp.bfloa...  6.87 us
    ppermute x1, starting transfers between devices, shards(): mate = lax.ppermute(own, AXES, mates)  6.62 us
    ppermute x1, starting transfers between devices, shards(): across = lax.ppermute(volume, AXES, bridges)  3.75 us
    ppermute x1, starting transfers between devices, shards(): lowest = lax.ppermute(cut, AXES, [(i, i + 2) for i in range(peers - 2)])  1.92 us
    ppermute x1, starting transfers between devices, shards(): lax.ppermute(jnp.where(upper, across[:WINDOW], across[SIDE - WINDOW:]), A...  1.89 us
    reshape x4, local copies, waits for them, and re-layouts, by_rows(): planes.reshape(4, 2, SIDE, SIDE)  1.78 us
  transfers between devices with their start and end apart: 4, of which 1 were waited for; matrix products, arithmetic and copies ran while one was open for 5% of the time, Pallas kernels for 0%

profile of v5, /device:TPU:5, one launch (start us, length us, event | category | flops | bytes accessed | tf_op | source)
XLA Modules:
  0.0 42.2 jit_solution(7113594556397221104)
XLA Ops:
  0.0 3.8 %collective-permute-start.2 = (bf16[4,2,16384]{2,1,0:T(2,128)(2,1)}, bf16[4,2,16384]{2,1,0:T(2,128)(2,1)S(1)}, u32[]{:S(2)}, u32[]{:S(2)}) collective-permute-start(bf16[4,2,16384]{2,1,0:T(2,128)(2,1)} %param.7), channel_id=1, source_target_pairs={{0,0},{1,2},{2,1},{3,4},{4,3},{5,6},{6,5},{7,8},{8,7},{9,10},{10,9... | collective-permute-start | bytes 786440 | tf_op jit(solution)/shard_map/ppermute | solution.py:263
  3.8 1.2 %reshape.39 = bf16[4,2,128,128]{3,2,1,0:T(8,128)(2,1)S(1)} reshape(bf16[4,2,16384]{2,1,0:T(2,128)(2,1)} %param.7) | data formatting | bytes 524288 | tf_op jit(solution)/shard_map/reshape | solution.py:255
  4.9 0.2 copy.19
  5.1 6.6 %collective-permute-start = (bf16[128,8,128]{2,1,0:T(8,128)(2,1)S(1)}, bf16[128,8,128]{2,1,0:T(8,128)(2,1)S(1)}, u32[]{:S(2)}, u32[]{:S(2)}) collective-permute-start(bf16[128,8,128]{2,1,0:T(8,128)(2,1)S(1)} %bitcast.28), channel_id=1, source_target_pairs={{0,1},{1,0},{2,3},{3,2},{4,5},{5,4},{6,7},{7,6},{8,9},{9,8},{10,11... | collective-permute-start | bytes 786440 | tf_op jit(solution)/shard_map/ppermute | solution.py:265
  11.8 0.0 copy-start.3
  11.8 0.1 fusion.5
  11.9 0.6 %copy-done.3 = bf16[3,3,3,4,128]{4,3,2,1,0:T(4,128)(2,1)S(1)} copy-done((bf16[3,3,3,4,128]{4,3,2,1,0:T(4,128)(2,1)S(1)}, bf16[3,3,3,4,128]{4,3,2,1,0:T(4,128)(2,1)}, u32[]{:S(2)}) %copy-start.3) | copy-done | bytes 27672
  12.7 0.0 collective-permute-done.2
  12.7 0.2 reshape.41
  13.0 0.2 copy.18
  13.2 0.0 copy-start
  13.2 0.1 broadcast_select_fusion
  13.3 1.9 %collective-permute-start.3 = (bf16[67,8,128]{2,1,0:T(8,128)(2,1)S(1)}, bf16[67,8,128]{2,1,0:T(8,128)(2,1)S(1)}, u32[]{:S(2)}, u32[]{:S(2)}) collective-permute-start(bf16[67,8,128]{2,1,0:T(8,128)(2,1)S(1)} %bitcast.33), channel_id=1, source_target_pairs={{0,1},{1,0},{2,3},{3,2},{4,5},{5,4},{6,7},{7,6},{8,9},{9,8},{10,11... | collective-permute-start | bytes 411656 | tf_op jit(solution)/shard_map/ppermute | solution.py:272
  15.2 0.0 collective-permute-done
  15.2 0.0 copy-start.1
  15.2 0.1 slice_select_fusion
  15.3 0.0 copy-start.2
  15.3 1.9 %collective-permute-start.1 = (bf16[67,4,128]{2,1,0:T(4,128)(2,1)S(1)}, bf16[67,4,128]{2,1,0:T(4,128)(2,1)S(1)}, u32[]{:S(2)}, u32[]{:S(2)}) collective-permute-start(bf16[67,4,128]{2,1,0:T(4,128)(2,1)S(1)} %slice.52), channel_id=1, source_target_pairs={{0,2},{1,3},{2,4},{3,5},{4,6},{5,7},{6,8},{7,9},{8,10},{9,11},{10,... | collective-permute-start | bytes 205832 | tf_op jit(solution)/shard_map/ppermute | solution.py:269
  17.3 0.0 copy-start.4
  17.3 0.0 copy-start.5
  17.3 0.6 %copy-done.4 = f32[128]{0:T(128)S(1)} copy-done((f32[128]{0:T(128)S(1)}, f32[128]{0:T(128)}, u32[]{:S(2)}) %copy-start.4) | copy-done | bytes 536
  17.9 0.0 copy-done.5
  18.0 7.1 %collective-permute-done.1.lowest = bf16[67,4,128]{2,1,0:T(4,128)(2,1)S(1)} collective-permute-done((bf16[67,4,128]{2,1,0:T(4,128)(2,1)S(1)}, bf16[67,4,128]{2,1,0:T(4,128)(2,1)S(1)}, u32[]{:S(2)}, u32[]{:S(2)}) %collective-permute-start.1) | collective-permute-done | bytes 68640 | tf_op jit(solution)/shard_map/ppermute | solution.py:269
  25.1 0.0 collective-permute-done.3.given
  25.1 0.0 copy-done
  25.1 0.0 copy-done.1
  25.1 0.0 copy-done.2
  25.1 6.9 %convolve.1 = bf16[128,512]{1,0:T(8,128)(2,1)S(1)} custom-call(bf16[67,4,128]{2,1,0:T(4,128)(2,1)S(1)} %collective-permute-done.1.lowest, bf16[67,8,128]{2,1,0:T(8,128)(2,1)S(1)} %bitcast.23, bf16[67,8,128]{2,1,0:T(8,128)(2,1)S(1)} %collective-permute-done.3.given, bf16[67,8,128]{2,1,0:T(8,128)(2,1)S(1)} %get-tuple-element.6.low, ...), custom_call_target="tpu_custom_call" | custom-call | flops 12000000000 | bytes 4000000 | tf_op jit(solution)/shard_map/convolve/pallas_call | solution.py:219
  32.0 9.6 %all_to_all.5 = bf16[16,8,512]{2,1,0:T(8,128)(2,1)S(1)} all-to-all(bf16[16,8,512]{2,1,0:T(8,128)(2,1)S(1)} %bitcast.24), channel_id=1, replica_groups=mesh['space'=16,'chan'=16] {'chan'}, dimensions={0} | all-to-all | bytes 262144 | tf_op jit(solution)/shard_map/all_to_all | solution.py:285
  41.5 0.7 %copy.14 = bf16[8,2,8,512]{3,0,1,2:T(8,128)(2,1)} copy(bf16[8,2,8,512]{3,2,1,0:T(8,128)(2,1)S(1)} %bitcast.32) | data formatting | bytes 262144 | tf_op jit(solution)/shard_map/reshape | solution.py:286
  (9 shorter events, 0.2 us)
Async XLA Ops:
  0.0 12.7 %collective-permute-start.2 = (bf16[4,2,16384]{2,1,0:T(2,128)(2,1)}, bf16[4,2,16384]{2,1,0:T(2,128)(2,1)S(1)}, u32[]{:S(2)}, u32[]{:S(2)}) collective-permute-start(bf16[4,2,16384]{2,1,0:T(2,128)(2,1)} %param.7), channel_id=1, source_target_pairs={{0,0},{1,2},{2,1},{3,4},{4,3},{5,6},{6,5},{7,8},{8,7},{9,10},{10,9... | collective-permute-start | bytes 786440 | tf_op jit(solution)/shard_map/ppermute | solution.py:263
  5.1 10.1 %collective-permute-start = (bf16[128,8,128]{2,1,0:T(8,128)(2,1)S(1)}, bf16[128,8,128]{2,1,0:T(8,128)(2,1)S(1)}, u32[]{:S(2)}, u32[]{:S(2)}) collective-permute-start(bf16[128,8,128]{2,1,0:T(8,128)(2,1)S(1)} %bitcast.28), channel_id=1, source_target_pairs={{0,1},{1,0},{2,3},{3,2},{4,5},{5,4},{6,7},{7,6},{8,9},{9,8},{10,11... | collective-permute-start | bytes 786440 | tf_op jit(solution)/shard_map/ppermute | solution.py:265
  11.8 0.7 %copy-start.3 = (bf16[3,3,3,4,128]{4,3,2,1,0:T(4,128)(2,1)S(1)}, bf16[3,3,3,4,128]{4,3,2,1,0:T(4,128)(2,1)}, u32[]{:S(2)}) copy-start(bf16[3,3,3,4,128]{4,3,2,1,0:T(4,128)(2,1)} %param.8) | copy-start | bytes 82948
  13.2 11.9 %copy-start = (bf16[3,3,3,128,128]{4,3,2,1,0:T(8,128)(2,1)S(1)}, bf16[3,3,3,128,128]{4,3,2,1,0:T(8,128)(2,1)}, u32[]{:S(2)}) copy-start(bf16[3,3,3,128,128]{4,3,2,1,0:T(8,128)(2,1)} %param.10) | copy-start | bytes 2654212
  13.3 11.8 %collective-permute-start.3 = (bf16[67,8,128]{2,1,0:T(8,128)(2,1)S(1)}, bf16[67,8,128]{2,1,0:T(8,128)(2,1)S(1)}, u32[]{:S(2)}, u32[]{:S(2)}) collective-permute-start(bf16[67,8,128]{2,1,0:T(8,128)(2,1)S(1)} %bitcast.33), channel_id=1, source_target_pairs={{0,1},{1,0},{2,3},{3,2},{4,5},{5,4},{6,7},{7,6},{8,9},{9,8},{10,11... | collective-permute-start | bytes 411656 | tf_op jit(solution)/shard_map/ppermute | solution.py:272
  15.2 9.9 %copy-start.1 = (bf16[384,256]{1,0:T(8,128)(2,1)S(1)}, bf16[384,256]{1,0:T(8,128)(2,1)}, u32[]{:S(2)}) copy-start(bf16[384,256]{1,0:T(8,128)(2,1)} %constant.25.clone.pick) | copy-start | bytes 589828
  15.3 9.8 %copy-start.2 = (bf16[256,256]{1,0:T(8,128)(2,1)S(1)}, bf16[256,256]{1,0:T(8,128)(2,1)}, u32[]{:S(2)}) copy-start(bf16[256,256]{1,0:T(8,128)(2,1)} %constant.26.clone.order) | copy-start | bytes 393220
  15.3 9.7 %collective-permute-start.1 = (bf16[67,4,128]{2,1,0:T(4,128)(2,1)S(1)}, bf16[67,4,128]{2,1,0:T(4,128)(2,1)S(1)}, u32[]{:S(2)}, u32[]{:S(2)}) collective-permute-start(bf16[67,4,128]{2,1,0:T(4,128)(2,1)S(1)} %slice.52), channel_id=1, source_target_pairs={{0,2},{1,3},{2,4},{3,5},{4,6},{5,7},{6,8},{7,9},{8,10},{9,11},{10,... | collective-permute-start | bytes 205832 | tf_op jit(solution)/shard_map/ppermute | solution.py:269
  17.3 0.7 %copy-start.4 = (f32[128]{0:T(128)S(1)}, f32[128]{0:T(128)}, u32[]{:S(2)}) copy-start(f32[128]{0:T(128)} %param.11) | copy-start | bytes 1540
  17.3 0.7 %copy-start.5 = (f32[128]{0:T(128)S(1)}, f32[128]{0:T(128)}, u32[]{:S(2)}) copy-start(f32[128]{0:T(128)} %param.9) | copy-start | bytes 1540

commit v6 on v4

--- a/solution.py
+++ b/solution.py
@@ -9,25 +9,15 @@
 SIDE = 128
 AXES = ("space", "chan")
 WINDOW = 67
-ROWS = 36
+ROWS = 34
 LINE = 40
 LINES = 2960
+GROUP = 8
 SPLIT = 2
 
 
 def leaky_relu(value):
     return jnp.maximum(value, 0.2 * value)
-
-
-def column(place):
-    return 8 * (place % 8) + place // 8
-
-
-def pick_matrix():
-    row, source = np.arange(384)[:, None], np.arange(256)[None, :]
-    half, place = row % 128 // 64, row % 64
-    wanted = 2 * column(place) - 1 + row // 128
-    return (source // 128 == half) & (source % 128 == wanted)
 
 
 def order_matrix():
@@ -35,19 +25,19 @@
     return (pooled // 32 == place // 32) & (pooled % 32 == 4 * (place % 8) + place % 32 // 8)
 
 
-def body(first_swap, second_swap, low, high, w1, w2, bias, pick, order, out, lines, patches, center, shift, edges):
+def body(first_swap, second_swap, low, high, w1, w2, bias, order, out, lines, columns, patches, center, shift, edges):
     sums = pltpu.ACC
     pl.run_scoped(
         lambda *accumulators: compute(
             (accumulators[:16], accumulators[16:]),
-            *(first_swap, second_swap, low, high, w1, w2, bias, pick, order, out, lines, patches, center, shift, edges),
+            *(first_swap, second_swap, low, high, w1, w2, bias, order, out, lines, columns, patches, center, shift, edges),
         ),
         *[sums(unit)((64, 256), jnp.float32) for unit in range(2) for _ in range(16)],
     )
 
 
 def compute(
-    acc, first_swap, second_swap, low, high, w1, w2, bias, pick, order, out, lines, patches, center, shift, edges
+    acc, first_swap, second_swap, low, high, w1, w2, bias, order, out, lines, columns, patches, center, shift, edges
 ):
     core = lax.axis_index("chan") % 2
     pair = lax.axis_index("space") * (lax.axis_size("chan") // 2) + lax.axis_index("chan") // 2
@@ -62,59 +52,66 @@
     above = jnp.where(odd, two[:2], one[:2])
     for plane in range(3):
         lines[span, plane * 4 : plane * 4 + 4] = below[plane]
-    lines[span, 12:16] = jnp.zeros((WINDOW, 4, 128), jnp.float32)
+    lines[span, 12:16] = jnp.ones((WINDOW, 4, 128), jnp.float32)
     lines[span, 16:24] = low[...].astype(jnp.float32)
     lines[span, 24:32] = high[...].astype(jnp.float32)
     for plane in range(2):
         lines[span, 32 + plane * 4 : 36 + plane * 4] = above[plane]
     flat = lines.reshape(LINES, 128)
 
-    for step in range(ROWS // 4):
-        unit, base = step % 2, step // 2 % 2 * 6
-        taken = []
+    def gather(i):
+        turned = jnp.transpose(flat[i * 80 : i * 80 + 128].astype(jnp.bfloat16))
+        columns[i * 136 : i * 136 + 8, :] = jnp.zeros((8, 128), jnp.float32)
+        columns[i * 136 + 8 : i * 136 + 136, :] = turned.astype(jnp.float32)
+        every = [columns[pl.ds(i * 136 + 7 + k, 8, stride=16), :] for k in range(17)]
+        for tap in range(3):
+            picked = jnp.concatenate([every[2 * b + tap] for b in range(8)], axis=0)
+            patches[i * 64 : i * 64 + 64, tap * 128 : tap * 128 + 128] = picked.astype(jnp.bfloat16)
+
+    sublane = lax.broadcasted_iota(jnp.int32, (8, 256), 0)
+
+    def load(half):
+        for unit in range(2):
+            pltpu.matmul_push_rhs(w1[half * 256 : half * 256 + 256, unit * 256 : unit * 256 + 256], half, unit)
+
+    def multiply(i, place, half, staged):
+        if half == 0:
+            lhs = patches[i * 64 : i * 64 + 64, 0:256]
+        else:
+            lhs = patches[i * 64 : i * 64 + 64, 256:384]
+            lhs = jnp.concatenate([lhs, lhs], axis=1)
+        for unit in range(2):
+            pltpu.matmul_acc_lhs(acc[unit][place], lhs, staged)
+
+    def finish(index, place):
+        for unit in range(2):
+            row = leaky_relu(pltpu.matmul_pop(acc[unit][place]))
+            before = jnp.where(sublane == 0, 0.0, pltpu.roll(row[56:64], 1, 0))
+            after = jnp.where(sublane == 7, 0.0, pltpu.roll(row[0:8], 7, 0))
+            wide = jnp.concatenate([before, row, after], axis=0).astype(jnp.bfloat16)
+            row = row.astype(jnp.bfloat16)
+            for side in range(2):
+                lanes = slice(side * 128, side * 128 + 128)
+                center[unit * 2 + side, index * 64 : index * 64 + 64, :] = row[:, lanes]
+                shift[unit * 2 + side, index * 80 : index * 80 + 80, :] = wide[:, lanes]
+
+    groups = [range(i, min(i + GROUP, ROWS)) for i in range(0, ROWS, GROUP)]
+
+    def taken(turn):
+        return list(enumerate(groups[turn])) if 0 <= turn < len(groups) else []
+
+    for turn in range(len(groups) + 2):
         for half in range(2):
-            starts = [step * 320 + half * 80, step * 320 + half * 80 + 160]
-            taken.append(
-                jnp.concatenate([jnp.transpose(flat[at : at + 128].astype(jnp.bfloat16)) for at in starts], axis=1)
-            )
-        pltpu.matmul_push_rhs(jnp.concatenate(taken, axis=0), step // 2 % 2, unit)
-        for piece in range(6):
-            staged = step // 2 % 2 if piece == 0 else None
-            pltpu.matmul_acc_lhs(acc[unit][base + piece], pick[piece * 64 : piece * 64 + 64, :], staged)
-        for piece in range(6):
-            picked = pltpu.matmul_pop(acc[unit][base + piece]).astype(jnp.bfloat16)
-            lanes = slice(piece // 2 * 128, piece // 2 * 128 + 128)
-            for j in range(2):
-                at = step * 256 + j * 128 + piece % 2 * 64
-                patches[at : at + 64, lanes] = picked[:, j * 128 : j * 128 + 128]
-
-    sublane = lax.broadcasted_iota(jnp.int32, (8, 256), 0)
-    bias1 = jnp.concatenate([bias[0:1]] * 2, axis=1)
-    for chunk in range(ROWS // 6):
-        base = chunk % 2 * 6
-        for unit in range(2):
-            for half in range(2):
-                pltpu.matmul_push_rhs(w1[half * 256 : half * 256 + 256, unit * 256 : unit * 256 + 256], half, unit)
-                for r in range(6):
-                    at = (chunk * 6 + r) * 64
-                    if half == 0:
-                        lhs = patches[at : at + 64, 0:256]
-                    else:
-                        lhs = patches[at : at + 64, 256:384]
-                        lhs = jnp.concatenate([lhs, lhs], axis=1)
-                    pltpu.matmul_acc_lhs(acc[unit][base + r], lhs, half if r == 0 else None)
-        for unit in range(2):
-            for r in range(6):
-                index = chunk * 6 + r
-                row = leaky_relu(pltpu.matmul_pop(acc[unit][base + r]) + bias1)
-                before = jnp.where(sublane == 0, 0.0, pltpu.roll(row[56:64], 1, 0))
-                after = jnp.where(sublane == 7, 0.0, pltpu.roll(row[0:8], 7, 0))
-                wide = jnp.concatenate([before, row, after], axis=0).astype(jnp.bfloat16)
-                row = row.astype(jnp.bfloat16)
-                for side in range(2):
-                    lanes = slice(side * 128, side * 128 + 128)
-                    center[unit * 2 + side, index * 64 : index * 64 + 64, :] = row[:, lanes]
-                    shift[unit * 2 + side, index * 80 : index * 80 + 80, :] = wide[:, lanes]
+            if taken(turn - 1):
+                load(half)
+            for n in range(GROUP):
+                for place, i in taken(turn - 1)[n : n + 1]:
+                    multiply(i, (turn - 1) % 2 * GROUP + place, half, half if place == 0 else None)
+                if n % 2 == half:
+                    for _, i in taken(turn)[n : n + 1]:
+                        gather(i)
+                    for place, i in taken(turn - 2)[n : n + 1]:
+                        finish(i, turn % 2 * GROUP + place)
 
     @pl.when(core == 0)
     def _():
@@ -226,6 +223,7 @@
         out_specs=vmem,
         scratch_shapes=[
             pltpu.VMEM((LINES // LINE, LINE, 128), jnp.float32),
+            pltpu.VMEM((ROWS * 136, 128), jnp.float32),
             pltpu.VMEM((ROWS * 64, 384), jnp.bfloat16),
             pltpu.VMEM((4, ROWS * 64, 128), jnp.bfloat16),
             pltpu.VMEM((4, ROWS * 80, 128), jnp.bfloat16),
@@ -237,7 +235,7 @@
     )(*operands)
 
 
-def spread_weights(weight):
+def spread_weights(weight, bias):
     channels = weight.shape[4]
     taps = jnp.transpose(weight, (2, 1, 0, 3, 4)).reshape(3, 3, 12, channels)
 
@@ -251,7 +249,14 @@
         pad(taps, 28, 0),
     ]
     spread = jnp.concatenate(planes, axis=3).reshape(3, 120, 4 * channels)
-    return jnp.pad(spread, ((0, 1), (0, 8), (0, 0))).reshape(512, 4 * channels)
+    spread = jnp.pad(spread, ((0, 1), (0, 8), (0, 0))).reshape(512, 4 * channels)
+    parts = []
+    for _ in range(3):
+        parts.append(lax.reduce_precision(bias, 8, 7))
+        bias = bias - parts[-1]
+    parts = jnp.tile(jnp.stack(parts).astype(weight.dtype), (1, 4))
+    start = 128 + LINE + 12
+    return spread + jnp.pad(parts, ((start, 512 - 3 - start), (0, 0)))
 
 
 def shards(volume, conv1_weight, conv1_bias, conv2_weight, conv2_bias):
@@ -277,10 +282,9 @@
         second_swap,
         low,
         high,
-        spread_weights(conv1_weight),
+        spread_weights(conv1_weight, conv1_bias),
         conv2_weight.reshape(3, 1152, 128),
         jnp.stack([conv1_bias, conv2_bias]),
-        jnp.asarray(pick_matrix(), jnp.bfloat16),
         jnp.asarray(order_matrix(), jnp.bfloat16),
     )
     moved = lax.all_to_all(half.reshape(16, 8, 512), "chan", split_axis=0, concat_axis=0, tiled=True)
@@ -290,5 +294,4 @@
 def solution(mesh):
     in_specs = (P(None, AXES, None), P(), P(), P(), P())
     out_specs = P("chan", "space", None)
-    function = jax.shard_map(shards, mesh=mesh, in_specs=in_specs, out_specs=out_specs, check_vma=False)
-    return function
+    return jax.shard_map(shards, mesh=mesh, in_specs=in_specs, out_specs=out_specs, check_vma=False)

time: 35.9 us -> 36.5 us (1.017)
  local copies, waits for them, and re-layouts: 3.22 us -> 3.76 us
    ppermute x1, waiting for transfers between devices: 0.84 us -> 0.01 us  [shards(): mate = lax.ppermute(own, AXES, [(i, i ^ 1) for i in range(peers)])]
    ppermute x1, waiting for transfers between devices: 4.21 us -> 4.96 us  [shards(): lax.ppermute(jnp.where(odd, upward, downward), AXES, [(i, i ^ 1) if i in...]
    unnamed x12, local copies, waits for them, and re-layouts: 0.77 us -> 1.31 us
  transfers between devices with their start and end apart: 3 -> 3, of which waited for: 3 -> 2; matrix products, arithmetic and copies ran while one was open for 1% -> 1% of each run, Pallas kernels for 0% -> 0%
where the time goes in v6:
time: 36.5 us; the launch traced here: 36.3 us
  blocking collectives  10.2 us (28%)
  starting transfers between devices  8.85 us (24%)
  Pallas kernels  6.98 us (19%)
  waiting for transfers between devices  5.87 us (16%)
  local copies, waits for them, and re-layouts  3.76 us (10%)
  other arithmetic  0.49 us (1%)
    all_to_all x1, blocking collectives, shards(): lax.all_to_all(half.reshape(16, 8, 512), 'chan', split_axis=0, concat_axi...  10.2 us
    ppermute x1, starting transfers between devices, shards(): lax.ppermute(jnp.where(odd, upward, downward), AXES, [(i, i ^ 1) if i in...  8.08 us
    pallas_call x1, Pallas kernels, convolve(): pl.pallas_call(body, out_shape=jax.ShapeDtypeStruct((128, 512), jnp.bfloa...  6.98 us
    ppermute x1, waiting for transfers between devices, shards(): lax.ppermute(jnp.where(odd, upward, downward), AXES, [(i, i ^ 1) if i in...  4.96 us
    reshape x2, local copies, waits for them, and re-layouts, shards(): volume.reshape(4, 2, SIDE, SIDE)  1.36 us
    unnamed x12, local copies, waits for them, and re-layouts  1.31 us
    ppermute x1, waiting for transfers between devices, shards(): lax.ppermute(jnp.where(odd, downward, upward), AXES, [(i, i ^ 2) for i in...  0.9 us
    ppermute x1, starting transfers between devices, shards(): mate = lax.ppermute(own, AXES, [(i, i ^ 1) for i in range(peers)])  0.76 us
  transfers between devices with their start and end apart: 3, of which 2 were waited for; matrix products, arithmetic and copies ran while one was open for 1% of the time, Pallas kernels for 0%

profile of v6, /device:TPU:5, one launch (start us, length us, event | category | flops | bytes accessed | tf_op | source)
XLA Modules:
  0.0 36.3 jit_solution(17017509916370447437)
XLA Ops:
  0.0 1.2 %reshape.60 = bf16[4,2,128,128]{3,2,1,0:T(8,128)(2,1)S(1)} reshape(bf16[4,2,16384]{2,1,0:T(2,128)(2,1)} %param.6) | data formatting | bytes 524288 | tf_op jit(solution)/shard_map/reshape | solution.py:265
  1.2 0.0 copy-start.2
  1.2 0.2 copy.17
  1.4 0.8 %collective-permute-start = (bf16[128,8,128]{2,1,0:T(8,128)(2,1)S(1)}, bf16[128,8,128]{2,1,0:T(8,128)(2,1)S(1)}, u32[]{:S(2)}, u32[]{:S(2)}) collective-permute-start(bf16[128,8,128]{2,1,0:T(8,128)(2,1)S(1)} %bitcast.41), channel_id=1, source_target_pairs={{0,1},{1,0},{2,3},{3,2},{4,5},{5,4},{6,7},{7,6},{8,9},{9,8},{10,11... | collective-permute-start | bytes 786440 | tf_op jit(solution)/shard_map/ppermute | solution.py:266
  2.1 0.0 copy-done.2
  2.2 0.0 copy-start.3
  2.2 0.6 %copy-done.3 = f32[128]{0:T(128)S(1)} copy-done((f32[128]{0:T(128)S(1)}, f32[128]{0:T(128)}, u32[]{:S(2)}) %copy-start.3) | copy-done | bytes 536
  2.9 0.1 fusion.5
  3.0 0.0 copy-start.4
  3.0 0.6 %copy-done.4 = f32[128]{0:T(128)S(1)} copy-done((f32[128]{0:T(128)S(1)}, f32[128]{0:T(128)}, u32[]{:S(2)}) %copy-start.4) | copy-done | bytes 536
  3.7 0.1 pad.49.clone
  3.8 0.1 fusion.12
  3.9 0.0 collective-permute-done
  3.9 0.1 slice_select_fusion.1
  4.0 0.1 slice_bitcast_fusion.1
  4.1 0.0 copy-start
  4.1 0.2 broadcast_select_fusion
  4.3 8.1 %collective-permute-start.2 = (bf16[3,67,4,128]{3,2,1,0:T(4,128)(2,1)S(1)}, bf16[3,67,4,128]{3,2,1,0:T(4,128)(2,1)S(1)}, u32[]{:S(2)}, u32[]{:S(2)}) collective-permute-start(bf16[3,67,4,128]{3,2,1,0:T(4,128)(2,1)S(1)} %get-tuple-element.5), channel_id=1, source_target_pairs={{0,1},{1,0},{2,4},{3,5},{4,2},{5,3},{6,8},{7,9},{8,6},{9,7},{10,12... | collective-permute-start | bytes 617480 | tf_op jit(solution)/shard_map/ppermute | solution.py:275
  12.4 0.0 collective-permute-start.1
  12.4 0.0 copy-start.1
  12.4 0.1 bitcast_add_fusion.w1
  12.5 5.0 %collective-permute-done.2.second_swap = bf16[3,67,4,128]{3,2,1,0:T(4,128)(2,1)S(1)} collective-permute-done((bf16[3,67,4,128]{3,2,1,0:T(4,128)(2,1)S(1)}, bf16[3,67,4,128]{3,2,1,0:T(4,128)(2,1)S(1)}, u32[]{:S(2)}, u32[]{:S(2)}) %collective-permute-start.2) | collective-permute-done | bytes 205856 | tf_op jit(solution)/shard_map/ppermute | solution.py:275
  17.5 0.9 %collective-permute-done.1.first_swap = bf16[3,67,4,128]{3,2,1,0:T(4,128)(2,1)S(1)} collective-permute-done((bf16[3,67,4,128]{3,2,1,0:T(4,128)(2,1)S(1)}, bf16[3,67,4,128]{3,2,1,0:T(4,128)(2,1)S(1)}, u32[]{:S(2)}, u32[]{:S(2)}) %collective-permute-start.1) | collective-permute-done | bytes 205856 | tf_op jit(solution)/shard_map/ppermute | solution.py:274
  18.4 0.0 copy-done
  18.4 0.0 copy-done.1
  18.4 7.0 %convolve.1 = bf16[128,512]{1,0:T(8,128)(2,1)S(1)} custom-call(bf16[3,67,4,128]{3,2,1,0:T(4,128)(2,1)S(1)} %collective-permute-done.1.first_swap, bf16[3,67,4,128]{3,2,1,0:T(4,128)(2,1)S(1)} %collective-permute-done.2.second_swap, bf16[67,8,128]{2,1,0:T(8,128)(2,1)S(1)} %get-tuple-element.7.low, bf16[67,8,128]{2,1,0:T(8,128)(2,1)S(1)} %get-tuple-element.8.high, ...), custom_call_target="tpu_custom_call" | custom-call | flops 12000000000 | bytes 4000000 | tf_op jit(solution)/shard_map/convolve/pallas_call | solution.py:219
  25.3 10.2 %all_to_all.5 = bf16[16,8,512]{2,1,0:T(8,128)(2,1)S(1)} all-to-all(bf16[16,8,512]{2,1,0:T(8,128)(2,1)S(1)} %bitcast.38), channel_id=1, replica_groups=mesh['space'=16,'chan'=16] {'chan'}, dimensions={0} | all-to-all | bytes 262144 | tf_op jit(solution)/shard_map/all_to_all | solution.py:290
  35.5 0.7 %copy.11 = bf16[8,2,8,512]{3,0,1,2:T(8,128)(2,1)} copy(bf16[8,2,8,512]{3,2,1,0:T(8,128)(2,1)S(1)} %bitcast.45) | data formatting | bytes 262144 | tf_op jit(solution)/shard_map/reshape | solution.py:291
  (11 shorter events, 0.2 us)
Async XLA Ops:
  1.2 1.0 %copy-start.2 = (bf16[3,3,3,4,128]{4,3,2,1,0:T(4,128)(2,1)S(1)}, bf16[3,3,3,4,128]{4,3,2,1,0:T(4,128)(2,1)}, u32[]{:S(2)}) copy-start(bf16[3,3,3,4,128]{4,3,2,1,0:T(4,128)(2,1)} %param.7) | copy-start | bytes 82948
  1.4 2.5 %collective-permute-start = (bf16[128,8,128]{2,1,0:T(8,128)(2,1)S(1)}, bf16[128,8,128]{2,1,0:T(8,128)(2,1)S(1)}, u32[]{:S(2)}, u32[]{:S(2)}) collective-permute-start(bf16[128,8,128]{2,1,0:T(8,128)(2,1)S(1)} %bitcast.41), channel_id=1, source_target_pairs={{0,1},{1,0},{2,3},{3,2},{4,5},{5,4},{6,7},{7,6},{8,9},{9,8},{10,11... | collective-permute-start | bytes 786440 | tf_op jit(solution)/shard_map/ppermute | solution.py:266
  2.2 0.7 %copy-start.3 = (f32[128]{0:T(128)S(1)}, f32[128]{0:T(128)}, u32[]{:S(2)}) copy-start(f32[128]{0:T(128)} %param.8) | copy-start | bytes 1540
  3.0 0.7 %copy-start.4 = (f32[128]{0:T(128)S(1)}, f32[128]{0:T(128)}, u32[]{:S(2)}) copy-start(f32[128]{0:T(128)} %param.10) | copy-start | bytes 1540
  4.1 14.3 %copy-start = (bf16[3,3,3,128,128]{4,3,2,1,0:T(8,128)(2,1)S(1)}, bf16[3,3,3,128,128]{4,3,2,1,0:T(8,128)(2,1)}, u32[]{:S(2)}) copy-start(bf16[3,3,3,128,128]{4,3,2,1,0:T(8,128)(2,1)} %param.9) | copy-start | bytes 2654212
  4.3 13.1 %collective-permute-start.2 = (bf16[3,67,4,128]{3,2,1,0:T(4,128)(2,1)S(1)}, bf16[3,67,4,128]{3,2,1,0:T(4,128)(2,1)S(1)}, u32[]{:S(2)}, u32[]{:S(2)}) collective-permute-start(bf16[3,67,4,128]{3,2,1,0:T(4,128)(2,1)S(1)} %get-tuple-element.5), channel_id=1, source_target_pairs={{0,1},{1,0},{2,4},{3,5},{4,2},{5,3},{6,8},{7,9},{8,6},{9,7},{10,12... | collective-permute-start | bytes 617480 | tf_op jit(solution)/shard_map/ppermute | solution.py:275
  12.4 5.9 %collective-permute-start.1 = (bf16[3,67,4,128]{3,2,1,0:T(4,128)(2,1)S(1)}, bf16[3,67,4,128]{3,2,1,0:T(4,128)(2,1)S(1)}, u32[]{:S(2)}, u32[]{:S(2)}) collective-permute-start(bf16[3,67,4,128]{3,2,1,0:T(4,128)(2,1)S(1)} %get-tuple-element.6), channel_id=1, source_target_pairs={{0,2},{1,3},{2,0},{3,1},{4,6},{5,7},{6,4},{7,5},{8,10},{9,11},{10,... | collective-permute-start | bytes 617480 | tf_op jit(solution)/shard_map/ppermute | solution.py:274
  12.4 5.9 %copy-start.1 = (bf16[256,256]{1,0:T(8,128)(2,1)S(1)}, bf16[256,256]{1,0:T(8,128)(2,1)}, u32[]{:S(2)}) copy-start(bf16[256,256]{1,0:T(8,128)(2,1)} %constant.39.clone.order) | copy-start | bytes 393220

commit v7 on v6

v7 whole, which is shorter than its diff:
```python
import jax
import jax.numpy as jnp
import numpy as np
from jax import lax
from jax.experimental import pallas as pl
from jax.experimental.pallas import tpu as pltpu
from jax.sharding import PartitionSpec as P

SIDE = 128
AXES = ("space", "chan")
WINDOW = 67
ROWS = 34
LINE = 40
LINES = 2960
GROUP = 8
SPLIT = 2


def leaky_relu(value):
    return jnp.maximum(value, 0.2 * value)


def gathered(columns, start, rows):
    columns[start : start + 8, :] = jnp.zeros((8, 128), jnp.float32)
    columns[start + 8 : start + 136, :] = jnp.transpose(rows.astype(jnp.bfloat16)).astype(jnp.float32)
    every = [columns[pl.ds(start + 7 + k, 8, stride=16), :] for k in range(17)]
    return [jnp.concatenate([every[2 * b + tap] for b in range(8)], axis=0).astype(jnp.bfloat16) for tap in range(3)]


def widened(row):
    sublane = lax.broadcasted_iota(jnp.int32, (8, row.shape[1]), 0)
    before = jnp.where(sublane == 0, 0.0, pltpu.roll(row[56:64], 1, 0))
    after = jnp.where(sublane == 7, 0.0, pltpu.roll(row[0:8], 7, 0))
    return jnp.concatenate([before, row, after], axis=0).astype(jnp.bfloat16)


def accumulators():
    return [pltpu.ACC(unit)((64, 256), jnp.float32) for unit in range(2) for _ in range(16)]


def local_body(low, high, w1, w2, bias, out, lines, columns, patches, center, shift):
    pl.run_scoped(
        lambda *acc: compute_local(
            (acc[:16], acc[16:]), low, high, w1, w2, bias, out, lines, columns, patches, center, shift
        ),
        *accumulators(),
    )


def compute_local(acc, low, high, w1, w2, bias, out, lines, columns, patches, center, shift):
    core = lax.axis_index("chan") % 2
    lines[0:3] = jnp.zeros((3, 16, 128), jnp.float32)
    lines[67:76] = jnp.zeros((9, 16, 128), jnp.float32)
    span = pl.ds(3 - 3 * core, WINDOW)
    lines[span, 0:8] = low[...].astype(jnp.float32)
    lines[span, 8:16] = high[...].astype(jnp.float32)
    flat = lines.reshape(76 * 16, 128)

    for i in range(0, ROWS, 2):
        rows = jnp.concatenate([flat[i * 32 : i * 32 + 64], flat[i * 32 + 32 : i * 32 + 96]], axis=0)
        for tap, picked in enumerate(gathered(columns, i // 2 * 136, rows)):
            patches[i * 32 : i * 32 + 64, tap * 128 : tap * 128 + 128] = picked

    bias1 = jnp.concatenate([bias[0:1]] * 2, axis=1)
    for unit, pieces in enumerate((range(0, 9), range(9, 17))):
        for half in range(2):
            pltpu.matmul_push_rhs(w1[half * 256 : half * 256 + 256, :], half, unit)
            for n, i in enumerate(pieces):
                if half == 0:
                    lhs = patches[i * 64 : i * 64 + 64, 0:256]
                else:
                    lhs = patches[i * 64 : i * 64 + 64, 256:384]
                    lhs = jnp.concatenate([lhs, lhs], axis=1)
                pltpu.matmul_acc_lhs(acc[unit][n], lhs, half if n == 0 else None)
        for n, i in enumerate(pieces):
            row = leaky_relu(pltpu.matmul_pop(acc[unit][n]) + bias1)
            wide = widened(row)
            row = row.astype(jnp.bfloat16)
            for side in range(2):
                lanes = slice(side * 128, side * 128 + 128)
                index = 2 * i + side
                center[index * 64 : index * 64 + 64, :] = row[:, lanes]
                shift[index * 80 : index * 80 + 80, :] = wide[:, lanes]

    @pl.when(core == 0)
    def _():
        center[0:64, :] = jnp.zeros((64, 128), jnp.bfloat16)
        shift[0:80, :] = jnp.zeros((80, 128), jnp.bfloat16)

    @pl.when(core == 1)
    def _():
        center[33 * 64 : 34 * 64, :] = jnp.zeros((64, 128), jnp.bfloat16)
        shift[33 * 80 : 34 * 80, :] = jnp.zeros((80, 128), jnp.bfloat16)

    bias2 = jnp.concatenate([bias[1:2]] * 2, axis=1)
    taps = [(r, c) for r in range(3) for c in range(3)]
    for t in range(0, 9, 2):
        pair_of = (taps[t : t + 2] * 2)[:2]
        rhs = [jnp.concatenate([block_of(w2, 2, r, c), block_of(w2, 1, r, c)], axis=1) for r, c in taps[t : t + 2]]
        if len(rhs) == 1:
            rhs.append(jnp.zeros((128, 256), jnp.bfloat16))
        rhs = jnp.concatenate(rhs, axis=0)
        for unit in range(2):
            pltpu.matmul_push_rhs(rhs, t // 2 % 2, unit)
            for i in range(16):
                row = unit * 16 + i
                lhs = jnp.concatenate([places_of(center, shift, row + r, c) for r, c in pair_of], axis=1)
                pltpu.matmul_acc_lhs(acc[unit][i], lhs, t // 2 % 2 if i == 0 else None)
    for i in range(16):
        for unit in range(2):
            out[unit * 16 + i] = pltpu.matmul_pop(acc[unit][i]) + bias2


def block_of(w2, depth_tap, row_tap, tap):
    if not 0 <= row_tap < 3:
        return jnp.zeros((128, 128), jnp.bfloat16)
    at = (row_tap * 3 + tap) * 128
    return w2[depth_tap, at : at + 128]


def places_of(center, shift, row, tap):
    if tap == 1:
        return center[row * 64 : row * 64 + 64, :]
    at = row * 80 + (0 if tap == 0 else 16)
    return shift[at : at + 64, :]


def order_matrix():
    pooled, place = np.arange(256)[:, None], np.arange(256)[None, :]
    return (pooled // 32 == place // 32) & (pooled % 32 == 4 * (place % 8) + place % 32 // 8)


def body(first_swap, second_swap, low, high, w1, w2, bias, order, partial, out, *scratch):
    pl.run_scoped(
        lambda *acc: compute(
            (acc[:16], acc[16:]),
            *(first_swap, second_swap, low, high, w1, w2, bias, order, partial, out),
            *scratch,
        ),
        *accumulators(),
    )


def compute(
    acc,
    first_swap,
    second_swap,
    low,
    high,
    w1,
    w2,
    bias,
    order,
    partial,
    out,
    lines,
    columns,
    patches,
    center,
    shift,
    edges,
):
    core = lax.axis_index("chan") % 2
    pair = lax.axis_index("space") * (lax.axis_size("chan") // 2) + lax.axis_index("chan") // 2
    pairs = lax.axis_size("space") * (lax.axis_size("chan") // 2)
    odd = pair % 2 == 1

    lines[0:3] = jnp.zeros((3, LINE, 128), jnp.float32)
    lines[67:74] = jnp.zeros((7, LINE, 128), jnp.float32)
    span = pl.ds(3 - 3 * core, WINDOW)
    one, two = first_swap[...].astype(jnp.float32), second_swap[...].astype(jnp.float32)
    below = jnp.where(pair == 0, 0.0, jnp.where(odd, one, two))
    above = jnp.where(odd, two[:2], one[:2])
    for plane in range(3):
        lines[span, plane * 4 : plane * 4 + 4] = below[plane]
    lines[span, 12:16] = jnp.ones((WINDOW, 4, 128), jnp.float32)
    lines[span, 16:24] = low[...].astype(jnp.float32)
    lines[span, 24:32] = high[...].astype(jnp.float32)
    for plane in range(2):
        lines[span, 32 + plane * 4 : 36 + plane * 4] = above[plane]
    flat = lines.reshape(LINES, 128)

    def gather(i):
        for tap, picked in enumerate(gathered(columns, i * 136, flat[i * 80 : i * 80 + 128])):
            patches[i * 64 : i * 64 + 64, tap * 128 : tap * 128 + 128] = picked

    bias1 = jnp.concatenate([bias[0:1]] * 2, axis=1)

    def load(half):
        for unit in range(2):
            pltpu.matmul_push_rhs(w1[half * 256 : half * 256 + 256, unit * 256 : unit * 256 + 256], half, unit)

    def multiply(i, place, half, staged):
        if half == 0:
            lhs = patches[i * 64 : i * 64 + 64, 0:256]
        else:
            lhs = patches[i * 64 : i * 64 + 64, 256:384]
            lhs = jnp.concatenate([lhs, lhs], axis=1)
        for unit in range(2):
            pltpu.matmul_acc_lhs(acc[unit][place], lhs, staged)

    def finish(index, place):
        for unit in range(2):
            row = pltpu.matmul_pop(acc[unit][place])
            if unit == 1:
                row = row[:, :128]
            row = leaky_relu(row + bias1[:, : row.shape[1]])
            wide = widened(row)
            row = row.astype(jnp.bfloat16)
            for side in range(2 - unit):
                lanes = slice(side * 128, side * 128 + 128)
                center[unit * 2 + side, index * 64 : index * 64 + 64, :] = row[:, lanes]
                shift[unit * 2 + side, index * 80 : index * 80 + 80, :] = wide[:, lanes]

    groups = [range(i, min(i + GROUP, ROWS)) for i in range(0, ROWS, GROUP)]

    def taken(turn):
        return list(enumerate(groups[turn])) if 0 <= turn < len(groups) else []

    for turn in range(len(groups) + 2):
        for half in range(2):
            if taken(turn - 1):
                load(half)
            for n in range(GROUP):
                for place, i in taken(turn - 1)[n : n + 1]:
                    multiply(i, (turn - 1) % 2 * GROUP + place, half, half if place == 0 else None)
                if n % 2 == half:
                    for _, i in taken(turn)[n : n + 1]:
                        gather(i)
                    for place, i in taken(turn - 2)[n : n + 1]:
                        finish(i, turn % 2 * GROUP + place)

    @pl.when(core == 0)
    def _():
        center[:, 0:64, :] = jnp.zeros((3, 64, 128), jnp.bfloat16)
        shift[:, 0:80, :] = jnp.zeros((3, 80, 128), jnp.bfloat16)

    @pl.when(core == 1)
    def _():
        center[:, 33 * 64 : 34 * 64, :] = jnp.zeros((3, 64, 128), jnp.bfloat16)
        shift[:, 33 * 80 : 34 * 80, :] = jnp.zeros((3, 80, 128), jnp.bfloat16)

    @pl.when(pair == 0)
    def _():
        center[0] = jnp.zeros((ROWS * 64, 128), jnp.bfloat16)
        shift[0] = jnp.zeros((ROWS * 80, 128), jnp.bfloat16)

    @pl.when(pair == pairs - 1)
    def _():
        center[2] = jnp.zeros((ROWS * 64, 128), jnp.bfloat16)
        shift[2] = jnp.zeros((ROWS * 80, 128), jnp.bfloat16)

    def block(plane, row, tap):
        return places_of(center.at[plane], shift.at[plane], row, tap)

    inner = [(r, c) for r in range(3) for c in range(3)]
    outer = [(r, c) for r in range(4) for c in range(3)]
    turn = 0
    for t in range(0, 12, 2):
        for unit, (plane, depth_tap) in enumerate(((0, 0), (2, 2))):
            rhs = jnp.concatenate(
                [
                    jnp.concatenate([block_of(w2, depth_tap, r, c), block_of(w2, depth_tap, r - 1, c)], axis=1)
                    for r, c in outer[t : t + 2]
                ],
                axis=0,
            )
            pltpu.matmul_push_rhs(rhs, turn % 2, unit)
            for i in range(16):
                lhs = jnp.concatenate([block(plane, 2 * i + r, c) for r, c in outer[t : t + 2]], axis=1)
                pltpu.matmul_acc_lhs(acc[unit][i], lhs, turn % 2 if i == 0 else None)
        turn += 1
    for unit in range(2):
        for i in range(16):
            value = pltpu.matmul_pop(acc[unit][i])
            for side in range(2):
                lanes = slice(unit * 128, unit * 128 + 128)
                edges[2 * i + side, :, lanes] = (
                    value[:, side * 128 : side * 128 + 128] + partial[2 * i + side, :, lanes]
                )

    pooled = {}
    for m in range(SPLIT):
        rows = 16 // SPLIT
        for t in range(0, 9, 2):
            pair_of = (inner[t : t + 2] * 2)[:2]
            rhs = [
                jnp.concatenate([block_of(w2, 1, r, c), block_of(w2, 0, r, c)], axis=1) for r, c in inner[t : t + 2]
            ]
            if len(rhs) == 1:
                rhs.append(jnp.zeros((128, 256), jnp.bfloat16))
            rhs = jnp.concatenate(rhs, axis=0)
            for unit in range(2):
                pltpu.matmul_push_rhs(rhs, turn % 2, unit)
                for i in range(rows):
                    row = unit * 16 + m * rows + i
                    lhs = jnp.concatenate([block(1, row + r, c) for r, c in pair_of], axis=1)
                    pltpu.matmul_acc_lhs(acc[unit][m * rows + i], lhs, turn % 2 if i == 0 else None)
            turn += 1
        for i in range(rows // 2):
            for unit in range(2):
                total = None
                for side in range(2):
                    piece = m * rows + 2 * i + side
                    value = pltpu.matmul_pop(acc[unit][piece]) + edges[unit * 16 + piece]
                    value = leaky_relu(value).astype(jnp.bfloat16).astype(jnp.float32)
                    value = value[:, :128] + value[:, 128:]
                    total = value if total is None else total + value
                total = jnp.concatenate(
                    [total[16 * k : 16 * k + 8] + total[16 * k + 8 : 16 * k + 16] for k in range(4)], axis=0
                )
                pooled[unit * 8 + m * (rows // 2) + i] = (total * 0.125).astype(jnp.bfloat16)

    for k in range(2):
        rhs = jnp.concatenate([pooled[i] for i in range(k * 8, k * 8 + 8)], axis=0)
        pltpu.matmul_push_rhs(jnp.concatenate([rhs, rhs], axis=1), k % 2, k)
        for piece in range(4):
            pltpu.matmul_acc_lhs(acc[k][piece], order[piece * 64 : piece * 64 + 64, :], k % 2 if piece == 0 else None)
        for h in range(2):
            ordered = [pltpu.matmul_pop(acc[k][2 * h + piece])[:, :128] for piece in range(2)]
            at = k * 256 + h * 128
            out[:, at : at + 128] = jnp.transpose(jnp.concatenate(ordered, axis=0)).astype(jnp.bfloat16)


def call(body, out, scratch, flops, *operands):
    vmem = pl.BlockSpec(memory_space=pltpu.VMEM)
    return pl.pallas_call(
        body,
        out_shape=jax.ShapeDtypeStruct(*out),
        in_specs=[vmem] * len(operands),
        out_specs=vmem,
        scratch_shapes=[pltpu.VMEM(*shape) for shape in scratch],
        compiler_params=pltpu.CompilerParams(vmem_limit_bytes=24 << 20),
        cost_estimate=pl.CostEstimate(flops=flops, bytes_accessed=4_000_000, transcendentals=0),
    )(*operands)


def local(*operands):
    scratch = [
        ((76, 16, 128), jnp.float32),
        ((ROWS // 2 * 136, 128), jnp.float32),
        ((ROWS * 32, 384), jnp.bfloat16),
        ((ROWS * 64, 128), jnp.bfloat16),
        ((ROWS * 80, 128), jnp.bfloat16),
    ]
    return call(local_body, ((32, 64, 256), jnp.float32), scratch, 2_000_000_000, *operands)


def convolve(*operands):
    scratch = [
        ((LINES // LINE, LINE, 128), jnp.float32),
        ((ROWS * 136, 128), jnp.float32),
        ((ROWS * 64, 384), jnp.bfloat16),
        ((3, ROWS * 64, 128), jnp.bfloat16),
        ((3, ROWS * 80, 128), jnp.bfloat16),
        ((32, 64, 256), jnp.float32),
    ]
    return call(body, ((128, 512), jnp.bfloat16), scratch, 8_000_000_000, *operands)


def spread_weights(weight):
    channels = weight.shape[4]
    taps = jnp.transpose(weight, (2, 1, 0, 3, 4)).reshape(3, 3, 12, channels)

    def pad(value, before, after):
        return jnp.pad(value, ((0, 0), (0, 0), (before, after), (0, 0)))

    planes = [
        pad(taps, 0, 28),
        pad(taps[:, :, :4], 8, 28) + pad(taps[:, :, 4:], 16, 16),
        pad(taps, 28, 0),
    ]
    spread = jnp.concatenate(planes, axis=3).reshape(3, 120, 3 * channels)
    spread = jnp.pad(spread, ((0, 1), (0, 8), (0, channels))).reshape(512, 4 * channels)
    inner = jnp.pad(pad(taps, 4, 0).reshape(3, 48, channels), ((0, 1), (0, 16), (0, 0)))
    inner = jnp.stack(
        [jnp.pad(inner, ((0, 0), (0, 0), (0, channels))), jnp.pad(inner, ((0, 0), (0, 0), (channels, 0)))], axis=1
    )
    return spread, inner.reshape(512, 2 * channels)


def shards(volume, conv1_weight, conv1_bias, conv2_weight, conv2_bias):
    peers = lax.axis_size("space") * lax.axis_size("chan")
    upper = lax.axis_index("chan") % 2 == 1
    own = jnp.transpose(volume.reshape(4, 2, SIDE, SIDE), (2, 1, 0, 3)).reshape(SIDE, 8, SIDE)
    mate = lax.ppermute(own, AXES, [(i, i ^ 1) for i in range(peers)])
    low = jnp.where(upper, mate[SIDE - WINDOW :], own[:WINDOW])
    high = jnp.where(upper, own[SIDE - WINDOW :], mate[:WINDOW])
    planes = [low[:, :4], low[:, 4:], high[:, :4], high[:, 4:]]
    upward = jnp.stack(planes[1:])
    downward = jnp.stack(planes[:2] + [jnp.zeros_like(planes[0])])
    odd = lax.axis_index("chan") // 2 % 2 == 1
    ends = (0, 1, peers - 2, peers - 1)
    first_swap = lax.ppermute(jnp.where(odd, downward, upward), AXES, [(i, i ^ 2) for i in range(peers)])
    second_swap = lax.ppermute(
        jnp.where(odd, upward, downward),
        AXES,
        [(i, i ^ 1) if i in ends else (i, i + 2 if i // 2 % 2 else i - 2) for i in range(peers)],
    )
    spread, inner = spread_weights(conv1_weight)
    w2 = conv2_weight.reshape(3, 1152, 128)
    bias = jnp.stack([conv1_bias, conv2_bias])
    partial = local(low, high, inner, w2, bias)
    half = convolve(
        *(first_swap, second_swap, low, high, spread, w2, bias),
        jnp.asarray(order_matrix(), jnp.bfloat16),
        partial,
    )
    moved = lax.all_to_all(half.reshape(16, 8, 512), "chan", split_axis=0, concat_axis=0, tiled=True)
    return jnp.transpose(moved.reshape(8, 2, 8, 512), (2, 0, 1, 3)).reshape(8, 8, 1024)


def solution(mesh):
    in_specs = (P(None, AXES, None), P(), P(), P(), P())
    out_specs = P("chan", "space", None)
    return jax.shard_map(shards, mesh=mesh, in_specs=in_specs, out_specs=out_specs, check_vma=False)
```

time: 36.5 us -> 34.9 us (0.956)
  waiting for transfers between devices: 5.87 us -> 3.54 us
  Pallas kernels: 6.98 us -> 8.41 us
  local copies, waits for them, and re-layouts: 3.76 us -> 3.26 us
    ppermute x1, waiting for transfers between devices: 4.96 us -> 2.65 us  [shards(): lax.ppermute(jnp.where(odd, upward, downward), AXES, [(i, i ^ 1) if i in...]
    pallas_call x1 -> x2, Pallas kernels: 6.98 us -> 8.41 us  [call(): pl.pallas_call(body, out_shape=jax.ShapeDtypeStruct(*out), in_specs=[vmem...]
    unnamed x12 -> x8, local copies, waits for them, and re-layouts: 1.31 us -> 0.03 us
    transpose x1, local copies, waits for them, and re-layouts: 0.01 us -> 0.76 us  [spread_weights(): taps = jnp.transpose(weight, (2, 1, 0, 3, 4)).reshape(3, 3, 12, channels)]
  transfers between devices with their start and end apart: 3 -> 3, of which waited for: 2 -> 2; matrix products, arithmetic and copies ran while one was open for 1% -> 3% of each run, Pallas kernels for 0% -> 7%
where the time goes in v7:
time: 34.9 us; the launch traced here: 34.7 us
  blocking collectives  10 us (29%)
  starting transfers between devices  8.85 us (25%)
  Pallas kernels  8.41 us (24%)
  waiting for transfers between devices  3.54 us (10%)
  local copies, waits for them, and re-layouts  3.26 us (9%)
  other arithmetic  0.41 us (1%)
    all_to_all x1, blocking collectives, shards(): lax.all_to_all(half.reshape(16, 8, 512), 'chan', split_axis=0, concat_axi...  10 us
    pallas_call x2, Pallas kernels, call(): pl.pallas_call(body, out_shape=jax.ShapeDtypeStruct(*out), in_specs=[vmem...  8.41 us
    ppermute x1, starting transfers between devices, shards(): lax.ppermute(jnp.where(odd, upward, downward), AXES, [(i, i ^ 1) if i in...  8.08 us
    ppermute x1, waiting for transfers between devices, shards(): lax.ppermute(jnp.where(odd, upward, downward), AXES, [(i, i ^ 1) if i in...  2.65 us
    reshape x2, local copies, waits for them, and re-layouts, shards(): volume.reshape(4, 2, SIDE, SIDE)  1.36 us
    ppermute x1, waiting for transfers between devices, shards(): lax.ppermute(jnp.where(odd, downward, upward), AXES, [(i, i ^ 2) for i in...  0.89 us
    ppermute x1, starting transfers between devices, shards(): mate = lax.ppermute(own, AXES, [(i, i ^ 1) for i in range(peers)])  0.76 us
    transpose x1, local copies, waits for them, and re-layouts, spread_weights(): taps = jnp.transpose(weight, (2, 1, 0, 3, 4)).reshape(3, 3, 12, channels)  0.76 us
  transfers between devices with their start and end apart: 3, of which 2 were waited for; matrix products, arithmetic and copies ran while one was open for 3% of the time, Pallas kernels for 7%

profile of v7, /device:TPU:5, one launch (start us, length us, event | category | flops | bytes accessed | tf_op | source)
XLA Modules:
  0.0 34.7 jit_solution(5179048216227314392)
XLA Ops:
  0.0 1.2 %reshape.35 = bf16[4,2,128,128]{3,2,1,0:T(8,128)(2,1)S(1)} reshape(bf16[4,2,16384]{2,1,0:T(2,128)(2,1)} %param.6) | data formatting | bytes 524288 | tf_op jit(solution)/shard_map/reshape | solution.py:385
  1.2 0.2 copy.16
  1.4 0.8 %collective-permute-start = (bf16[128,8,128]{2,1,0:T(8,128)(2,1)S(1)}, bf16[128,8,128]{2,1,0:T(8,128)(2,1)S(1)}, u32[]{:S(2)}, u32[]{:S(2)}) collective-permute-start(bf16[128,8,128]{2,1,0:T(8,128)(2,1)S(1)} %bitcast.40), channel_id=1, source_target_pairs={{0,1},{1,0},{2,3},{3,2},{4,5},{5,4},{6,7},{7,6},{8,9},{9,8},{10,11... | collective-permute-start | bytes 786440 | tf_op jit(solution)/shard_map/ppermute | solution.py:386
  2.1 0.8 %copy.11 = bf16[3,3,3,4,128]{4,3,2,1,0:T(4,128)(2,1)S(1)} copy(bf16[3,3,3,4,128]{4,3,0,1,2:T(4,128)(2,1)} %bitcast.46) | data formatting | bytes 55296 | tf_op jit(solution)/shard_map/transpose | solution.py:363
  3.0 0.0 copy-start.2
  3.0 0.0 copy-start.3
  3.1 0.0 copy-start
  3.2 0.1 pad.57.clone
  3.3 0.1 fusion.4
  3.4 0.0 collective-permute-done
  3.4 0.1 slice_select_fusion.1
  3.5 0.1 slice_bitcast_fusion.1
  3.6 0.2 broadcast_select_fusion
  3.8 8.1 %collective-permute-start.2 = (bf16[3,67,4,128]{3,2,1,0:T(4,128)(2,1)S(1)}, bf16[3,67,4,128]{3,2,1,0:T(4,128)(2,1)S(1)}, u32[]{:S(2)}, u32[]{:S(2)}) collective-permute-start(bf16[3,67,4,128]{3,2,1,0:T(4,128)(2,1)S(1)} %get-tuple-element.5), channel_id=1, source_target_pairs={{0,1},{1,0},{2,4},{3,5},{4,2},{5,3},{6,8},{7,9},{8,6},{9,7},{10,12... | collective-permute-start | bytes 617480 | tf_op jit(solution)/shard_map/ppermute | solution.py:395
  11.9 0.0 collective-permute-start.1
  11.9 0.0 copy-done.2
  11.9 0.0 copy-done.3
  12.0 0.0 copy-done
  12.0 0.0 copy-start.1
  12.0 2.5 %shard_map.64.partial = f32[32,64,256]{2,1,0:T(8,128)S(1)} custom-call(bf16[67,8,128]{2,1,0:T(8,128)(2,1)S(1)} %get-tuple-element.7.low, bf16[67,8,128]{2,1,0:T(8,128)(2,1)S(1)} %get-tuple-element.8.high, bf16[512,256]{1,0:T(8,128)(2,1)S(1)} %bitcast.35, bf16[3,1152,128]{2,1,0:T(8,128)(2,1)S(1)} %bitcast.37, f32[2,128]{1,0:T(2,128)S(1)} %pad_maximum_fusion.2.bias), custom_call_target="tpu_custom_call" | custom-call | flops 2000000000 | bytes 4000000 | tf_op jit(solution)/shard_map/pallas_call | solution.py:327
  14.5 2.6 %collective-permute-done.2.second_swap = bf16[3,67,4,128]{3,2,1,0:T(4,128)(2,1)S(1)} collective-permute-done((bf16[3,67,4,128]{3,2,1,0:T(4,128)(2,1)S(1)}, bf16[3,67,4,128]{3,2,1,0:T(4,128)(2,1)S(1)}, u32[]{:S(2)}, u32[]{:S(2)}) %collective-permute-start.2) | collective-permute-done | bytes 205856 | tf_op jit(solution)/shard_map/ppermute | solution.py:395
  17.1 0.9 %collective-permute-done.1.first_swap = bf16[3,67,4,128]{3,2,1,0:T(4,128)(2,1)S(1)} collective-permute-done((bf16[3,67,4,128]{3,2,1,0:T(4,128)(2,1)S(1)}, bf16[3,67,4,128]{3,2,1,0:T(4,128)(2,1)S(1)}, u32[]{:S(2)}, u32[]{:S(2)}) %collective-permute-start.1) | collective-permute-done | bytes 205856 | tf_op jit(solution)/shard_map/ppermute | solution.py:394
  18.0 0.0 copy-done.1
  18.0 6.0 %shard_map.65 = bf16[128,512]{1,0:T(8,128)(2,1)S(1)} custom-call(bf16[3,67,4,128]{3,2,1,0:T(4,128)(2,1)S(1)} %collective-permute-done.1.first_swap, bf16[3,67,4,128]{3,2,1,0:T(4,128)(2,1)S(1)} %collective-permute-done.2.second_swap, bf16[67,8,128]{2,1,0:T(8,128)(2,1)S(1)} %get-tuple-element.7.low, bf16[67,8,128]{2,1,0:T(8,128)(2,1)S(1)} %get-tuple-element.8.high, ...), custom_call_target="tpu_custom_call" | custom-call | flops 8000000000 | bytes 4000000 | tf_op jit(solution)/shard_map/pallas_call | solution.py:327
  24.0 10.0 %all_to_all.5 = bf16[16,8,512]{2,1,0:T(8,128)(2,1)S(1)} all-to-all(bf16[16,8,512]{2,1,0:T(8,128)(2,1)S(1)} %bitcast.36), channel_id=1, replica_groups=mesh['space'=16,'chan'=16] {'chan'}, dimensions={0} | all-to-all | bytes 262144 | tf_op jit(solution)/shard_map/all_to_all | solution.py:409
  34.0 0.7 %copy.13 = bf16[8,2,8,512]{3,0,1,2:T(8,128)(2,1)} copy(bf16[8,2,8,512]{3,2,1,0:T(8,128)(2,1)S(1)} %bitcast.44) | data formatting | bytes 262144 | tf_op jit(solution)/shard_map/reshape | solution.py:410
  (11 shorter events, 0.2 us)
Async XLA Ops:
  1.4 2.0 %collective-permute-start = (bf16[128,8,128]{2,1,0:T(8,128)(2,1)S(1)}, bf16[128,8,128]{2,1,0:T(8,128)(2,1)S(1)}, u32[]{:S(2)}, u32[]{:S(2)}) collective-permute-start(bf16[128,8,128]{2,1,0:T(8,128)(2,1)S(1)} %bitcast.40), channel_id=1, source_target_pairs={{0,1},{1,0},{2,3},{3,2},{4,5},{5,4},{6,7},{7,6},{8,9},{9,8},{10,11... | collective-permute-start | bytes 786440 | tf_op jit(solution)/shard_map/ppermute | solution.py:386
  3.0 8.9 %copy-start.2 = (f32[128]{0:T(128)S(1)}, f32[128]{0:T(128)}, u32[]{:S(2)}) copy-start(f32[128]{0:T(128)} %param.10) | copy-start | bytes 1540
  3.0 8.9 %copy-start.3 = (f32[128]{0:T(128)S(1)}, f32[128]{0:T(128)}, u32[]{:S(2)}) copy-start(f32[128]{0:T(128)} %param.8) | copy-start | bytes 1540
  3.1 8.9 %copy-start = (bf16[3,3,3,128,128]{4,3,2,1,0:T(8,128)(2,1)S(1)}, bf16[3,3,3,128,128]{4,3,2,1,0:T(8,128)(2,1)}, u32[]{:S(2)}) copy-start(bf16[3,3,3,128,128]{4,3,2,1,0:T(8,128)(2,1)} %param.9) | copy-start | bytes 2654212
  3.8 13.3 %collective-permute-start.2 = (bf16[3,67,4,128]{3,2,1,0:T(4,128)(2,1)S(1)}, bf16[3,67,4,128]{3,2,1,0:T(4,128)(2,1)S(1)}, u32[]{:S(2)}, u32[]{:S(2)}) collective-permute-start(bf16[3,67,4,128]{3,2,1,0:T(4,128)(2,1)S(1)} %get-tuple-element.5), channel_id=1, source_target_pairs={{0,1},{1,0},{2,4},{3,5},{4,2},{5,3},{6,8},{7,9},{8,6},{9,7},{10,12... | collective-permute-start | bytes 617480 | tf_op jit(solution)/shard_map/ppermute | solution.py:395
  11.9 6.1 %collective-permute-start.1 = (bf16[3,67,4,128]{3,2,1,0:T(4,128)(2,1)S(1)}, bf16[3,67,4,128]{3,2,1,0:T(4,128)(2,1)S(1)}, u32[]{:S(2)}, u32[]{:S(2)}) collective-permute-start(bf16[3,67,4,128]{3,2,1,0:T(4,128)(2,1)S(1)} %get-tuple-element.6), channel_id=1, source_target_pairs={{0,2},{1,3},{2,0},{3,1},{4,6},{5,7},{6,4},{7,5},{8,10},{9,11},{10,... | collective-permute-start | bytes 617480 | tf_op jit(solution)/shard_map/ppermute | solution.py:394
  12.0 6.0 %copy-start.1 = (bf16[256,256]{1,0:T(8,128)(2,1)S(1)}, bf16[256,256]{1,0:T(8,128)(2,1)}, u32[]{:S(2)}) copy-start(bf16[256,256]{1,0:T(8,128)(2,1)} %constant.39.clone.order) | copy-start | bytes 393220

commit v8 on v7

v8 whole, which is shorter than its diff:
```python
import jax
import jax.numpy as jnp
import numpy as np
from jax import lax
from jax.experimental import pallas as pl
from jax.experimental.pallas import tpu as pltpu
from jax.sharding import PartitionSpec as P

SIDE = 128
AXES = ("space", "chan")
WINDOW = 68
ROWS = 34
LINE = 20
GROUP = 6
SPLIT = 2


def leaky_relu(value):
    return jnp.maximum(value, 0.2 * value)


def column(place):
    return 8 * (place % 8) + place // 8


def gathered(columns, start, rows):
    columns[start : start + 8, :] = jnp.zeros((8, 128), jnp.float32)
    columns[start + 8 : start + 136, :] = jnp.transpose(rows.astype(jnp.bfloat16)).astype(jnp.float32)
    every = [columns[pl.ds(start + 7 + k, 8, stride=16), :] for k in range(17)]
    return [jnp.concatenate([every[2 * b + tap] for b in range(8)], axis=0).astype(jnp.bfloat16) for tap in range(3)]


def widened(row):
    sublane = lax.broadcasted_iota(jnp.int32, (8, row.shape[1]), 0)
    before = jnp.where(sublane == 0, 0.0, pltpu.roll(row[56:64], 1, 0))
    after = jnp.where(sublane == 7, 0.0, pltpu.roll(row[0:8], 7, 0))
    return jnp.concatenate([before, row, after], axis=0).astype(jnp.bfloat16)


def accumulators():
    return [pltpu.ACC(unit)((64, 256), jnp.float32) for unit in range(2) for _ in range(16)]


def local_body(low, high, w1, w2, bias, out, patches, lines, columns, center, shift):
    pl.run_scoped(
        lambda *acc: compute_local(
            (acc[:16], acc[16:]), low, high, w1, w2, bias, out, patches, lines, columns, center, shift
        ),
        *accumulators(),
    )


def compute_local(acc, low, high, w1, w2, bias, out, patches, lines, columns, center, shift):
    core = lax.axis_index("chan") % 2
    lines[0:4] = jnp.zeros((4, 16, 128), jnp.float32)
    lines[68:76] = jnp.zeros((8, 16, 128), jnp.float32)
    span = pl.ds(4 - 4 * core, WINDOW)
    lines[span, 0:8] = low[...].astype(jnp.float32)
    lines[span, 8:16] = high[...].astype(jnp.float32)
    flat = lines.reshape(76 * 16, 128)

    for i in range(0, ROWS, 2):
        rows = jnp.concatenate([flat[i * 32 + 16 : i * 32 + 80], flat[i * 32 + 48 : i * 32 + 112]], axis=0)
        for tap, picked in enumerate(gathered(columns, i // 2 * 136, rows)):
            patches[i * 32 : i * 32 + 64, tap * 128 : tap * 128 + 128] = picked

    bias1 = jnp.concatenate([bias[0:1]] * 2, axis=1)
    for unit, pieces in enumerate((range(0, 9), range(9, 17))):
        for half in range(2):
            pltpu.matmul_push_rhs(w1[half * 256 : half * 256 + 256, :], half, unit)
            for n, i in enumerate(pieces):
                if half == 0:
                    lhs = patches[i * 64 : i * 64 + 64, 0:256]
                else:
                    lhs = patches[i * 64 : i * 64 + 64, 256:384]
                    lhs = jnp.concatenate([lhs, lhs], axis=1)
                pltpu.matmul_acc_lhs(acc[unit][n], lhs, half if n == 0 else None)
        for n, i in enumerate(pieces):
            row = leaky_relu(pltpu.matmul_pop(acc[unit][n]) + bias1)
            wide = widened(row)
            row = row.astype(jnp.bfloat16)
            for side in range(2):
                lanes = slice(side * 128, side * 128 + 128)
                index = 2 * i + side
                center[index * 64 : index * 64 + 64, :] = row[:, lanes]
                shift[index * 80 : index * 80 + 80, :] = wide[:, lanes]

    @pl.when(core == 0)
    def _():
        center[0:64, :] = jnp.zeros((64, 128), jnp.bfloat16)
        shift[0:80, :] = jnp.zeros((80, 128), jnp.bfloat16)

    @pl.when(core == 1)
    def _():
        center[33 * 64 : 34 * 64, :] = jnp.zeros((64, 128), jnp.bfloat16)
        shift[33 * 80 : 34 * 80, :] = jnp.zeros((80, 128), jnp.bfloat16)

    bias2 = jnp.concatenate([bias[1:2]] * 2, axis=1)
    taps = [(r, c) for r in range(3) for c in range(3)]
    for t in range(0, 9, 2):
        pair_of = (taps[t : t + 2] * 2)[:2]
        rhs = [jnp.concatenate([block_of(w2, 2, r, c), block_of(w2, 1, r, c)], axis=1) for r, c in taps[t : t + 2]]
        if len(rhs) == 1:
            rhs.append(jnp.zeros((128, 256), jnp.bfloat16))
        rhs = jnp.concatenate(rhs, axis=0)
        for unit in range(2):
            pltpu.matmul_push_rhs(rhs, t // 2 % 2, unit)
            for i in range(16):
                row = unit * 16 + i
                lhs = jnp.concatenate([places_of(center, shift, row + r, c) for r, c in pair_of], axis=1)
                pltpu.matmul_acc_lhs(acc[unit][i], lhs, t // 2 % 2 if i == 0 else None)
    for i in range(16):
        for unit in range(2):
            out[unit * 16 + i] = pltpu.matmul_pop(acc[unit][i]) + bias2


def block_of(w2, depth_tap, row_tap, tap):
    if not 0 <= row_tap < 3:
        return jnp.zeros((128, 128), jnp.bfloat16)
    at = (row_tap * 3 + tap) * 128
    return w2[depth_tap, at : at + 128]


def places_of(center, shift, row, tap):
    if tap == 1:
        return center[row * 64 : row * 64 + 64, :]
    at = row * 80 + (0 if tap == 0 else 16)
    return shift[at : at + 64, :]


def pool_matrix():
    pooled, cell = np.arange(64)[:, None], np.arange(256)[None, :]
    return pooled == cell // 128 * 32 + column(cell % 64) // 2


def body(first_swap, second_swap, w1, w2, bias, pool, partial, known, out, *scratch):
    pl.run_scoped(
        lambda *acc: compute(
            (acc[:16], acc[16:]),
            *(first_swap, second_swap, w1, w2, bias, pool, partial, known, out),
            *scratch,
        ),
        *accumulators(),
    )


def compute(
    acc,
    first_swap,
    second_swap,
    w1,
    w2,
    bias,
    pool,
    partial,
    known,
    out,
    lines,
    columns,
    patches,
    center,
    shift,
    edges,
    cells,
):
    core = lax.axis_index("chan") % 2
    pair = lax.axis_index("space") * (lax.axis_size("chan") // 2) + lax.axis_index("chan") // 2
    pairs = lax.axis_size("space") * (lax.axis_size("chan") // 2)
    odd = pair % 2 == 1

    for g in range(35):
        pieces = []
        for t in (2 * g, 2 * g + 1):
            at = t - 3 + 4 * core
            inside = (at >= 0) & (at < WINDOW)
            at = jnp.clip(at, 0, WINDOW - 1)
            for plane in range(5):
                if plane < 3:
                    keep = inside & (pair != 0)
                    x, y = first_swap[plane, at], second_swap[plane, at]
                else:
                    keep = inside
                    x, y = second_swap[plane - 3, at], first_swap[plane - 3, at]
                value = jnp.where(odd, x.astype(jnp.float32), y.astype(jnp.float32))
                pieces.append(jnp.where(keep, value, 0.0))
        lines[g * 40 : g * 40 + 40, :] = jnp.concatenate(pieces, axis=0)

    for i in range(0, ROWS, 2):
        rows = jnp.concatenate([lines[i * 40 : i * 40 + 64, :], lines[i * 40 + 40 : i * 40 + 104, :]], axis=0)
        for tap, picked in enumerate(gathered(columns, i // 2 * 136, rows)):
            patches[i * 32 : i * 32 + 64, tap * 128 : tap * 128 + 128] = picked

    @pl.when(core == 2)
    def _():
        columns[0:8, :] = jnp.zeros((8, 128), jnp.float32)

    def both(i, tile):
        at = slice(i * 64, i * 64 + 64)
        if tile == 0:
            return known[at, 0:256]
        if tile == 1:
            return jnp.concatenate([known[at, 256:384], patches[at, 0:128]], axis=1)
        return patches[at, 128:384]

    def arrived(i, tile):
        at = slice(i * 64, i * 64 + 64)
        if tile == 0:
            return patches[at, 0:256]
        return jnp.concatenate([patches[at, 256:384]] * 2, axis=1)

    bias1 = jnp.concatenate([bias[0:1]] * 2, axis=1)
    work = []
    for unit in range(2):
        jobs = [(1 + unit, 512 + 768 * unit, 3, both, range(i, min(i + GROUP, 17))) for i in range(0, 17, GROUP)]
        jobs += [(0, 0, 2, arrived, part) for part in ((range(0, 5), range(5, 9)), (range(9, 13), range(13, 17)))[unit]]
        work.append(jobs)
    for turn in range(len(work[0]) + 1):
        base = turn % 2 * 8
        if turn < len(work[0]):
            for unit in range(2):
                _, start, tiles, lhs_of, pairs_of_rows = work[unit][turn]
                for tile in range(tiles):
                    pltpu.matmul_push_rhs(w1[start + tile * 256 : start + tile * 256 + 256, :], tile % 2, unit)
                    for n, i in enumerate(pairs_of_rows):
                        pltpu.matmul_acc_lhs(acc[unit][base + n], lhs_of(i, tile), tile % 2 if n == 0 else None)
        if turn:
            for unit in range(2):
                plane, _, _, _, pairs_of_rows = work[unit][turn - 1]
                for n, i in enumerate(pairs_of_rows):
                    row = leaky_relu(pltpu.matmul_pop(acc[unit][8 - base + n]) + bias1)
                    wide = widened(row)
                    row = row.astype(jnp.bfloat16)
                    for side in range(2):
                        lanes = slice(side * 128, side * 128 + 128)
                        index = 2 * i + side
                        center[plane, index * 64 : index * 64 + 64, :] = row[:, lanes]
                        shift[plane, index * 80 : index * 80 + 80, :] = wide[:, lanes]

    @pl.when(core == 0)
    def _():
        center[:, 0:64, :] = jnp.zeros((3, 64, 128), jnp.bfloat16)
        shift[:, 0:80, :] = jnp.zeros((3, 80, 128), jnp.bfloat16)

    @pl.when(core == 1)
    def _():
        center[:, 33 * 64 : 34 * 64, :] = jnp.zeros((3, 64, 128), jnp.bfloat16)
        shift[:, 33 * 80 : 34 * 80, :] = jnp.zeros((3, 80, 128), jnp.bfloat16)

    def block(plane, row, tap):
        return places_of(center.at[plane], shift.at[plane], row, tap)

    inner = [(r, c) for r in range(3) for c in range(3)]
    outer = [(r, c) for r in range(4) for c in range(3)]
    turn = 0
    for t in range(0, 12, 2):
        for unit, (plane, depth_tap) in enumerate(((0, 0), (2, 2))):
            rhs = jnp.concatenate(
                [
                    jnp.concatenate([block_of(w2, depth_tap, r, c), block_of(w2, depth_tap, r - 1, c)], axis=1)
                    for r, c in outer[t : t + 2]
                ],
                axis=0,
            )
            pltpu.matmul_push_rhs(rhs, turn % 2, unit)
            for i in range(16):
                lhs = jnp.concatenate([block(plane, 2 * i + r, c) for r, c in outer[t : t + 2]], axis=1)
                pltpu.matmul_acc_lhs(acc[unit][i], lhs, turn % 2 if i == 0 else None)
        turn += 1
    for unit in range(2):
        for i in range(16):
            value = pltpu.matmul_pop(acc[unit][i])
            value = jnp.where(pair == (pairs - 1 if unit else 0), 0.0, value)
            for side in range(2):
                lanes = slice(unit * 128, unit * 128 + 128)
                edges[2 * i + side, :, lanes] = (
                    value[:, side * 128 : side * 128 + 128] + partial[2 * i + side, :, lanes]
                )

    def active(rows):
        for i in rows:
            for unit in range(2):
                value = leaky_relu(pltpu.matmul_pop(acc[unit][i]) + edges[unit * 16 + i])
                at = (unit * 16 + i) * 64
                cells[at : at + 64, :] = value.astype(jnp.bfloat16)

    def pooled(quarters):
        for k in quarters:
            for unit in range(2):
                at = (unit * 4 + k) * 256
                pltpu.matmul_push_rhs(cells[at : at + 256, :], k % 2, unit)
                pltpu.matmul_acc_lhs(acc[unit][k], pool[...], k % 2)
        for k in quarters[::2]:
            for unit in range(2):
                sums = jnp.concatenate([pltpu.matmul_pop(acc[unit][k + n]) for n in range(2)], axis=0)
                mean = (sums[:, :128] + sums[:, 128:]) * 0.125
                at = unit * 256 + k * 64
                out[:, at : at + 128] = jnp.transpose(mean).astype(jnp.bfloat16)

    for m in range(SPLIT):
        rows = 16 // SPLIT
        for t in range(0, 9, 2):
            pair_of = (inner[t : t + 2] * 2)[:2]
            rhs = [
                jnp.concatenate([block_of(w2, 1, r, c), block_of(w2, 0, r, c)], axis=1) for r, c in inner[t : t + 2]
            ]
            if len(rhs) == 1:
                rhs.append(jnp.zeros((128, 256), jnp.bfloat16))
            rhs = jnp.concatenate(rhs, axis=0)
            for unit in range(2):
                pltpu.matmul_push_rhs(rhs, turn % 2, unit)
                for i in range(rows):
                    row = unit * 16 + m * rows + i
                    lhs = jnp.concatenate([block(1, row + r, c) for r, c in pair_of], axis=1)
                    pltpu.matmul_acc_lhs(acc[unit][m * rows + i], lhs, turn % 2 if i == 0 else None)
            turn += 1
        active(range(m * rows, m * rows + rows))
    pooled(range(4))


def call(body, out, scratch, flops, *operands):
    vmem = pl.BlockSpec(memory_space=pltpu.VMEM)
    return pl.pallas_call(
        body,
        out_shape=[jax.ShapeDtypeStruct(*shape) for shape in out],
        in_specs=[vmem] * len(operands),
        out_specs=[vmem] * len(out),
        scratch_shapes=[pltpu.VMEM(*shape) for shape in scratch],
        compiler_params=pltpu.CompilerParams(vmem_limit_bytes=24 << 20),
        cost_estimate=pl.CostEstimate(flops=flops, bytes_accessed=4_000_000, transcendentals=0),
    )(*operands)


def local(*operands):
    out = [((32, 64, 256), jnp.float32), ((ROWS * 32, 384), jnp.bfloat16)]
    scratch = [
        ((76, 16, 128), jnp.float32),
        ((ROWS // 2 * 136, 128), jnp.float32),
        ((ROWS * 64, 128), jnp.bfloat16),
        ((ROWS * 80, 128), jnp.bfloat16),
    ]
    return call(local_body, out, scratch, 2_000_000_000, *operands)


def convolve(*operands):
    scratch = [
        ((35 * 2 * LINE, 128), jnp.float32),
        ((ROWS // 2 * 136, 128), jnp.float32),
        ((ROWS * 32, 384), jnp.bfloat16),
        ((3, ROWS * 64, 128), jnp.bfloat16),
        ((3, ROWS * 80, 128), jnp.bfloat16),
        ((32, 64, 256), jnp.float32),
        ((2048, 256), jnp.bfloat16),
    ]
    return call(body, [((128, 512), jnp.bfloat16)], scratch, 8_000_000_000, *operands)[0]


def spread_weights(weight):
    channels = weight.shape[4]
    taps = jnp.transpose(weight, (2, 1, 0, 3, 4)).reshape(3, 3, 12, channels)

    def paired(value, before, after):
        value = jnp.pad(value, ((0, 0), (0, 0), (before, after), (0, 0)))
        value = value.reshape(3, -1, channels)
        value = jnp.pad(value, ((0, 0), (0, 64 - value.shape[1]), (0, 0)))
        sides = [jnp.pad(value, ((0, 0), (0, 0), (0, channels))), jnp.pad(value, ((0, 0), (0, 0), (channels, 0)))]
        return jnp.stack(sides, axis=1).reshape(384, 2 * channels)

    nothing = jnp.zeros((128, 2 * channels), weight.dtype)
    inner = jnp.concatenate([paired(taps, 4, 0), nothing])
    first, rest = taps[:, :, :4], taps[:, :, 4:]
    others = [paired(taps, 0, 8), nothing]
    others += [paired(rest, 0, 8), paired(first, 8, 8)]
    others += [paired(first, 12, 0), paired(rest, 12, 0)]
    return jnp.concatenate(others), inner


def shards(volume, conv1_weight, conv1_bias, conv2_weight, conv2_bias):
    peers = lax.axis_size("space") * lax.axis_size("chan")
    upper = lax.axis_index("chan") % 2 == 1
    own = jnp.transpose(volume.reshape(4, 2, SIDE, SIDE), (2, 1, 0, 3)).reshape(SIDE, 8, SIDE)
    mate = lax.ppermute(own, AXES, [(i, i ^ 1) for i in range(peers)])
    low = jnp.where(upper, mate[SIDE - WINDOW :], own[:WINDOW])
    high = jnp.where(upper, own[SIDE - WINDOW :], mate[:WINDOW])
    planes = [low[:, :4], low[:, 4:], high[:, :4], high[:, 4:]]
    upward = jnp.stack(planes[1:])
    downward = jnp.stack(planes[:2] + [jnp.zeros_like(planes[0])])
    odd = lax.axis_index("chan") // 2 % 2 == 1
    ends = (0, 1, peers - 2, peers - 1)
    first_swap = lax.ppermute(jnp.where(odd, downward, upward), AXES, [(i, i ^ 2) for i in range(peers)])
    second_swap = lax.ppermute(
        jnp.where(odd, upward, downward),
        AXES,
        [(i, i ^ 1) if i in ends else (i, i + 2 if i // 2 % 2 else i - 2) for i in range(peers)],
    )
    spread, inner = spread_weights(conv1_weight)
    w2 = conv2_weight.reshape(3, 1152, 128)
    bias = jnp.stack([conv1_bias, conv2_bias])
    partial, known = local(low, high, inner, w2, bias)
    half = convolve(
        *(first_swap, second_swap, spread, w2, bias),
        jnp.asarray(pool_matrix(), jnp.bfloat16),
        partial,
        known,
    )
    moved = lax.all_to_all(half.reshape(16, 8, 512), "chan", split_axis=0, concat_axis=0, tiled=True)
    return jnp.transpose(moved.reshape(8, 2, 8, 512), (2, 0, 1, 3)).reshape(8, 8, 1024)


def solution(mesh):
    in_specs = (P(None, AXES, None), P(), P(), P(), P())
    out_specs = P("chan", "space", None)
    return jax.shard_map(shards, mesh=mesh, in_specs=in_specs, out_specs=out_specs, check_vma=False)
```

time: 34.9 us -> 35.1 us (level)
  Pallas kernels: 8.41 us -> 7.88 us
  waiting for transfers between devices: 3.54 us -> 3.9 us
    pallas_call x2, Pallas kernels: 8.41 us -> 7.88 us  [call(): pl.pallas_call(body, out_shape=[jax.ShapeDtypeStruct(*shape) for shape in...]
    ppermute x1, waiting for transfers between devices: 2.65 us -> 3 us  [shards(): lax.ppermute(jnp.where(odd, upward, downward), AXES, [(i, i ^ 1) if i in...]
  transfers between devices with their start and end apart: 3 -> 3, of which waited for: 2 -> 2; matrix products, arithmetic and copies ran while one was open for 3% -> 4% of each run, Pallas kernels for 7% -> 7%
where the time goes in v8:
time: 35.1 us; the launch traced here: 34.9 us
  blocking collectives  9.74 us (28%)
  starting transfers between devices  8.85 us (25%)
  Pallas kernels  7.88 us (22%)
  waiting for transfers between devices  3.9 us (11%)
  local copies, waits for them, and re-layouts  3.56 us (10%)
  other arithmetic  0.5 us (1%)
  between operations  0.43 us (1%)
    all_to_all x1, blocking collectives, shards(): lax.all_to_all(half.reshape(16, 8, 512), 'chan', split_axis=0, concat_axi...  9.74 us
    ppermute x1, starting transfers between devices, shards(): lax.ppermute(jnp.where(odd, upward, downward), AXES, [(i, i ^ 1) if i in...  8.08 us
    pallas_call x2, Pallas kernels, call(): pl.pallas_call(body, out_shape=[jax.ShapeDtypeStruct(*shape) for shape in...  7.88 us
    ppermute x1, waiting for transfers between devices, shards(): lax.ppermute(jnp.where(odd, upward, downward), AXES, [(i, i ^ 1) if i in...  3 us
    reshape x2, local copies, waits for them, and re-layouts, shards(): volume.reshape(4, 2, SIDE, SIDE)  1.36 us
    ppermute x1, waiting for transfers between devices, shards(): lax.ppermute(jnp.where(odd, downward, upward), AXES, [(i, i ^ 2) for i in...  0.9 us
    ppermute x1, starting transfers between devices, shards(): mate = lax.ppermute(own, AXES, [(i, i ^ 1) for i in range(peers)])  0.76 us
    transpose x1, local copies, waits for them, and re-layouts, spread_weights(): taps = jnp.transpose(weight, (2, 1, 0, 3, 4)).reshape(3, 3, 12, channels)  0.76 us
  transfers between devices with their start and end apart: 3, of which 2 were waited for; matrix products, arithmetic and copies ran while one was open for 4% of the time, Pallas kernels for 7%

profile of v8, /device:TPU:5, one launch (start us, length us, event | category | flops | bytes accessed | tf_op | source)
XLA Modules:
  0.0 34.9 jit_solution(2600797381032126949)
XLA Ops:
  0.0 1.2 %reshape.59 = bf16[4,2,128,128]{3,2,1,0:T(8,128)(2,1)S(1)} reshape(bf16[4,2,16384]{2,1,0:T(2,128)(2,1)} %param.6) | data formatting | bytes 524288 | tf_op jit(solution)/shard_map/reshape | solution.py:380
  1.2 0.2 copy.26
  1.4 0.8 %collective-permute-start = (bf16[128,8,128]{2,1,0:T(8,128)(2,1)S(1)}, bf16[128,8,128]{2,1,0:T(8,128)(2,1)S(1)}, u32[]{:S(2)}, u32[]{:S(2)}) collective-permute-start(bf16[128,8,128]{2,1,0:T(8,128)(2,1)S(1)} %bitcast.72), channel_id=1, source_target_pairs={{0,1},{1,0},{2,3},{3,2},{4,5},{5,4},{6,7},{7,6},{8,9},{9,8},{10,11... | collective-permute-start | bytes 786440 | tf_op jit(solution)/shard_map/ppermute | solution.py:381
  2.1 0.8 %copy.16 = bf16[3,3,3,4,128]{4,3,2,1,0:T(4,128)(2,1)S(1)} copy(bf16[3,3,3,4,128]{4,3,0,1,2:T(4,128)(2,1)} %bitcast.86) | data formatting | bytes 55296 | tf_op jit(solution)/shard_map/transpose | solution.py:359
  3.6 0.0 copy-start.2
  3.6 0.0 copy-start.3
  3.7 0.0 copy-start
  3.8 0.1 pad.126.clone
  3.9 0.1 fusion
  4.0 0.0 collective-permute-done
  4.0 0.1 slice_bitcast_fusion.1
  4.1 0.3 broadcast_select_fusion
  4.4 8.1 %collective-permute-start.2 = (bf16[3,68,4,128]{3,2,1,0:T(4,128)(2,1)S(1)}, bf16[3,68,4,128]{3,2,1,0:T(4,128)(2,1)S(1)}, u32[]{:S(2)}, u32[]{:S(2)}) collective-permute-start(bf16[3,68,4,128]{3,2,1,0:T(4,128)(2,1)S(1)} %get-tuple-element.9), channel_id=1, source_target_pairs={{0,1},{1,0},{2,4},{3,5},{4,2},{5,3},{6,8},{7,9},{8,6},{9,7},{10,12... | collective-permute-start | bytes 626696 | tf_op jit(solution)/shard_map/ppermute | solution.py:390
  12.5 0.0 collective-permute-start.1
  12.5 0.0 copy-done.2
  12.5 0.0 copy-done.3
  12.6 0.0 copy-done
  12.6 0.0 copy-start.1
  12.6 2.4 %shard_map.64 = (f32[32,64,256]{2,1,0:T(8,128)S(1)}, bf16[1088,384]{1,0:T(8,128)(2,1)S(1)}) custom-call(bf16[68,8,128]{2,1,0:T(8,128)(2,1)S(1)} %get-tuple-element.11.low, bf16[68,8,128]{2,1,0:T(8,128)(2,1)S(1)} %get-tuple-element.12.high, bf16[512,256]{1,0:T(8,128)(2,1)S(1)} %concatenate.7.w1, bf16[3,1152,128]{2,1,0:T(8,128)(2,1)S(1)} %bitcast.70, ...), custom_call_target="tpu_custom_call" | custom-call | flops 2000000000 | bytes 4000000 | tf_op jit(solution)/shard_map/pallas_call | solution.py:322
  15.0 3.0 %collective-permute-done.2.second_swap = bf16[3,68,4,128]{3,2,1,0:T(4,128)(2,1)S(1)} collective-permute-done((bf16[3,68,4,128]{3,2,1,0:T(4,128)(2,1)S(1)}, bf16[3,68,4,128]{3,2,1,0:T(4,128)(2,1)S(1)}, u32[]{:S(2)}, u32[]{:S(2)}) %collective-permute-start.2) | collective-permute-done | bytes 208928 | tf_op jit(solution)/shard_map/ppermute | solution.py:390
  18.0 0.9 %collective-permute-done.1.first_swap = bf16[3,68,4,128]{3,2,1,0:T(4,128)(2,1)S(1)} collective-permute-done((bf16[3,68,4,128]{3,2,1,0:T(4,128)(2,1)S(1)}, bf16[3,68,4,128]{3,2,1,0:T(4,128)(2,1)S(1)}, u32[]{:S(2)}, u32[]{:S(2)}) %collective-permute-start.1) | collective-permute-done | bytes 208928 | tf_op jit(solution)/shard_map/ppermute | solution.py:389
  18.9 0.0 copy-done.1
  18.9 5.4 %shard_map.65 = bf16[128,512]{1,0:T(8,128)(2,1)S(1)} custom-call(bf16[3,68,4,128]{3,2,1,0:T(4,128)(2,1)S(1)} %collective-permute-done.1.first_swap, bf16[3,68,4,128]{3,2,1,0:T(4,128)(2,1)S(1)} %collective-permute-done.2.second_swap, bf16[2048,256]{1,0:T(8,128)(2,1)S(1)} %constant_dynamic-update-slice_fusion.w1, bf16[3,1152,128]{2,1,0:T(8,128)(2,1)S(1)} %bitcast.71, ...), custom_call_target="tpu_custom_call" | custom-call | flops 8000000000 | bytes 4000000 | tf_op jit(solution)/shard_map/pallas_call | solution.py:322
  24.4 9.7 %all_to_all.5 = bf16[16,8,512]{2,1,0:T(8,128)(2,1)S(1)} all-to-all(bf16[16,8,512]{2,1,0:T(8,128)(2,1)S(1)} %bitcast.69), channel_id=1, replica_groups=mesh['space'=16,'chan'=16] {'chan'}, dimensions={0} | all-to-all | bytes 262144 | tf_op jit(solution)/shard_map/all_to_all | solution.py:405
  34.1 0.7 %copy.23 = bf16[8,2,8,512]{3,0,1,2:T(8,128)(2,1)} copy(bf16[8,2,8,512]{3,2,1,0:T(8,128)(2,1)S(1)} %bitcast.82) | data formatting | bytes 262144 | tf_op jit(solution)/shard_map/reshape | solution.py:406
  (39 shorter events, 0.6 us)
Async XLA Ops:
  1.4 2.6 %collective-permute-start = (bf16[128,8,128]{2,1,0:T(8,128)(2,1)S(1)}, bf16[128,8,128]{2,1,0:T(8,128)(2,1)S(1)}, u32[]{:S(2)}, u32[]{:S(2)}) collective-permute-start(bf16[128,8,128]{2,1,0:T(8,128)(2,1)S(1)} %bitcast.72), channel_id=1, source_target_pairs={{0,1},{1,0},{2,3},{3,2},{4,5},{5,4},{6,7},{7,6},{8,9},{9,8},{10,11... | collective-permute-start | bytes 786440 | tf_op jit(solution)/shard_map/ppermute | solution.py:381
  3.6 8.9 %copy-start.2 = (f32[128]{0:T(128)S(1)}, f32[128]{0:T(128)}, u32[]{:S(2)}) copy-start(f32[128]{0:T(128)} %param.10) | copy-start | bytes 1540
  3.6 8.9 %copy-start.3 = (f32[128]{0:T(128)S(1)}, f32[128]{0:T(128)}, u32[]{:S(2)}) copy-start(f32[128]{0:T(128)} %param.8) | copy-start | bytes 1540
  3.7 8.9 %copy-start = (bf16[3,3,3,128,128]{4,3,2,1,0:T(8,128)(2,1)S(1)}, bf16[3,3,3,128,128]{4,3,2,1,0:T(8,128)(2,1)}, u32[]{:S(2)}) copy-start(bf16[3,3,3,128,128]{4,3,2,1,0:T(8,128)(2,1)} %param.9) | copy-start | bytes 2654212
  4.4 13.6 %collective-permute-start.2 = (bf16[3,68,4,128]{3,2,1,0:T(4,128)(2,1)S(1)}, bf16[3,68,4,128]{3,2,1,0:T(4,128)(2,1)S(1)}, u32[]{:S(2)}, u32[]{:S(2)}) collective-permute-start(bf16[3,68,4,128]{3,2,1,0:T(4,128)(2,1)S(1)} %get-tuple-element.9), channel_id=1, source_target_pairs={{0,1},{1,0},{2,4},{3,5},{4,2},{5,3},{6,8},{7,9},{8,6},{9,7},{10,12... | collective-permute-start | bytes 626696 | tf_op jit(solution)/shard_map/ppermute | solution.py:390
  12.5 6.4 %collective-permute-start.1 = (bf16[3,68,4,128]{3,2,1,0:T(4,128)(2,1)S(1)}, bf16[3,68,4,128]{3,2,1,0:T(4,128)(2,1)S(1)}, u32[]{:S(2)}, u32[]{:S(2)}) collective-permute-start(bf16[3,68,4,128]{3,2,1,0:T(4,128)(2,1)S(1)} %get-tuple-element.10), channel_id=1, source_target_pairs={{0,2},{1,3},{2,0},{3,1},{4,6},{5,7},{6,4},{7,5},{8,10},{9,11},{10,... | collective-permute-start | bytes 626696 | tf_op jit(solution)/shard_map/ppermute | solution.py:389
  12.6 6.4 %copy-start.1 = (bf16[64,256]{1,0:T(8,128)(2,1)S(1)}, bf16[64,256]{1,0:T(8,128)(2,1)}, u32[]{:S(2)}) copy-start(bf16[64,256]{1,0:T(8,128)(2,1)} %constant.40.clone.pool) | copy-start | bytes 98308

commit v9 on v8

--- a/solution.py
+++ b/solution.py
@@ -386,9 +386,11 @@
     downward = jnp.stack(planes[:2] + [jnp.zeros_like(planes[0])])
     odd = lax.axis_index("chan") // 2 % 2 == 1
     ends = (0, 1, peers - 2, peers - 1)
-    first_swap = lax.ppermute(jnp.where(odd, downward, upward), AXES, [(i, i ^ 2) for i in range(peers)])
+    one, two = jnp.where(odd, downward, upward), jnp.where(odd, upward, downward)
+    one, two, conv1_weight = lax.optimization_barrier((one, two, conv1_weight))
+    first_swap = lax.ppermute(one, AXES, [(i, i ^ 2) for i in range(peers)])
     second_swap = lax.ppermute(
-        jnp.where(odd, upward, downward),
+        two,
         AXES,
         [(i, i ^ 1) if i in ends else (i, i + 2 if i // 2 % 2 else i - 2) for i in range(peers)],
     )

time: 35.1 us -> 34.2 us (0.974)
  waiting for transfers between devices: 3.9 us -> 1.51 us
  other arithmetic: 0.5 us -> 1.16 us
  starting transfers between devices: 8.85 us -> 9.31 us
    ppermute x2, waiting for transfers between devices: 3.9 us -> 1.21 us  [the longest x1 1.2 us: shards(): lax.ppermute(two, AXES, [(i, i ^ 1) if i in ends else (i, i + 2 if i // 2...]
    unnamed x13 -> x11, local copies, waits for them, and re-layouts: 0.09 us -> 0.96 us
    transpose x1, local copies, waits for them, and re-layouts: 0.76 us -> 0.01 us  [spread_weights(): taps = jnp.transpose(weight, (2, 1, 0, 3, 4)).reshape(3, 3, 12, channels)]
    another operation x1, other arithmetic: 0.01 us -> 0.68 us  [shards(): bias = jnp.stack([conv1_bias, conv2_bias])]
    ppermute x2, starting transfers between devices: 8.09 us -> 8.55 us  [the longest x1 7.16 us: shards(): lax.ppermute(two, AXES, [(i, i ^ 1) if i in ends else (i, i + 2 if i // 2...]
  transfers between devices with their start and end apart: 3 -> 3, of which waited for: 2 -> 2; matrix products, arithmetic and copies ran while one was open for 4% -> 3% of each run, Pallas kernels for 7% -> 7%
where the time goes in v9:
time: 34.2 us; the launch traced here: 33.8 us
  blocking collectives  9.83 us (29%)
  starting transfers between devices  9.31 us (27%)
  Pallas kernels  7.99 us (23%)
  local copies, waits for them, and re-layouts  3.68 us (11%)
  waiting for transfers between devices  1.51 us (4%)
  other arithmetic  1.16 us (3%)
  between operations  0.37 us (1%)
    all_to_all x1, blocking collectives, shards(): lax.all_to_all(half.reshape(16, 8, 512), 'chan', split_axis=0, concat_axi...  9.83 us
    pallas_call x2, Pallas kernels, call(): pl.pallas_call(body, out_shape=[jax.ShapeDtypeStruct(*shape) for shape in...  7.99 us
    ppermute x1, starting transfers between devices, shards(): lax.ppermute(two, AXES, [(i, i ^ 1) if i in ends else (i, i + 2 if i // 2...  7.16 us
    ppermute x1, starting transfers between devices, shards(): first_swap = lax.ppermute(one, AXES, [(i, i ^ 2) for i in range(peers)])  1.38 us
    reshape x2, local copies, waits for them, and re-layouts, shards(): volume.reshape(4, 2, SIDE, SIDE)  1.36 us
    ppermute x1, waiting for transfers between devices, shards(): lax.ppermute(two, AXES, [(i, i ^ 1) if i in ends else (i, i + 2 if i // 2...  1.2 us
    unnamed x11, local copies, waits for them, and re-layouts  0.96 us
    ppermute x1, starting transfers between devices, shards(): mate = lax.ppermute(own, AXES, [(i, i ^ 1) for i in range(peers)])  0.76 us
  transfers between devices with their start and end apart: 3, of which 2 were waited for; matrix products, arithmetic and copies ran while one was open for 3% of the time, Pallas kernels for 7%

profile of v9, /device:TPU:5, one launch (start us, length us, event | category | flops | bytes accessed | tf_op | source)
XLA Modules:
  0.0 33.8 jit_solution(4607773244895995645)
XLA Ops:
  0.0 0.0 copy-start.2
  0.0 1.2 %reshape.59 = bf16[4,2,128,128]{3,2,1,0:T(8,128)(2,1)S(1)} reshape(bf16[4,2,16384]{2,1,0:T(2,128)(2,1)} %param.6) | data formatting | bytes 524288 | tf_op jit(solution)/shard_map/reshape | solution.py:380
  1.2 0.2 copy.26
  1.4 0.8 %collective-permute-start = (bf16[128,8,128]{2,1,0:T(8,128)(2,1)S(1)}, bf16[128,8,128]{2,1,0:T(8,128)(2,1)S(1)}, u32[]{:S(2)}, u32[]{:S(2)}) collective-permute-start(bf16[128,8,128]{2,1,0:T(8,128)(2,1)S(1)} %bitcast.72), channel_id=1, source_target_pairs={{0,1},{1,0},{2,3},{3,2},{4,5},{5,4},{6,7},{7,6},{8,9},{9,8},{10,11... | collective-permute-start | bytes 786440 | tf_op jit(solution)/shard_map/ppermute | solution.py:381
  2.1 0.7 %pad_maximum_fusion.7.bias = f32[2,128]{1,0:T(2,128)S(1)} fusion(f32[1,128]{1,0:T(1,128)} %bitcast.87, f32[1,128]{1,0:T(1,128)} %bitcast.88), kind=kLoop, calls=%fused_computation.34 | loop fusion | flops 256 | bytes 2048 | tf_op jit(solution)/shard_map/stack | solution.py:399
  2.8 0.1 pad.126.clone
  2.9 0.1 fusion
  3.0 0.3 collective-permute-done
  3.3 0.1 slice_bitcast_fusion.1
  3.4 0.3 broadcast_select_fusion
  3.8 0.0 copy-done.2
  4.3 1.4 %collective-permute-start.1 = (bf16[3,68,4,128]{3,2,1,0:T(4,128)(2,1)S(1)}, bf16[3,68,4,128]{3,2,1,0:T(4,128)(2,1)S(1)}, u32[]{:S(2)}, u32[]{:S(2)}) collective-permute-start(bf16[3,68,4,128]{3,2,1,0:T(4,128)(2,1)S(1)} %get-tuple-element.10), channel_id=1, source_target_pairs={{0,2},{1,3},{2,0},{3,1},{4,6},{5,7},{6,4},{7,5},{8,10},{9,11},{10,... | collective-permute-start | bytes 626696 | tf_op jit(solution)/shard_map/ppermute | solution.py:391
  5.7 7.2 %collective-permute-start.2 = (bf16[3,68,4,128]{3,2,1,0:T(4,128)(2,1)S(1)}, bf16[3,68,4,128]{3,2,1,0:T(4,128)(2,1)S(1)}, u32[]{:S(2)}, u32[]{:S(2)}) collective-permute-start(bf16[3,68,4,128]{3,2,1,0:T(4,128)(2,1)S(1)} %get-tuple-element.11), channel_id=1, source_target_pairs={{0,1},{1,0},{2,4},{3,5},{4,2},{5,3},{6,8},{7,9},{8,6},{9,7},{10,12... | collective-permute-start | bytes 626696 | tf_op jit(solution)/shard_map/ppermute | solution.py:392
  12.9 0.0 copy-start
  13.2 0.9 %copy-done = bf16[3,3,3,128,128]{4,3,2,1,0:T(8,128)(2,1)S(1)} copy-done((bf16[3,3,3,128,128]{4,3,2,1,0:T(8,128)(2,1)S(1)}, bf16[3,3,3,128,128]{4,3,2,1,0:T(8,128)(2,1)}, u32[]{:S(2)}) %copy-start) | copy-done | bytes 884760
  14.1 0.0 copy-start.1
  14.1 2.4 %shard_map.64 = (f32[32,64,256]{2,1,0:T(8,128)S(1)}, bf16[1088,384]{1,0:T(8,128)(2,1)S(1)}) custom-call(bf16[68,8,128]{2,1,0:T(8,128)(2,1)S(1)} %get-tuple-element.17.low, bf16[68,8,128]{2,1,0:T(8,128)(2,1)S(1)} %get-tuple-element.18.high, bf16[512,256]{1,0:T(8,128)(2,1)S(1)} %concatenate.7.w1, bf16[3,1152,128]{2,1,0:T(8,128)(2,1)S(1)} %bitcast.70, ...), custom_call_target="tpu_custom_call" | custom-call | flops 2000000000 | bytes 4000000 | tf_op jit(solution)/shard_map/pallas_call | solution.py:322
  16.5 0.0 collective-permute-done.1.first_swap
  16.5 1.2 %collective-permute-done.2.second_swap = bf16[3,68,4,128]{3,2,1,0:T(4,128)(2,1)S(1)} collective-permute-done((bf16[3,68,4,128]{3,2,1,0:T(4,128)(2,1)S(1)}, bf16[3,68,4,128]{3,2,1,0:T(4,128)(2,1)S(1)}, u32[]{:S(2)}, u32[]{:S(2)}) %collective-permute-start.2) | collective-permute-done | bytes 208928 | tf_op jit(solution)/shard_map/ppermute | solution.py:392
  17.7 0.0 copy-done.1
  17.7 5.5 %shard_map.65 = bf16[128,512]{1,0:T(8,128)(2,1)S(1)} custom-call(bf16[3,68,4,128]{3,2,1,0:T(4,128)(2,1)S(1)} %collective-permute-done.1.first_swap, bf16[3,68,4,128]{3,2,1,0:T(4,128)(2,1)S(1)} %collective-permute-done.2.second_swap, bf16[2048,256]{1,0:T(8,128)(2,1)S(1)} %constant_dynamic-update-slice_fusion.w1, bf16[3,1152,128]{2,1,0:T(8,128)(2,1)S(1)} %bitcast.71, ...), custom_call_target="tpu_custom_call" | custom-call | flops 8000000000 | bytes 4000000 | tf_op jit(solution)/shard_map/pallas_call | solution.py:322
  23.3 9.8 %all_to_all.5 = bf16[16,8,512]{2,1,0:T(8,128)(2,1)S(1)} all-to-all(bf16[16,8,512]{2,1,0:T(8,128)(2,1)S(1)} %bitcast.69), channel_id=1, replica_groups=mesh['space'=16,'chan'=16] {'chan'}, dimensions={0} | all-to-all | bytes 262144 | tf_op jit(solution)/shard_map/all_to_all | solution.py:407
  33.1 0.7 %copy.23 = bf16[8,2,8,512]{3,0,1,2:T(8,128)(2,1)} copy(bf16[8,2,8,512]{3,2,1,0:T(8,128)(2,1)S(1)} %bitcast.82) | data formatting | bytes 262144 | tf_op jit(solution)/shard_map/reshape | solution.py:408
  (39 shorter events, 0.6 us)
Async XLA Ops:
  0.0 3.8 %copy-start.2 = (bf16[3,3,3,4,128]{4,3,2,1,0:T(4,128)(2,1)S(1)}, bf16[3,3,3,4,128]{4,3,2,1,0:T(4,128)(2,1)}, u32[]{:S(2)}) copy-start(bf16[3,3,3,4,128]{4,3,2,1,0:T(4,128)(2,1)} %param.7) | copy-start | bytes 82948
  1.4 1.9 %collective-permute-start = (bf16[128,8,128]{2,1,0:T(8,128)(2,1)S(1)}, bf16[128,8,128]{2,1,0:T(8,128)(2,1)S(1)}, u32[]{:S(2)}, u32[]{:S(2)}) collective-permute-start(bf16[128,8,128]{2,1,0:T(8,128)(2,1)S(1)} %bitcast.72), channel_id=1, source_target_pairs={{0,1},{1,0},{2,3},{3,2},{4,5},{5,4},{6,7},{7,6},{8,9},{9,8},{10,11... | collective-permute-start | bytes 786440 | tf_op jit(solution)/shard_map/ppermute | solution.py:381
  4.3 12.2 %collective-permute-start.1 = (bf16[3,68,4,128]{3,2,1,0:T(4,128)(2,1)S(1)}, bf16[3,68,4,128]{3,2,1,0:T(4,128)(2,1)S(1)}, u32[]{:S(2)}, u32[]{:S(2)}) collective-permute-start(bf16[3,68,4,128]{3,2,1,0:T(4,128)(2,1)S(1)} %get-tuple-element.10), channel_id=1, source_target_pairs={{0,2},{1,3},{2,0},{3,1},{4,6},{5,7},{6,4},{7,5},{8,10},{9,11},{10,... | collective-permute-start | bytes 626696 | tf_op jit(solution)/shard_map/ppermute | solution.py:391
  5.7 12.1 %collective-permute-start.2 = (bf16[3,68,4,128]{3,2,1,0:T(4,128)(2,1)S(1)}, bf16[3,68,4,128]{3,2,1,0:T(4,128)(2,1)S(1)}, u32[]{:S(2)}, u32[]{:S(2)}) collective-permute-start(bf16[3,68,4,128]{3,2,1,0:T(4,128)(2,1)S(1)} %get-tuple-element.11), channel_id=1, source_target_pairs={{0,1},{1,0},{2,4},{3,5},{4,2},{5,3},{6,8},{7,9},{8,6},{9,7},{10,12... | collective-permute-start | bytes 626696 | tf_op jit(solution)/shard_map/ppermute | solution.py:392
  12.9 1.2 %copy-start = (bf16[3,3,3,128,128]{4,3,2,1,0:T(8,128)(2,1)S(1)}, bf16[3,3,3,128,128]{4,3,2,1,0:T(8,128)(2,1)}, u32[]{:S(2)}) copy-start(bf16[3,3,3,128,128]{4,3,2,1,0:T(8,128)(2,1)} %param.9) | copy-start | bytes 2654212
  14.1 3.7 %copy-start.1 = (bf16[64,256]{1,0:T(8,128)(2,1)S(1)}, bf16[64,256]{1,0:T(8,128)(2,1)}, u32[]{:S(2)}) copy-start(bf16[64,256]{1,0:T(8,128)(2,1)} %constant.40.clone.pool) | copy-start | bytes 98308

commit v10 on v9

--- a/solution.py
+++ b/solution.py
@@ -378,9 +378,11 @@
     peers = lax.axis_size("space") * lax.axis_size("chan")
     upper = lax.axis_index("chan") % 2 == 1
     own = jnp.transpose(volume.reshape(4, 2, SIDE, SIDE), (2, 1, 0, 3)).reshape(SIDE, 8, SIDE)
-    mate = lax.ppermute(own, AXES, [(i, i ^ 1) for i in range(peers)])
-    low = jnp.where(upper, mate[SIDE - WINDOW :], own[:WINDOW])
-    high = jnp.where(upper, own[SIDE - WINDOW :], mate[:WINDOW])
+    first_rows, last_rows = own[:WINDOW], own[SIDE - WINDOW :]
+    mine = jnp.where(upper, last_rows, first_rows)
+    mate = lax.ppermute(jnp.where(upper, first_rows, last_rows), AXES, [(i, i ^ 1) for i in range(peers)])
+    low = jnp.where(upper, mate, mine)
+    high = jnp.where(upper, mine, mate)
     planes = [low[:, :4], low[:, 4:], high[:, :4], high[:, 4:]]
     upward = jnp.stack(planes[1:])
     downward = jnp.stack(planes[:2] + [jnp.zeros_like(planes[0])])

time: 34.2 us -> 34.2 us (level)
  no operation moved by 1% of the time
where the time goes in v10:
time: 34.2 us; the launch traced here: 33.8 us
  blocking collectives  9.82 us (29%)
  starting transfers between devices  9.31 us (27%)
  Pallas kernels  7.99 us (23%)
  local copies, waits for them, and re-layouts  3.59 us (10%)
  waiting for transfers between devices  1.45 us (4%)
  other arithmetic  1.26 us (4%)
  between operations  0.37 us (1%)
    all_to_all x1, blocking collectives, shards(): lax.all_to_all(half.reshape(16, 8, 512), 'chan', split_axis=0, concat_axi...  9.82 us
    pallas_call x2, Pallas kernels, call(): pl.pallas_call(body, out_shape=[jax.ShapeDtypeStruct(*shape) for shape in...  7.99 us
    ppermute x1, starting transfers between devices, shards(): lax.ppermute(two, AXES, [(i, i ^ 1) if i in ends else (i, i + 2 if i // 2...  7.16 us
    ppermute x1, starting transfers between devices, shards(): first_swap = lax.ppermute(one, AXES, [(i, i ^ 2) for i in range(peers)])  1.38 us
    reshape x2, local copies, waits for them, and re-layouts, shards(): volume.reshape(4, 2, SIDE, SIDE)  1.36 us
    ppermute x1, waiting for transfers between devices, shards(): lax.ppermute(two, AXES, [(i, i ^ 1) if i in ends else (i, i + 2 if i // 2...  1.21 us
    unnamed x11, local copies, waits for them, and re-layouts  0.96 us
    ppermute x1, starting transfers between devices, shards(): lax.ppermute(jnp.where(upper, first_rows, last_rows), AXES, [(i, i ^ 1) f...  0.76 us
  transfers between devices with their start and end apart: 3, of which 2 were waited for; matrix products, arithmetic and copies ran while one was open for 3% of the time, Pallas kernels for 7%

profile of v10, /device:TPU:5, one launch (start us, length us, event | category | flops | bytes accessed | tf_op | source)
XLA Modules:
  0.0 33.8 jit_solution(11859730757092066699)
XLA Ops:
  0.0 0.0 copy-start.2
  0.0 1.2 %reshape.61 = bf16[4,2,128,128]{3,2,1,0:T(8,128)(2,1)S(1)} reshape(bf16[4,2,16384]{2,1,0:T(2,128)(2,1)} %param.6) | data formatting | bytes 524288 | tf_op jit(solution)/shard_map/reshape | solution.py:380
  1.2 0.2 copy.25
  1.4 0.1 broadcast_select_fusion.3
  1.5 0.8 %collective-permute-start = (bf16[68,8,128]{2,1,0:T(8,128)(2,1)S(1)}, bf16[68,8,128]{2,1,0:T(8,128)(2,1)S(1)}, u32[]{:S(2)}, u32[]{:S(2)}) collective-permute-start(bf16[68,8,128]{2,1,0:T(8,128)(2,1)S(1)} %bitcast.83), channel_id=1, source_target_pairs={{0,1},{1,0},{2,3},{3,2},{4,5},{5,4},{6,7},{7,6},{8,9},{9,8},{10,11... | collective-permute-start | bytes 417800 | tf_op jit(solution)/shard_map/ppermute | solution.py:383
  2.3 0.1 pad.126.clone
  2.3 0.7 %pad_maximum_fusion.7.bias = f32[2,128]{1,0:T(2,128)S(1)} fusion(f32[1,128]{1,0:T(1,128)} %bitcast.85, f32[1,128]{1,0:T(1,128)} %bitcast.86), kind=kLoop, calls=%fused_computation.37 | loop fusion | flops 256 | bytes 2048 | tf_op jit(solution)/shard_map/stack | solution.py:401
  3.0 0.2 collective-permute-done
  3.3 0.1 slice_bitcast_fusion.1
  3.4 0.3 broadcast_select_fusion
  3.7 0.0 copy-done.2
  4.2 1.4 %collective-permute-start.1 = (bf16[3,68,4,128]{3,2,1,0:T(4,128)(2,1)S(1)}, bf16[3,68,4,128]{3,2,1,0:T(4,128)(2,1)S(1)}, u32[]{:S(2)}, u32[]{:S(2)}) collective-permute-start(bf16[3,68,4,128]{3,2,1,0:T(4,128)(2,1)S(1)} %get-tuple-element.10), channel_id=1, source_target_pairs={{0,2},{1,3},{2,0},{3,1},{4,6},{5,7},{6,4},{7,5},{8,10},{9,11},{10,... | collective-permute-start | bytes 626696 | tf_op jit(solution)/shard_map/ppermute | solution.py:393
  5.6 7.2 %collective-permute-start.2 = (bf16[3,68,4,128]{3,2,1,0:T(4,128)(2,1)S(1)}, bf16[3,68,4,128]{3,2,1,0:T(4,128)(2,1)S(1)}, u32[]{:S(2)}, u32[]{:S(2)}) collective-permute-start(bf16[3,68,4,128]{3,2,1,0:T(4,128)(2,1)S(1)} %get-tuple-element.11), channel_id=1, source_target_pairs={{0,1},{1,0},{2,4},{3,5},{4,2},{5,3},{6,8},{7,9},{8,6},{9,7},{10,12... | collective-permute-start | bytes 626696 | tf_op jit(solution)/shard_map/ppermute | solution.py:394
  12.8 0.0 copy-start
  13.1 0.9 %copy-done = bf16[3,3,3,128,128]{4,3,2,1,0:T(8,128)(2,1)S(1)} copy-done((bf16[3,3,3,128,128]{4,3,2,1,0:T(8,128)(2,1)S(1)}, bf16[3,3,3,128,128]{4,3,2,1,0:T(8,128)(2,1)}, u32[]{:S(2)}) %copy-start) | copy-done | bytes 884760
  14.0 0.0 copy-start.1
  14.0 2.4 %shard_map.64 = (f32[32,64,256]{2,1,0:T(8,128)S(1)}, bf16[1088,384]{1,0:T(8,128)(2,1)S(1)}) custom-call(bf16[68,8,128]{2,1,0:T(8,128)(2,1)S(1)} %get-tuple-element.17.low, bf16[68,8,128]{2,1,0:T(8,128)(2,1)S(1)} %get-tuple-element.18.high, bf16[512,256]{1,0:T(8,128)(2,1)S(1)} %concatenate.7.w1, bf16[3,1152,128]{2,1,0:T(8,128)(2,1)S(1)} %bitcast.69, ...), custom_call_target="tpu_custom_call" | custom-call | flops 2000000000 | bytes 4000000 | tf_op jit(solution)/shard_map/pallas_call | solution.py:322
  16.5 0.0 collective-permute-done.1.first_swap
  16.5 1.2 %collective-permute-done.2.second_swap = bf16[3,68,4,128]{3,2,1,0:T(4,128)(2,1)S(1)} collective-permute-done((bf16[3,68,4,128]{3,2,1,0:T(4,128)(2,1)S(1)}, bf16[3,68,4,128]{3,2,1,0:T(4,128)(2,1)S(1)}, u32[]{:S(2)}, u32[]{:S(2)}) %collective-permute-start.2) | collective-permute-done | bytes 208928 | tf_op jit(solution)/shard_map/ppermute | solution.py:394
  17.7 0.0 copy-done.1
  17.7 5.5 %shard_map.65 = bf16[128,512]{1,0:T(8,128)(2,1)S(1)} custom-call(bf16[3,68,4,128]{3,2,1,0:T(4,128)(2,1)S(1)} %collective-permute-done.1.first_swap, bf16[3,68,4,128]{3,2,1,0:T(4,128)(2,1)S(1)} %collective-permute-done.2.second_swap, bf16[2048,256]{1,0:T(8,128)(2,1)S(1)} %constant_dynamic-update-slice_fusion.w1, bf16[3,1152,128]{2,1,0:T(8,128)(2,1)S(1)} %bitcast.70, ...), custom_call_target="tpu_custom_call" | custom-call | flops 8000000000 | bytes 4000000 | tf_op jit(solution)/shard_map/pallas_call | solution.py:322
  23.2 9.8 %all_to_all.5 = bf16[16,8,512]{2,1,0:T(8,128)(2,1)S(1)} all-to-all(bf16[16,8,512]{2,1,0:T(8,128)(2,1)S(1)} %bitcast.68), channel_id=1, replica_groups=mesh['space'=16,'chan'=16] {'chan'}, dimensions={0} | all-to-all | bytes 262144 | tf_op jit(solution)/shard_map/all_to_all | solution.py:409
  33.1 0.7 %copy.23 = bf16[8,2,8,512]{3,0,1,2:T(8,128)(2,1)} copy(bf16[8,2,8,512]{3,2,1,0:T(8,128)(2,1)S(1)} %bitcast.79) | data formatting | bytes 262144 | tf_op jit(solution)/shard_map/reshape | solution.py:410
  (39 shorter events, 0.6 us)
Async XLA Ops:
  0.0 3.7 %copy-start.2 = (bf16[3,3,3,4,128]{4,3,2,1,0:T(4,128)(2,1)S(1)}, bf16[3,3,3,4,128]{4,3,2,1,0:T(4,128)(2,1)}, u32[]{:S(2)}) copy-start(bf16[3,3,3,4,128]{4,3,2,1,0:T(4,128)(2,1)} %param.7) | copy-start | bytes 82948
  1.5 1.8 %collective-permute-start = (bf16[68,8,128]{2,1,0:T(8,128)(2,1)S(1)}, bf16[68,8,128]{2,1,0:T(8,128)(2,1)S(1)}, u32[]{:S(2)}, u32[]{:S(2)}) collective-permute-start(bf16[68,8,128]{2,1,0:T(8,128)(2,1)S(1)} %bitcast.83), channel_id=1, source_target_pairs={{0,1},{1,0},{2,3},{3,2},{4,5},{5,4},{6,7},{7,6},{8,9},{9,8},{10,11... | collective-permute-start | bytes 417800 | tf_op jit(solution)/shard_map/ppermute | solution.py:383
  4.2 12.2 %collective-permute-start.1 = (bf16[3,68,4,128]{3,2,1,0:T(4,128)(2,1)S(1)}, bf16[3,68,4,128]{3,2,1,0:T(4,128)(2,1)S(1)}, u32[]{:S(2)}, u32[]{:S(2)}) collective-permute-start(bf16[3,68,4,128]{3,2,1,0:T(4,128)(2,1)S(1)} %get-tuple-element.10), channel_id=1, source_target_pairs={{0,2},{1,3},{2,0},{3,1},{4,6},{5,7},{6,4},{7,5},{8,10},{9,11},{10,... | collective-permute-start | bytes 626696 | tf_op jit(solution)/shard_map/ppermute | solution.py:393
  5.6 12.1 %collective-permute-start.2 = (bf16[3,68,4,128]{3,2,1,0:T(4,128)(2,1)S(1)}, bf16[3,68,4,128]{3,2,1,0:T(4,128)(2,1)S(1)}, u32[]{:S(2)}, u32[]{:S(2)}) collective-permute-start(bf16[3,68,4,128]{3,2,1,0:T(4,128)(2,1)S(1)} %get-tuple-element.11), channel_id=1, source_target_pairs={{0,1},{1,0},{2,4},{3,5},{4,2},{5,3},{6,8},{7,9},{8,6},{9,7},{10,12... | collective-permute-start | bytes 626696 | tf_op jit(solution)/shard_map/ppermute | solution.py:394
  12.8 1.2 %copy-start = (bf16[3,3,3,128,128]{4,3,2,1,0:T(8,128)(2,1)S(1)}, bf16[3,3,3,128,128]{4,3,2,1,0:T(8,128)(2,1)}, u32[]{:S(2)}) copy-start(bf16[3,3,3,128,128]{4,3,2,1,0:T(8,128)(2,1)} %param.9) | copy-start | bytes 2654212
  14.0 3.7 %copy-start.1 = (bf16[64,256]{1,0:T(8,128)(2,1)S(1)}, bf16[64,256]{1,0:T(8,128)(2,1)}, u32[]{:S(2)}) copy-start(bf16[64,256]{1,0:T(8,128)(2,1)} %constant.40.clone.pool) | copy-start | bytes 98308
